TPU v7x, 128 devices: a whole 4x4x4 slice. The times are simulated.
128 devices in a mesh: dp: 16 (over y, z), seq: 8 (over x, core).
Axes of the slice: x: 4, y: 4, z: 4, core: 2. Of those that a mesh axis runs over, the one named last changes fastest.
Arguments:
- queries: bfloat16 [16, 1024, 4096], P('dp', 'seq'), may hold values from -12 to 12
- key_states: bfloat16 [16, 1024, 512], P('dp', 'seq'), may hold values from -12 to 12
- value_states: bfloat16 [16, 1024, 512], P('dp', 'seq'), may hold values from -6 to 6
- out_grad: bfloat16 [16, 1024, 4096], P('dp', 'seq'), may hold values from -6 to 6
- layer_input: bfloat16 [16, 1024, 8192], P('dp', 'seq'), may hold values from -6 to 6
- lengths: int32 [16, 8], P('dp'), may hold values from 1 to 512, 1024 in all within a row
Outputs:
- query_grad: bfloat16 [16, 1024, 4096], P('dp', 'seq')
- key_grad: bfloat16 [16, 1024, 512], P('dp', 'seq')
- value_grad: bfloat16 [16, 1024, 512], P('dp', 'seq')
- value_weight_grad: float32 [8192, 512], P(('dp', 'seq'))
Inputs may be any that keep to these rules, and one draw needn't show every extreme that they name: `lengths`: each row sums to 1024 and its largest entry is exactly 512.
All inputs are finite; a program needn't handle non-finite values.
Results may differ from a plain program's by a relative error of at most 0.018.
Values may be sent and summed in bfloat16 or wider, within the bound.
No kernel may reach another device: no remote copies, remote signals or barrier semaphores. Data moves between devices by JAX's collectives and lax.ppermute only.
A program may use at most 192 MiB of HBM per device.

v0:
```python
import math

import jax
import jax.numpy as jnp
from jax import lax
from jax.sharding import PartitionSpec as P

D = 8192
HQ = 32
HK = 4
HD = 128


def side_by_side(arrays, axis, split_dim, concat_dim, along):
    ends, at = ([], 0)
    for a in arrays[:-1]:
        at += a.shape[along]
        ends.append(at)
    both = jnp.concatenate(arrays, axis=along)
    return tuple(
        jnp.split(
            lax.all_to_all(both, axis, split_axis=split_dim, concat_axis=concat_dim, tiled=True),
            ends,
            axis=along,
        )
    )


def in_order(pieces, dim):
    dims = list(pieces.shape[1:])
    dims[dim] *= pieces.shape[0]
    return jnp.moveaxis(pieces, 0, dim).reshape(dims)


def sent_to_all(value, axis):
    size = lax.axis_size(axis)
    return lax.all_to_all(
        jnp.broadcast_to(value[None], (size, *value.shape)), axis, 0, 0, tiled=True
    )


def collect(value, axis, dim):
    return in_order(sent_to_all(value, axis), dim)


def in_blocks(value, dim, size):
    dims = value.shape
    pieces = value.reshape(*dims[:dim], size, dims[dim] // size, *dims[dim + 1 :])
    return jnp.moveaxis(pieces, dim, 0)


def summed_on_arrival(value, axis, dim):
    size = lax.axis_size(axis)
    pieces = lax.all_to_all(in_blocks(value, dim, size), axis, 0, 0, tiled=True)
    return jnp.sum(pieces.astype(jnp.float32), axis=0)


def attention_grads(query_heads, grad_heads, key_heads, value_heads, segment_ids):
    streams, full_len, per_device, head_size = query_heads.shape
    score_scale = HD ** (-0.5)
    score_form = "sqhd,skhd->shqk"
    back_form = "shqk,skhd->sqhd"
    block_rows = min(512, full_len)
    block_count = full_len // block_rows
    positions = jnp.arange(full_len, dtype=jnp.int32)
    key_total = jnp.zeros((streams, full_len, per_device, head_size), jnp.float32)
    value_total = jnp.zeros((streams, full_len, per_device, head_size), jnp.float32)
    query_parts = []
    for block_index in range(block_count):
        start_row = block_index * block_rows
        stop_row = start_row + block_rows
        query_block = query_heads[:, start_row:stop_row]
        grad_block = grad_heads[:, start_row:stop_row]
        key_block = key_heads[:, :stop_row]
        value_block = value_heads[:, :stop_row]
        allowed = (segment_ids[:, start_row:stop_row, None] == segment_ids[:, None, :stop_row]) & (
            positions[None, None, :stop_row] <= positions[None, start_row:stop_row, None]
        )
        scores = (
            jnp.einsum(score_form, query_block, key_block, preferred_element_type=jnp.float32)
            * score_scale
        )
        scores = jnp.where(allowed[:, None], scores, -jnp.inf)
        row_peak = jnp.max(scores, axis=-1, keepdims=True)
        exponent = jnp.exp(scores - row_peak)
        attn_weights = exponent / jnp.sum(exponent, axis=-1, keepdims=True)
        prob_grad = jnp.einsum(
            score_form, grad_block, value_block, preferred_element_type=jnp.float32
        )
        row_delta = jnp.sum(attn_weights * prob_grad, axis=-1, keepdims=True)
        score_grad = (attn_weights * (prob_grad - row_delta) * score_scale).astype(jnp.bfloat16)
        weights_half = attn_weights.astype(jnp.bfloat16)
        query_parts.append(
            jnp.einsum(back_form, score_grad, key_block, preferred_element_type=jnp.float32).astype(
                jnp.bfloat16
            )
        )
        key_total = key_total.at[:, :stop_row].add(
            jnp.einsum(
                "shqk,sqhd->skhd", score_grad, query_block, preferred_element_type=jnp.float32
            )
        )
        value_total = value_total.at[:, :stop_row].add(
            jnp.einsum(
                "shqk,sqhd->skhd", weights_half, grad_block, preferred_element_type=jnp.float32
            )
        )
    query_out = jnp.concatenate(query_parts, axis=1)
    return (query_out, key_total.astype(jnp.bfloat16), value_total.astype(jnp.bfloat16))


def shards(queries, key_states, value_states, out_grad, layer_input, lengths):
    seq_count = lax.axis_size("seq")
    dp_count = lax.axis_size("dp")
    streams, local_len, query_width = queries.shape
    group_size = HQ // HK
    copy_count = seq_count // HK
    full_len = local_len * seq_count
    query_four = queries.reshape(streams, local_len, HQ, HD)
    grad_four = out_grad.reshape(streams, local_len, HQ, HD)
    key_four = key_states.reshape(streams, local_len, HK, HD)
    value_four = value_states.reshape(streams, local_len, HK, HD)
    key_spread = jnp.broadcast_to(
        key_four[:, :, :, None, :], (streams, local_len, HK, group_size, HD)
    ).reshape(streams, local_len, HQ, HD)
    value_spread = jnp.broadcast_to(
        value_four[:, :, :, None, :], (streams, local_len, HK, group_size, HD)
    ).reshape(streams, local_len, HQ, HD)
    query_heads, grad_heads, key_heads, value_heads = side_by_side(
        (query_four, grad_four, key_spread, value_spread), "seq", 2, 1, 0
    )
    positions = jnp.arange(full_len, dtype=jnp.int32)
    sample_ends = jnp.cumsum(lengths, axis=1)
    segment_ids = jnp.sum(
        (sample_ends[:, None, :] <= positions[None, :, None]).astype(jnp.int32), axis=2
    )
    query_out, key_out, value_out = attention_grads(
        query_heads, grad_heads, key_heads, value_heads, segment_ids
    )
    query_tok = lax.all_to_all(query_out, "seq", split_axis=1, concat_axis=2, tiled=True)
    key_local = jnp.sum(key_out.astype(jnp.float32), axis=2, keepdims=True)
    value_local = jnp.sum(value_out.astype(jnp.float32), axis=2, keepdims=True)
    key_tok, value_tok = tuple(
        (
            part.astype(jnp.float32)
            for part in side_by_side(
                (key_local.astype(jnp.bfloat16), value_local.astype(jnp.bfloat16)), "seq", 1, 2, 0
            )
        )
    )
    key_grad = (
        jnp.sum(key_tok.reshape(streams, local_len, HK, copy_count, HD), axis=3)
        .astype(jnp.bfloat16)
        .reshape(streams, local_len, HK * HD)
    )
    value_grad = (
        jnp.sum(value_tok.reshape(streams, local_len, HK, copy_count, HD), axis=3)
        .astype(jnp.bfloat16)
        .reshape(streams, local_len, HK * HD)
    )
    query_grad = query_tok.reshape(streams, local_len, HQ * HD)
    row_count = D // (dp_count * seq_count)
    split_input = layer_input.reshape(streams, local_len, dp_count, seq_count, row_count)
    input_mine = lax.all_to_all(split_input, "seq", split_axis=3, concat_axis=1, tiled=True)
    value_whole = collect(value_grad, "seq", 1)
    input_flat = input_mine.reshape(streams * full_len, dp_count * row_count)
    value_flat = value_whole.reshape(streams * full_len, HK * HD)
    stream_part = lax.dot_general(
        input_flat, value_flat, (((0,), (0,)), ((), ())), preferred_element_type=jnp.float32
    )
    weight_sum = summed_on_arrival(stream_part.astype(jnp.bfloat16), "dp", 0)
    token_total = streams * dp_count * full_len
    value_weight_grad = weight_sum / math.sqrt(token_total)
    return (query_grad, key_grad, value_grad, value_weight_grad)


def solution(mesh):
    return jax.shard_map(
        shards,
        mesh=mesh,
        in_specs=(
            P("dp", "seq", None),
            P("dp", "seq", None),
            P("dp", "seq", None),
            P("dp", "seq", None),
            P("dp", "seq", None),
            P("dp", None),
        ),
        out_specs=(
            P("dp", "seq", None),
            P("dp", "seq", None),
            P("dp", "seq", None),
            P(("dp", "seq"), None),
        ),
        check_vma=False,
    )
```

profile of v0, /device:TPU:0, one launch (start us, length us, event | category | flops | bytes accessed | tf_op | source)
XLA Modules:
  0.0 265.3 jit_solution(6539051387735233870)
XLA Ops:
  0.6 1.0 copy.230
  1.7 1.0 copy.231
  2.7 1.6 copy.186
  4.3 1.6 copy.187
  5.9 0.2 broadcast_in_dim.42
  6.2 0.2 broadcast_in_dim.39
  6.4 0.6 pad_maximum_fusion
  7.0 2.3 copy.190
  9.3 4.7 %all-to-all-start = ((bf16[4,128,32,128]{1,3,0,2:T(8,128)(2,1)}), bf16[4,128,32,128]{1,3,0,2:T(8,128)(2,1)}, u32[]{:S(2)}, u32[]{:S(2)}) async-start(bf16[4,128,32,128]{1,3,0,2:T(8,128)(2,1)} %copy.190), calls=%async_computation | async-start | bytes 8388608 | tf_op jit(solution)/shard_map/all_to_all | solution.py:22
  14.0 0.2 reduce_window_sum.11
  14.2 0.1 convert_reduce_fusion.1
  14.3 0.3 compare_and_fusion
  14.6 1.4 fusion.40
  16.0 47.6 %all-to-all-done = bf16[4,128,32,128]{1,3,0,2:T(8,128)(2,1)} async-done(((bf16[4,128,32,128]{1,3,0,2:T(8,128)(2,1)}), bf16[4,128,32,128]{1,3,0,2:T(8,128)(2,1)}, u32[]{:S(2)}, u32[]{:S(2)}) %all-to-all-start) | async-done | bytes 4194336 | tf_op jit(solution)/shard_map/all_to_all | solution.py:22
  63.6 6.4 %copy.191 = bf16[4,128,32,128]{3,1,2,0:T(8,128)(2,1)} copy(bf16[4,128,32,128]{1,3,0,2:T(8,128)(2,1)} %all-to-all-done) | data formatting | bytes 8388608 | tf_op jit(solution)/shard_map/all_to_all | solution.py:22
  70.0 2.7 %fusion.94 = (bf16[1,8,128,4,128]{4,2,3,1,0:T(8,128)(2,1)S(1)}, bf16[1,8,128,4,128]{4,2,3,1,0:T(8,128)(2,1)S(1)}, bf16[1,8,128,4,128]{4,2,3,1,0:T(8,128)(2,1)S(1)}, bf16[1,8,128,4,128]{4,2,3,1,0:T(8,128)(2,1)S(1)}) fusion(bf16[4,8,128,4,128]{4,2,3,1,0:T(8,128)(2,1)} %bitcast.120), kind=kLoop, calls=%fused_computation.84 | loop fusion | bytes 8388608 | tf_op jit(solution)/shard_map/split | solution.py:21
  72.7 0.1 copy.193
  72.8 0.0 copy-start
  72.9 0.1 copy.195
  72.9 0.1 copy.192
  73.0 0.1 copy.194
  73.1 2.6 fusion.78
  75.7 0.7 fusion.79
  76.4 2.1 fusion.98
  78.6 2.0 copy-done.3
  80.6 1.9 fusion.52
  82.5 9.0 %fusion.55 = f32[1,512,4,128]{1,3,2,0:T(8,128)} fusion(f32[4,512,512]{1,2,0:T(8,128)} %fusion.78, bf16[1,1024,4,128]{3,1,2,0:T(8,128)(2,1)} %bitcast.139, f32[4,512,512]{1,2,0:T(8,128)} %copy-done.3, f32[4,512]{1,0:T(4,128)S(1)} %get-tuple-element.86), kind=kOutput, calls=%fused_computation.48 | convolution fusion | flops 275778048 | bytes 18366464 | tf_op jit(solution)/shard_map/shqk,sqhd->skhd/dot_general | solution.py:99
  91.5 4.5 %fusion.80 = f32[4,512,1024]{2,1,0:T(8,128)} fusion(bf16[1024,4,128]{2,0,1:T(8,128)(2,1)S(1)} %bitcast.124, bf16[1,1024,4,128]{3,1,2,0:T(8,128)(2,1)S(1)} %bitcast.127), kind=kOutput, calls=%fused_computation.67 | convolution fusion | flops 536870912 | bytes 9961472 | tf_op jit(solution)/shard_map/sqhd,skhd->shqk/dot_general | solution.py:87
  96.0 7.4 %fusion.97 = (f32[4,512]{1,0:T(4,128)S(1)}, f32[4,512,1024]{2,1,0:T(8,128)}) fusion(pred[512,1024]{1,0:T(8,128)(4,1)} %fusion.40, bf16[1024,4,128]{2,0,1:T(8,128)(2,1)S(1)} %bitcast.135, bf16[1,1024,4,128]{3,1,2,0:T(8,128)(2,1)} %bitcast.140), kind=kOutput, calls=%fused_computation.87 | convolution fusion | flops 545260544 | bytes 10493952 | tf_op jit(solution)/shard_map/sub | solution.py:85
  103.3 4.8 %fusion.67 = bf16[1024,128]{0,1:T(8,128)(2,1)S(1)} fusion(f32[1,512,4,128]{1,3,2,0:T(8,128)} %fusion.52, bf16[1,1024,4,128]{3,1,2,0:T(8,128)(2,1)S(1)} %bitcast.128, f32[4,512,1024]{2,1,0:T(8,128)} %get-tuple-element.85, f32[4,512]{1,0:T(4,128)S(1)} %get-tuple-element.84), kind=kOutput, calls=%fused_computation.52 | convolution fusion | flops 542507008 | bytes 10231808 | tf_op jit(solution)/shard_map/shqk,sqhd->skhd/dot_general | solution.py:104
  108.2 22.4 %fusion.64 = bf16[1024,128]{0,1:T(8,128)(2,1)S(1)} fusion(f32[4,512,1024]{2,1,0:T(8,128)} %fusion.80, f32[1,512,4,128]{1,3,2,0:T(8,128)} %fusion.55, bf16[1,1024,4,128]{3,1,2,0:T(8,128)(2,1)S(1)} %bitcast.141, f32[4,512,1024]{2,1,0:T(8,128)} %get-tuple-element.85, f32[4,512]{1,0:T(4,128)S(1)} %get-tuple-element.84), kind=kOutput, calls=%fused_computation.51 | convolution fusion | flops 552995840 | bytes 35405824 | tf_op jit(solution)/shard_map/shqk,sqhd->skhd/dot_general | solution.py:99
  130.6 0.1 pad_maximum_fusion.2
  130.7 1.1 copy.209
  131.8 4.1 %all-to-all-start.2 = ((bf16[2,1024,1,128]{3,0,2,1:T(2,128)(2,1)}), bf16[2,1024,1,128]{3,0,2,1:T(2,128)(2,1)}, u32[]{:S(2)}, u32[]{:S(2)}) async-start(bf16[2,1024,1,128]{3,0,2,1:T(2,128)(2,1)} %copy.209), calls=%async_computation.2 | async-start | bytes 1048576 | tf_op jit(solution)/shard_map/all_to_all | solution.py:22
  135.9 3.2 %copy.215 = bf16[1,128,8192]{1,2,0:T(8,128)(2,1)S(1)} copy(bf16[1,128,8192]{2,1,0:T(8,128)(2,1)} %param.22) | data formatting | bytes 4194304 | tf_op args[4]
  139.2 1.6 copy.216
  140.8 5.5 %all-to-all-done.2 = bf16[2,1024,1,128]{3,0,2,1:T(2,128)(2,1)} async-done(((bf16[2,1024,1,128]{3,0,2,1:T(2,128)(2,1)}), bf16[2,1024,1,128]{3,0,2,1:T(2,128)(2,1)}, u32[]{:S(2)}, u32[]{:S(2)}) %all-to-all-start.2) | async-done | bytes 524320 | tf_op jit(solution)/shard_map/all_to_all | solution.py:22
  146.2 3.6 %all-to-all-start.4 = ((bf16[1,128,16,8,64]{1,4,2,0,3:T(8,128)(2,1)}), bf16[1,128,16,8,64]{1,4,2,0,3:T(8,128)(2,1)S(1)}, u32[]{:S(2)}, u32[]{:S(2)}) async-start(bf16[1,128,16,8,64]{1,4,2,0,3:T(8,128)(2,1)} %copy.216), calls=%async_computation.4 | async-start | bytes 4194304 | tf_op jit(solution)/shard_map/all_to_all | solution.py:164
  149.8 1.1 copy.210
  151.0 0.7 fusion.95
  151.7 1.7 reduce.30
  153.4 1.0 copy.212
  154.4 0.8 copy.214
  155.2 21.8 %all-to-all-done.4 = bf16[1,128,16,8,64]{1,4,2,0,3:T(8,128)(2,1)S(1)} async-done(((bf16[1,128,16,8,64]{1,4,2,0,3:T(8,128)(2,1)}), bf16[1,128,16,8,64]{1,4,2,0,3:T(8,128)(2,1)S(1)}, u32[]{:S(2)}, u32[]{:S(2)}) %all-to-all-start.4) | async-done | bytes 2097184 | tf_op jit(solution)/shard_map/all_to_all | solution.py:164
  176.9 2.0 broadcast_in_dim.77
  178.9 4.2 %all-to-all-start.3 = ((bf16[8,1,128,512]{3,2,1,0:T(8,128)(2,1)}), bf16[8,1,128,512]{3,2,1,0:T(8,128)(2,1)}, u32[]{:S(2)}, u32[]{:S(2)}) async-start(bf16[8,1,128,512]{3,2,1,0:T(8,128)(2,1)} %broadcast_in_dim.77), calls=%async_computation.3 | async-start | bytes 2097152 | tf_op jit(solution)/shard_map/all_to_all | solution.py:37
  183.2 8.5 %fusion.73 = bf16[1,512,4,128]{1,3,2,0:T(8,128)(2,1)} fusion(f32[4,512,512]{1,2,0:T(8,128)} %fusion.78, bf16[1,1024,4,128]{3,1,2,0:T(8,128)(2,1)S(1)} %bitcast.136, f32[4,512,512]{1,2,0:T(8,128)} %copy-done.3, f32[4,512]{1,0:T(4,128)S(1)} %get-tuple-element.86), kind=kOutput, calls=%fused_computation.54 | convolution fusion | flops 276040192 | bytes 17842176 | tf_op jit(solution)/shard_map/shqk,skhd->sqhd/dot_general | solution.py:94
  191.7 23.9 %fusion.70 = bf16[1,512,4,128]{1,3,2,0:T(8,128)(2,1)} fusion(bf16[1024,4,128]{2,0,1:T(8,128)(2,1)S(1)} %bitcast.137, f32[4,512,1024]{2,1,0:T(8,128)} %fusion.80, f32[4,512,1024]{2,1,0:T(8,128)} %get-tuple-element.85, f32[4,512]{1,0:T(4,128)S(1)} %get-tuple-element.84), kind=kOutput, calls=%fused_computation.53 | convolution fusion | flops 551816192 | bytes 18358272 | tf_op jit(solution)/shard_map/shqk,skhd->sqhd/dot_general | solution.py:94
  215.6 1.3 pad_maximum_fusion.1
  216.9 1.4 copy.201
  218.4 4.7 %all-to-all-start.1 = ((bf16[1,1024,4,128]{3,2,0,1:T(4,128)(2,1)}), bf16[1,1024,4,128]{3,2,0,1:T(4,128)(2,1)S(1)}, u32[]{:S(2)}, u32[]{:S(2)}) async-start(bf16[1,1024,4,128]{3,2,0,1:T(4,128)(2,1)} %copy.201), calls=%async_computation.1 | async-start | bytes 2097152 | tf_op jit(solution)/shard_map/all_to_all | solution.py:140
  223.1 1.8 copy.217
  224.8 2.5 fusion.49
  227.4 1.3 copy.218
  228.7 10.3 %all-to-all-done.1 = bf16[1,1024,4,128]{3,2,0,1:T(4,128)(2,1)S(1)} async-done(((bf16[1,1024,4,128]{3,2,0,1:T(4,128)(2,1)}), bf16[1,1024,4,128]{3,2,0,1:T(4,128)(2,1)S(1)}, u32[]{:S(2)}, u32[]{:S(2)}) %all-to-all-start.1) | async-done | bytes 1048608 | tf_op jit(solution)/shard_map/all_to_all | solution.py:140
  239.0 8.2 %all-to-all-start.5 = ((bf16[16,64,512]{2,1,0:T(8,128)(2,1)}), bf16[16,64,512]{2,1,0:T(8,128)(2,1)S(1)}, u32[]{:S(2)}, u32[]{:S(2)}) async-start(bf16[16,64,512]{2,1,0:T(8,128)(2,1)} %bitcast.54), calls=%async_computation.5 | async-start | bytes 2097152 | tf_op jit(solution)/shard_map/all_to_all | solution.py:54
  247.2 0.1 copy.211
  247.4 0.8 copy.219
  248.1 0.8 copy.220
  248.9 0.4 copy.202
  249.3 1.6 reshape.620
  250.9 13.6 %all-to-all-done.5 = bf16[16,64,512]{2,1,0:T(8,128)(2,1)S(1)} async-done(((bf16[16,64,512]{2,1,0:T(8,128)(2,1)}), bf16[16,64,512]{2,1,0:T(8,128)(2,1)S(1)}, u32[]{:S(2)}, u32[]{:S(2)}) %all-to-all-start.5) | async-done | bytes 1048608 | tf_op jit(solution)/shard_map/all_to_all | solution.py:54
  264.5 0.1 convert_reduce_fusion
  264.6 0.7 broadcast_multiply_fusion
  (13 shorter events, 0.1 us)
Async XLA Ops:
  9.3 4.7 %copy-start.2 = (s32[1,8]{1,0:T(1,128)S(1)}, s32[1,8]{1,0:T(1,128)}, u32[]{:S(2)}) copy-start(s32[1,8]{1,0:T(1,128)} %param.23) | copy-start | bytes 100
  9.3 54.3 %all-to-all-start = ((bf16[4,128,32,128]{1,3,0,2:T(8,128)(2,1)}), bf16[4,128,32,128]{1,3,0,2:T(8,128)(2,1)}, u32[]{:S(2)}, u32[]{:S(2)}) async-start(bf16[4,128,32,128]{1,3,0,2:T(8,128)(2,1)} %copy.190), calls=%async_computation | async-start | bytes 8388608 | tf_op jit(solution)/shard_map/all_to_all | solution.py:22
  72.8 2.9 %copy-start = (bf16[1,8,128,4,128]{4,2,1,3,0:T(8,128)(2,1)}, bf16[1,8,128,4,128]{4,2,1,3,0:T(8,128)(2,1)S(1)}, u32[]{:S(2)}) copy-start(bf16[1,8,128,4,128]{4,2,1,3,0:T(8,128)(2,1)S(1)} %copy.193) | copy-start | bytes 3145732
  78.6 2.0 copy-start.3
  103.3 4.8 %copy-start.1 = (bf16[1,8,128,4,128]{4,2,1,3,0:T(8,128)(2,1)S(1)}, bf16[1,8,128,4,128]{4,2,1,3,0:T(8,128)(2,1)}, u32[]{:S(2)}) copy-start(bf16[1,8,128,4,128]{4,2,1,3,0:T(8,128)(2,1)} %copy-done) | copy-start | bytes 3145732
  131.8 14.5 %all-to-all-start.2 = ((bf16[2,1024,1,128]{3,0,2,1:T(2,128)(2,1)}), bf16[2,1024,1,128]{3,0,2,1:T(2,128)(2,1)}, u32[]{:S(2)}, u32[]{:S(2)}) async-start(bf16[2,1024,1,128]{3,0,2,1:T(2,128)(2,1)} %copy.209), calls=%async_computation.2 | async-start | bytes 1048576 | tf_op jit(solution)/shard_map/all_to_all | solution.py:22
  146.2 30.7 %all-to-all-start.4 = ((bf16[1,128,16,8,64]{1,4,2,0,3:T(8,128)(2,1)}), bf16[1,128,16,8,64]{1,4,2,0,3:T(8,128)(2,1)S(1)}, u32[]{:S(2)}, u32[]{:S(2)}) async-start(bf16[1,128,16,8,64]{1,4,2,0,3:T(8,128)(2,1)} %copy.216), calls=%async_computation.4 | async-start | bytes 4194304 | tf_op jit(solution)/shard_map/all_to_all | solution.py:164
  178.9 39.5 %all-to-all-start.3 = ((bf16[8,1,128,512]{3,2,1,0:T(8,128)(2,1)}), bf16[8,1,128,512]{3,2,1,0:T(8,128)(2,1)}, u32[]{:S(2)}, u32[]{:S(2)}) async-start(bf16[8,1,128,512]{3,2,1,0:T(8,128)(2,1)} %broadcast_in_dim.77), calls=%async_computation.3 | async-start | bytes 2097152 | tf_op jit(solution)/shard_map/all_to_all | solution.py:37
  218.4 20.6 %all-to-all-start.1 = ((bf16[1,1024,4,128]{3,2,0,1:T(4,128)(2,1)}), bf16[1,1024,4,128]{3,2,0,1:T(4,128)(2,1)S(1)}, u32[]{:S(2)}, u32[]{:S(2)}) async-start(bf16[1,1024,4,128]{3,2,0,1:T(4,128)(2,1)} %copy.201), calls=%async_computation.1 | async-start | bytes 2097152 | tf_op jit(solution)/shard_map/all_to_all | solution.py:140
  239.0 25.5 %all-to-all-start.5 = ((bf16[16,64,512]{2,1,0:T(8,128)(2,1)}), bf16[16,64,512]{2,1,0:T(8,128)(2,1)S(1)}, u32[]{:S(2)}, u32[]{:S(2)}) async-start(bf16[16,64,512]{2,1,0:T(8,128)(2,1)} %bitcast.54), calls=%async_computation.5 | async-start | bytes 2097152 | tf_op jit(solution)/shard_map/all_to_all | solution.py:54
where the time goes:
time: 266 us; the launch traced here: 265 us
  waiting for transfers between devices  98.7 us (37%)
  matrix products  88.3 us (33%)
  local copies, waits for them, and re-layouts  39.2 us (15%)
  starting transfers between devices  29.5 us (11%)
  other arithmetic  8.58 us (3%)
    all_to_all x2, waiting for transfers between devices, side_by_side(): lax.all_to_all(both, axis, split_axis=split_dim, concat_axis=concat_dim,...  53.1 us
    dot_general x2, matrix products, attention_grads(): jnp.einsum(back_form, score_grad, key_block, preferred_element_type=jnp.f...  32.5 us
    dot_general x2, matrix products, attention_grads(): jnp.einsum('shqk,sqhd->skhd', score_grad, query_block, preferred_element_...  31.4 us
    all_to_all x1, waiting for transfers between devices, shards(): lax.all_to_all(split_input, 'seq', split_axis=3, concat_axis=1, tiled=True)  21.8 us
    all_to_all x1, waiting for transfers between devices, summed_on_arrival(): pieces = lax.all_to_all(in_blocks(value, dim, size), axis, 0, 0, tiled=True)  13.6 us
    all_to_all x1, waiting for transfers between devices, shards(): lax.all_to_all(query_out, 'seq', split_axis=1, concat_axis=2, tiled=True)  10.3 us
    unnamed x13, local copies, waits for them, and re-layouts  9.98 us
    all_to_all x2, starting transfers between devices, side_by_side(): lax.all_to_all(both, axis, split_axis=split_dim, concat_axis=concat_dim,...  8.82 us
  transfers between devices with their start and end apart: 6, of which 5 were waited for; matrix products, arithmetic and copies ran while one was open for 21% of the time, Pallas kernels for 0%

commit v1 on v0

v1 whole, which is shorter than its diff:
```python
import math

import jax
import jax.numpy as jnp
from jax import lax
from jax.experimental import pallas as pl
from jax.experimental.pallas import tpu as pltpu
from jax.sharding import Mesh, PartitionSpec as P

D = 8192
HQ = 32
HK = 4
HD = 128
LEN = 1024
BLK = 128
NBLK = LEN // BLK
WIN = 5
SCALE = HD ** (-0.5)
EXP2_SCALE = SCALE * math.log2(math.e)
MASKED = -1e30
GROUP = HQ // HK
NT = (((1,), (1,)), ((), ()))
NN = (((1,), (0,)), ((), ()))


def dot(a, b, dims):
    return lax.dot_general(a, b, dims, preferred_element_type=jnp.float32)


def attention_kernel(
    info, q_own, do_own, q_oth, do_oth, k_ref, v_ref,
    dq_own, dq_oth, dk_ref, dv_ref,
    k_t, dk_acc, dv_acc, bias_ref,
):
    chip, core = info[0], info[1]
    k_t[...] = k_ref[...].reshape(LEN, HD).T
    dk_acc[...] = jnp.zeros_like(dk_acc)
    dv_acc[...] = jnp.zeros_like(dv_acc)
    for tile in range(2):
        q_ref, do_ref, dq_ref = ((q_own, do_own, dq_own), (q_oth, do_oth, dq_oth))[tile]
        block = 2 * chip + (core if tile == 0 else 1 - core)
        first = jnp.maximum(block - (WIN - 1), 0)
        rows = pl.ds(pl.multiple_of(first * BLK, BLK), WIN * BLK)
        k_pos = first * BLK + lax.broadcasted_iota(jnp.int32, (WIN * BLK, 2 * BLK), 0)
        lane = lax.broadcasted_iota(jnp.int32, (1, 2 * BLK), 1)
        q_pos = block * BLK + (lane & (BLK - 1))
        begin = jnp.zeros_like(q_pos)
        end = jnp.int32(0)
        for sample in range(8):
            end = end + info[2 + sample]
            begin = jnp.where(end <= q_pos, end, begin)
        allowed = (k_pos >= begin) & (k_pos <= q_pos)
        bias_ref[...] = jnp.where(allowed, 0.0, MASKED)
        k_win = k_ref[pl.ds(first, WIN)].reshape(WIN * BLK, HD)
        v_win = v_ref[pl.ds(first, WIN)].reshape(WIN * BLK, HD)
        for pair in range(GROUP // 2):
            cols = [slice((2 * pair + i) * HD, (2 * pair + i + 1) * HD) for i in range(2)]
            q_two = jnp.concatenate([q_ref[:, c] for c in cols], axis=0)
            do_two = jnp.concatenate([do_ref[:, c] for c in cols], axis=0)
            scores = dot(k_win, q_two, NT) * EXP2_SCALE + bias_ref[...]
            exponent = jnp.exp2(scores - jnp.max(scores, axis=0, keepdims=True))
            probs = exponent * (1.0 / jnp.sum(exponent, axis=0, keepdims=True))
            dprobs = dot(v_win, do_two, NT)
            delta = jnp.sum(probs * dprobs, axis=0, keepdims=True)
            dscores = (probs * (dprobs - delta)).astype(jnp.bfloat16)
            dv_acc[rows, :] += dot(probs.astype(jnp.bfloat16), do_two, NN)
            dk_acc[rows, :] += dot(dscores, q_two, NN)
            dq_t = dot(k_t[:, rows], dscores, NN) * SCALE
            for i in range(2):
                dq_ref[:, cols[i]] = dq_t[:, i * BLK : (i + 1) * BLK].T.astype(jnp.bfloat16)
    dk_ref[...] = (dk_acc[...] * SCALE).astype(jnp.bfloat16).reshape(dk_ref.shape)
    dv_ref[...] = dv_acc[...].astype(jnp.bfloat16).reshape(dv_ref.shape)


def attention(info, queries, out_grad, others, kv):
    width = GROUP * HD
    half = HQ * HD // 2
    own = pl.BlockSpec((BLK, width), lambda g, s: (0, s[1] * 2 + g))

    def other(which):
        return pl.BlockSpec((None, BLK, width), lambda g, s: (which, 0, g))

    def keys(which):
        return pl.BlockSpec((NBLK, None, BLK, HD), lambda g, s: (0, which, 0, g))

    part = pl.BlockSpec((NBLK, BLK, HD), lambda g, s: (0, 0, g))
    part_shape = jax.ShapeDtypeStruct((NBLK, BLK, 2 * HD), jnp.bfloat16)
    return pl.pallas_call(
        attention_kernel,
        grid_spec=pltpu.PrefetchScalarGridSpec(
            num_scalar_prefetch=1,
            grid=(2,),
            in_specs=[own, own, other(0), other(1), keys(0), keys(1)],
            out_specs=[own, pl.BlockSpec((BLK, width), lambda g, s: (0, g)), part, part],
            scratch_shapes=[
                pltpu.VMEM((HD, LEN), jnp.bfloat16),
                pltpu.VMEM((LEN, HD), jnp.float32),
                pltpu.VMEM((LEN, HD), jnp.float32),
                pltpu.VMEM((WIN * BLK, 2 * BLK), jnp.float32),
            ],
        ),
        out_shape=[
            jax.ShapeDtypeStruct((BLK, HQ * HD), jnp.bfloat16),
            jax.ShapeDtypeStruct((BLK, half), jnp.bfloat16),
            part_shape,
            part_shape,
        ],
        name="attention_backward",
    )(info, queries, out_grad, others, others, kv, kv)


SWAP = [(0, 1), (1, 0)]


def shards(queries, key_states, value_states, out_grad, layer_input, lengths):
    chip, core = lax.axis_index("x"), lax.axis_index("core")
    queries, out_grad = queries[0], out_grad[0]
    half = HQ * HD // 2

    kv = jnp.stack([key_states[0], value_states[0]]).reshape(2, BLK, 2, 2 * HD)
    kv = jnp.broadcast_to(jnp.moveaxis(kv, 2, 0)[None], (4, 2, 2, BLK, 2 * HD))
    kv = lax.all_to_all(kv.reshape(NBLK, 2, BLK, 2 * HD), ("x", "core"), 0, 0, tiled=True)

    def other_half(a):
        return lax.dynamic_slice(a, (0, (1 - core) * half), (BLK, half))

    others = lax.ppermute(jnp.stack([other_half(queries), other_half(out_grad)]), "core", SWAP)

    x_z = lax.all_to_all(layer_input[0].reshape(BLK, 4, 4, D // 16), "z", 2, 0, tiled=True)
    x_own = x_z.reshape(4 * BLK, D // 4)
    x_oth = lax.ppermute(x_own, "core", SWAP)

    info = jnp.concatenate([jnp.stack([chip, core]).astype(jnp.int32), lengths[0]])
    dq_own, dq_oth, dk, dv = attention(info, queries, out_grad, others, kv)

    dv = lax.all_to_all(dv.reshape(4, 2 * BLK, 2 * HD), "x", 0, 0, tiled=True)
    dv = jnp.sum(dv.astype(jnp.float32), axis=0).astype(jnp.bfloat16)

    dv_z = lax.all_to_all(jnp.broadcast_to(dv[None], (4, 2 * BLK, 2 * HD)), "z", 0, 0, tiled=True)
    dv_z = dv_z.reshape(4, 2, BLK, 2 * HD)
    dv_own = lax.dynamic_index_in_dim(dv_z, core, 1, False).reshape(4 * BLK, 2 * HD)
    dv_oth = lax.dynamic_index_in_dim(dv_z, 1 - core, 1, False).reshape(4 * BLK, 2 * HD)
    over_tokens = (((0,), (0,)), ((), ()))
    weight = dot(x_own, dv_own, over_tokens) + dot(x_oth, dv_oth, over_tokens)
    weight = weight.astype(jnp.bfloat16).reshape(32, 64, 2 * HD)
    weight = lax.all_to_all(weight, ("y", "x", "core"), 0, 0, tiled=True)
    weight = jnp.sum(weight.reshape(16, 2, 64, 2 * HD).astype(jnp.float32), axis=0)
    weight = jnp.moveaxis(weight, 0, 1).reshape(64, HK * HD) / math.sqrt(16 * LEN)

    dq_got = lax.ppermute(dq_oth, "core", SWAP)
    query_grad = lax.dynamic_update_slice(dq_own, dq_got, (0, (1 - core) * half))

    dk = lax.all_to_all(dk, ("x", "core"), 0, 0, tiled=True)
    dk = jnp.sum(dk.reshape(4, 2, BLK, 2 * HD).astype(jnp.float32), axis=0)
    key_grad = jnp.moveaxis(dk.astype(jnp.bfloat16), 0, 1).reshape(BLK, HK * HD)

    dv_rows = dv.reshape(2, BLK, 2 * HD)
    dv_keep = lax.dynamic_index_in_dim(dv_rows, core, 0, False)
    dv_got = lax.ppermute(lax.dynamic_index_in_dim(dv_rows, 1 - core, 0, False), "core", SWAP)
    low = jnp.where(core == 0, dv_keep, dv_got)
    high = jnp.where(core == 0, dv_got, dv_keep)
    value_grad = jnp.concatenate([low, high], axis=1)
    return query_grad[None], key_grad[None], value_grad[None], weight


def solution(mesh):
    whole = Mesh(mesh.devices.reshape(4, 4, 4, 2), ("y", "z", "x", "core"))
    rows = P(("y", "z"), ("x", "core"), None)
    return jax.shard_map(
        shards,
        mesh=whole,
        in_specs=(rows,) * 5 + (P(("y", "z"), None),),
        out_specs=(rows,) * 3 + (P(("y", "z", "x", "core"), None),),
        check_vma=False,
    )
```

time: 266 us -> 140 us (0.53)
  matrix products: 88.3 us -> 3.06 us
  waiting for transfers between devices: 98.7 us -> 64.9 us
  local copies, waits for them, and re-layouts: 39.2 us -> 15.8 us
  Pallas kernels: 0 us -> 15.2 us
  blocking collectives: 0 us -> 12.9 us
  starting transfers between devices: 29.5 us -> 23.4 us
  other arithmetic: 8.58 us -> 2.68 us
    dot_general x10 -> x2, matrix products: 81 us -> 3.06 us  [dot(): return lax.dot_general(a, b, dims, preferred_element_type=jnp.float32)]
    all_to_all x6 -> x5, waiting for transfers between devices: 98.7 us -> 64.4 us  [the longest x1 23.9 us: shards(): lax.all_to_all(layer_input[0].reshape(BLK, 4, 4, D // 16), 'z', 2, 0, til...]
    pallas_call x0 -> x1, Pallas kernels: none -> 15.2 us  [attention(): pl.pallas_call(attention_kernel, grid_spec=pltpu.PrefetchScalarGridSpec(n...]
    all_to_all x0 -> x1, blocking collectives: none -> 12.9 us  [shards(): dv = lax.all_to_all(dv.reshape(4, 2 * BLK, 2 * HD), 'x', 0, 0, tiled=True)]
    all_to_all x4 -> x0, local copies, waits for them, and re-layouts: 9.63 us -> none  [the longest x2 7.5 us: side_by_side(): lax.all_to_all(both, axis, split_axis=split_dim, concat_axis=concat_dim,...]
    sub x1 -> x0, matrix products: 7.35 us -> none  [attention_grads(): exponent = jnp.exp(scores - row_peak)]
    all_to_all x6 -> x5, starting transfers between devices: 29.5 us -> 22.3 us  [the longest x1 5.55 us: shards(): lax.all_to_all(layer_input[0].reshape(BLK, 4, 4, D // 16), 'z', 2, 0, til...]
    unnamed x13 -> x16, local copies, waits for them, and re-layouts: 9.98 us -> 4.02 us
  transfers between devices with their start and end apart: 6 -> 9, of which waited for: 5 -> 6; matrix products, arithmetic and copies ran while one was open for 21% -> 10% of each run, Pallas kernels for 0% -> 11%
where the time goes in v1:
time: 140 us; the launch traced here: 139 us
  waiting for transfers between devices  64.9 us (46%)
  starting transfers between devices  23.4 us (17%)
  local copies, waits for them, and re-layouts  15.8 us (11%)
  Pallas kernels  15.2 us (11%)
  blocking collectives  12.9 us (9%)
  matrix products  3.06 us (2%)
  other arithmetic  2.68 us (2%)
    all_to_all x1, waiting for transfers between devices, shards(): lax.all_to_all(layer_input[0].reshape(BLK, 4, 4, D // 16), 'z', 2, 0, til...  23.9 us
    pallas_call x1, Pallas kernels, attention(): pl.pallas_call(attention_kernel, grid_spec=pltpu.PrefetchScalarGridSpec(n...  15.2 us
    all_to_all x1, waiting for transfers between devices, shards(): weight = lax.all_to_all(weight, ('y', 'x', 'core'), 0, 0, tiled=True)  13.6 us
    all_to_all x1, blocking collectives, shards(): dv = lax.all_to_all(dv.reshape(4, 2 * BLK, 2 * HD), 'x', 0, 0, tiled=True)  12.9 us
    all_to_all x1, waiting for transfers between devices, shards(): lax.all_to_all(kv.reshape(NBLK, 2, BLK, 2 * HD), ('x', 'core'), 0, 0, til...  12.5 us
    all_to_all x1, waiting for transfers between devices, shards(): lax.all_to_all(jnp.broadcast_to(dv[None], (4, 2 * BLK, 2 * HD)), 'z', 0,...  8.58 us
    all_to_all x1, waiting for transfers between devices, shards(): dk = lax.all_to_all(dk, ('x', 'core'), 0, 0, tiled=True)  5.78 us
    all_to_all x1, starting transfers between devices, shards(): lax.all_to_all(layer_input[0].reshape(BLK, 4, 4, D // 16), 'z', 2, 0, til...  5.55 us
  transfers between devices with their start and end apart: 9, of which 6 were waited for; matrix products, arithmetic and copies ran while one was open for 10% of the time, Pallas kernels for 11%

profile of v1, /device:TPU:0, one launch (start us, length us, event | category | flops | bytes accessed | tf_op | source)
XLA Modules:
  0.0 138.8 jit_solution(10208174117039199457)
XLA Ops:
  0.6 3.3 %reshape_squeeze.3 = bf16[128,4,4,512]{3,2,1,0:T(4,128)(2,1)S(1)} reshape(bf16[1,128,8192]{2,1,0:T(8,128)(2,1)} %param.10) | data formatting | bytes 4194304 | tf_op jit(solution)/shard_map/reshape;squeeze | solution.py:129
  4.0 2.1 %copy.19 = bf16[128,4,4,512]{3,1,0,2:T(4,128)(2,1)} copy(bf16[128,4,4,512]{3,2,1,0:T(4,128)(2,1)S(1)} %reshape_squeeze.3) | data formatting | bytes 4194304 | tf_op jit(solution)/shard_map/reshape;squeeze | solution.py:129
  6.1 0.0 copy-start.2
  6.1 5.5 %all-to-all-start.4 = ((bf16[128,4,4,512]{3,1,0,2:T(4,128)(2,1)}), bf16[128,4,4,512]{3,1,0,2:T(4,128)(2,1)S(1)}, u32[]{:S(2)}, u32[]{:S(2)}) async-start(bf16[128,4,4,512]{3,1,0,2:T(4,128)(2,1)} %copy.19), calls=%async_computation.4 | async-start | bytes 4194304 | tf_op jit(solution)/shard_map/all_to_all | solution.py:129
  11.6 0.0 copy-done.2
  11.7 0.0 copy-start.3
  11.7 0.0 copy-start.4
  11.7 1.2 constant_dynamic-slice_fusion.2
  12.8 1.1 pad_maximum_fusion
  13.9 0.0 collective-permute-start
  13.9 0.0 copy-done.3
  13.9 0.0 copy-done.4
  13.9 0.1 reshape.55
  14.1 23.9 %all-to-all-done.4 = bf16[128,4,4,512]{3,1,0,2:T(4,128)(2,1)S(1)} async-done(((bf16[128,4,4,512]{3,1,0,2:T(4,128)(2,1)}), bf16[128,4,4,512]{3,1,0,2:T(4,128)(2,1)S(1)}, u32[]{:S(2)}, u32[]{:S(2)}) %all-to-all-start.4) | async-done | bytes 2097184 | tf_op jit(solution)/shard_map/all_to_all | solution.py:129
  38.0 0.0 copy-start.1
  38.0 1.2 broadcast_in_dim.20
  39.2 4.3 %all-to-all-start = ((bf16[8,2,128,256]{3,2,1,0:T(8,128)(2,1)}), bf16[8,2,128,256]{3,2,1,0:T(8,128)(2,1)S(1)}, u32[]{:S(2)}, u32[]{:S(2)}) async-start(bf16[8,2,128,256]{3,2,1,0:T(8,128)(2,1)} %bitcast.48), calls=%async_computation | async-start | bytes 2097152 | tf_op jit(solution)/shard_map/all_to_all | solution.py:122
  43.5 0.0 copy-done.1
  43.5 0.0 copy-start.5
  43.5 2.2 %copy.24 = bf16[64,8,4,512]{3,1,2,0:T(8,128)(2,1)S(1)} copy(bf16[64,8,4,512]{3,2,1,0:T(4,128)(2,1)} %bitcast.47) | data formatting | bytes 4194304
  45.7 0.6 collective-permute-start.3
  46.3 0.0 copy-done.5
  46.3 0.6 pad_add_fusion.info
  46.9 12.5 %all-to-all-done.k_ref.v_ref = bf16[8,2,128,256]{3,2,1,0:T(8,128)(2,1)S(1)} async-done(((bf16[8,2,128,256]{3,2,1,0:T(8,128)(2,1)}), bf16[8,2,128,256]{3,2,1,0:T(8,128)(2,1)S(1)}, u32[]{:S(2)}, u32[]{:S(2)}) %all-to-all-start) | async-done | bytes 1048608 | tf_op jit(solution)/shard_map/all_to_all | solution.py:122
  59.4 0.0 copy-start
  59.4 0.0 collective-permute-done.q_oth.do_oth
  59.4 1.0 copy-done
  60.4 15.2 %attention_backward.1 = (bf16[128,4096]{1,0:T(8,128)(2,1)}, bf16[128,2048]{1,0:T(8,128)(2,1)}, bf16[8,128,256]{2,1,0:T(8,128)(2,1)}, bf16[8,128,256]{2,1,0:T(8,128)(2,1)}) custom-call(s32[10]{0:T(128)} %pad_add_fusion.info, bf16[128,4096]{1,0:T(8,128)(2,1)} %bitcast.50, bf16[128,4096]{1,0:T(8,128)(2,1)} %bitcast.51, ...), custom_call_target="tpu_custom_call" | custom-call | tf_op jit(solution)/shard_map/attention_backward/pallas_call | solution.py:88
  75.6 12.9 %all_to_all.40 = bf16[4,256,256]{2,1,0:T(8,128)(2,1)S(1)} all-to-all(bf16[4,256,256]{2,1,0:T(8,128)(2,1)} %bitcast.59), channel_id=1, replica_groups=mesh['y'=4,'z'=4,'x'=4,'core'=2] {'x'}, dimensions={0} | all-to-all | bytes 1048576 | tf_op jit(solution)/shard_map/all_to_all | solution.py:136
  88.5 0.1 reduce_sum.34
  88.6 0.9 broadcast_in_dim.24
  89.5 3.5 %all-to-all-start.3 = ((bf16[4,256,256]{2,1,0:T(8,128)(2,1)}), bf16[4,256,256]{2,1,0:T(8,128)(2,1)S(1)}, u32[]{:S(2)}, u32[]{:S(2)}) async-start(bf16[4,256,256]{2,1,0:T(8,128)(2,1)} %broadcast_in_dim.24), calls=%async_computation.3 | async-start | bytes 1048576 | tf_op jit(solution)/shard_map/all_to_all | solution.py:139
  93.0 8.6 %all-to-all-done.3 = bf16[4,256,256]{2,1,0:T(8,128)(2,1)S(1)} async-done(((bf16[4,256,256]{2,1,0:T(8,128)(2,1)}), bf16[4,256,256]{2,1,0:T(8,128)(2,1)S(1)}, u32[]{:S(2)}, u32[]{:S(2)}) %all-to-all-start.3) | async-done | bytes 524320 | tf_op jit(solution)/shard_map/all_to_all | solution.py:139
  101.5 3.5 %all-to-all-start.1 = ((bf16[8,128,256]{2,1,0:T(8,128)(2,1)}), bf16[8,128,256]{2,1,0:T(8,128)(2,1)S(1)}, u32[]{:S(2)}, u32[]{:S(2)}) async-start(bf16[8,128,256]{2,1,0:T(8,128)(2,1)} %get-tuple-element.10), calls=%async_computation.1 | async-start | bytes 1048576 | tf_op jit(solution)/shard_map/all_to_all | solution.py:153
  105.1 0.7 fusion.2
  105.8 0.0 collective-permute-done.3
  105.8 2.3 %fusion.1 = bf16[2048,256]{0,1:T(8,128)(2,1)S(1)} fusion(f32[256,2048]{1,0:T(8,128)S(1)} %fusion.2, bf16[512,256]{1,0:T(8,128)(2,1)S(1)} %bitcast.58, bf16[512,2048]{1,0:T(8,128)(2,1)} %collective-permute-done.3), kind=kOutput, calls=%fused_computation.2 | convolution fusion | flops 537919488 | bytes 5505024 | tf_op jit(solution)/shard_map/dot_general | solution.py:27
  108.2 0.0 copy-start.6
  108.2 1.3 copy.20
  109.5 5.8 %all-to-all-done.1 = bf16[8,128,256]{2,1,0:T(8,128)(2,1)S(1)} async-done(((bf16[8,128,256]{2,1,0:T(8,128)(2,1)}), bf16[8,128,256]{2,1,0:T(8,128)(2,1)S(1)}, u32[]{:S(2)}, u32[]{:S(2)}) %all-to-all-start.1) | async-done | bytes 524320 | tf_op jit(solution)/shard_map/all_to_all | solution.py:153
  115.3 5.4 %all-to-all-start.5 = ((bf16[32,64,256]{2,1,0:T(8,128)(2,1)}), bf16[32,64,256]{2,1,0:T(8,128)(2,1)S(1)}, u32[]{:S(2)}, u32[]{:S(2)}) async-start(bf16[32,64,256]{2,1,0:T(8,128)(2,1)} %bitcast.23), calls=%async_computation.5 | async-start | bytes 2097152 | tf_op jit(solution)/shard_map/all_to_all | solution.py:146
  120.7 0.0 copy-done.6
  120.7 0.4 collective-permute-start.1
  121.1 0.2 collective-permute-start.2
  121.3 0.1 reduce_sum.33
  121.4 0.1 copy.18
  121.5 0.8 copy.22
  122.3 0.5 collective-permute-done.2
  122.8 0.7 maximum_bitcast_fusion
  123.5 0.0 collective-permute-done.1
  123.5 0.8 bitcast_dynamic-update-slice_fusion
  124.3 13.6 %all-to-all-done.5 = bf16[32,64,256]{2,1,0:T(8,128)(2,1)S(1)} async-done(((bf16[32,64,256]{2,1,0:T(8,128)(2,1)}), bf16[32,64,256]{2,1,0:T(8,128)(2,1)S(1)}, u32[]{:S(2)}, u32[]{:S(2)}) %all-to-all-start.5) | async-done | bytes 1048608 | tf_op jit(solution)/shard_map/all_to_all | solution.py:146
  137.9 0.1 convert_reduce_fusion
  138.1 0.7 copy.23
  (6 shorter events, 0.1 us)
Async XLA Ops:
  6.1 5.6 %copy-start.2 = (bf16[1,128,4096]{2,1,0:T(8,128)(2,1)S(1)}, bf16[1,128,4096]{2,1,0:T(8,128)(2,1)}, u32[]{:S(2)}) copy-start(bf16[1,128,4096]{2,1,0:T(8,128)(2,1)} %param.6) | copy-start | bytes 3145732
  6.1 31.9 %all-to-all-start.4 = ((bf16[128,4,4,512]{3,1,0,2:T(4,128)(2,1)}), bf16[128,4,4,512]{3,1,0,2:T(4,128)(2,1)S(1)}, u32[]{:S(2)}, u32[]{:S(2)}) async-start(bf16[128,4,4,512]{3,1,0,2:T(4,128)(2,1)} %copy.19), calls=%async_computation.4 | async-start | bytes 4194304 | tf_op jit(solution)/shard_map/all_to_all | solution.py:129
  11.7 2.3 %copy-start.3 = (bf16[1,128,512]{2,1,0:T(8,128)(2,1)S(1)}, bf16[1,128,512]{2,1,0:T(8,128)(2,1)}, u32[]{:S(2)}) copy-start(bf16[1,128,512]{2,1,0:T(8,128)(2,1)} %param.8) | copy-start | bytes 393220
  11.7 2.3 %copy-start.4 = (bf16[1,128,512]{2,1,0:T(8,128)(2,1)S(1)}, bf16[1,128,512]{2,1,0:T(8,128)(2,1)}, u32[]{:S(2)}) copy-start(bf16[1,128,512]{2,1,0:T(8,128)(2,1)} %param.7) | copy-start | bytes 393220
  13.9 45.5 %collective-permute-start = (bf16[2,128,2048]{2,1,0:T(8,128)(2,1)}, bf16[2,128,2048]{2,1,0:T(8,128)(2,1)}, u32[]{:S(2)}, u32[]{:S(2)}) collective-permute-start(bf16[2,128,2048]{2,1,0:T(8,128)(2,1)} %pad_maximum_fusion), channel_id=1, source_target_pairs={{0,1},{1,0},{2,3},{3,2},{4,5},{5,4},{6,7},{7,6},{8,9},{9,8},{10,11... | collective-permute-start | bytes 3145736 | tf_op jit(solution)/shard_map/ppermute | solution.py:127
  38.0 5.5 %copy-start.1 = (bf16[128,4,4,512]{3,1,0,2:T(4,128)(2,1)}, bf16[128,4,4,512]{3,1,0,2:T(4,128)(2,1)S(1)}, u32[]{:S(2)}) copy-start(bf16[128,4,4,512]{3,1,0,2:T(4,128)(2,1)S(1)} %all-to-all-done.4) | copy-start | bytes 6291460
  39.2 20.2 %all-to-all-start = ((bf16[8,2,128,256]{3,2,1,0:T(8,128)(2,1)}), bf16[8,2,128,256]{3,2,1,0:T(8,128)(2,1)S(1)}, u32[]{:S(2)}, u32[]{:S(2)}) async-start(bf16[8,2,128,256]{3,2,1,0:T(8,128)(2,1)} %bitcast.48), calls=%async_computation | async-start | bytes 2097152 | tf_op jit(solution)/shard_map/all_to_all | solution.py:122
  43.5 2.8 %copy-start.5 = (s32[1,8]{1,0:T(1,128)S(1)}, s32[1,8]{1,0:T(1,128)}, u32[]{:S(2)}) copy-start(s32[1,8]{1,0:T(1,128)} %param.11) | copy-start | bytes 100
  45.7 60.1 %collective-permute-start.3 = (bf16[512,2048]{1,0:T(8,128)(2,1)S(1)}, bf16[512,2048]{1,0:T(8,128)(2,1)}, u32[]{:S(2)}, u32[]{:S(2)}) collective-permute-start(bf16[512,2048]{1,0:T(8,128)(2,1)S(1)} %bitcast.45), channel_id=1, source_target_pairs={{0,1},{1,0},{2,3},{3,2},{4,5},{5,4},{6,7},{7,6},{8,9},{9,8},{10,11... | collective-permute-start | bytes 6291464 | tf_op jit(solution)/shard_map/ppermute | solution.py:131
  59.4 1.0 copy-start
  89.5 12.1 %all-to-all-start.3 = ((bf16[4,256,256]{2,1,0:T(8,128)(2,1)}), bf16[4,256,256]{2,1,0:T(8,128)(2,1)S(1)}, u32[]{:S(2)}, u32[]{:S(2)}) async-start(bf16[4,256,256]{2,1,0:T(8,128)(2,1)} %broadcast_in_dim.24), calls=%async_computation.3 | async-start | bytes 1048576 | tf_op jit(solution)/shard_map/all_to_all | solution.py:139
  101.5 13.7 %all-to-all-start.1 = ((bf16[8,128,256]{2,1,0:T(8,128)(2,1)}), bf16[8,128,256]{2,1,0:T(8,128)(2,1)S(1)}, u32[]{:S(2)}, u32[]{:S(2)}) async-start(bf16[8,128,256]{2,1,0:T(8,128)(2,1)} %get-tuple-element.10), calls=%async_computation.1 | async-start | bytes 1048576 | tf_op jit(solution)/shard_map/all_to_all | solution.py:153
  108.2 12.6 %copy-start.6 = (bf16[128,2048]{1,0:T(8,128)(2,1)S(1)}, bf16[128,2048]{1,0:T(8,128)(2,1)}, u32[]{:S(2)}) copy-start(bf16[128,2048]{1,0:T(8,128)(2,1)} %get-tuple-element.9) | copy-start | bytes 1572868
  115.3 22.7 %all-to-all-start.5 = ((bf16[32,64,256]{2,1,0:T(8,128)(2,1)}), bf16[32,64,256]{2,1,0:T(8,128)(2,1)S(1)}, u32[]{:S(2)}, u32[]{:S(2)}) async-start(bf16[32,64,256]{2,1,0:T(8,128)(2,1)} %bitcast.23), calls=%async_computation.5 | async-start | bytes 2097152 | tf_op jit(solution)/shard_map/all_to_all | solution.py:146
  120.7 2.8 %collective-permute-start.1 = (bf16[128,2048]{1,0:T(8,128)(2,1)S(1)}, bf16[128,2048]{1,0:T(8,128)(2,1)S(1)}, u32[]{:S(2)}, u32[]{:S(2)}) collective-permute-start(bf16[128,2048]{1,0:T(8,128)(2,1)S(1)} %copy-done.6), channel_id=1, source_target_pairs={{0,1},{1,0},{2,3},{3,2},{4,5},{5,4},{6,7},{7,6},{8,9},{9,8},{10,11... | collective-permute-start | bytes 1572872 | tf_op jit(solution)/shard_map/ppermute | solution.py:150
  121.1 1.7 %collective-permute-start.2 = (bf16[128,256]{1,0:T(8,128)(2,1)S(1)}, bf16[128,256]{1,0:T(8,128)(2,1)S(1)}, u32[]{:S(2)}, u32[]{:S(2)}) collective-permute-start(bf16[128,256]{1,0:T(8,128)(2,1)S(1)} %dynamic-slice_bitcast_fusion), channel_id=1, source_target_pairs={{0,1},{1,0},{2,3},{3,2},{4,5},{5,4},{6,7},{7,6},{8,9},{9,8},{10,11... | collective-permute-start | bytes 196616 | tf_op jit(solution)/shard_map/ppermute | solution.py:159

commit v2 on v1

v2 whole, which is shorter than its diff:
```python
import math

import jax
import jax.numpy as jnp
from jax import lax
from jax.experimental import pallas as pl
from jax.experimental.pallas import tpu as pltpu
from jax.sharding import Mesh, PartitionSpec as P


D = 8192
HQ = 32
HK = 4
HD = 128
LEN = 1024
BLK = 128
SPAN = 6
WIN = 5
GROUP = HQ // HK
PAIRS = GROUP // 2
WIDTH = GROUP * HD
HALF = HQ * HD // 2
COLS = 2 * HD
FEAT = D // 16
SCALE = HD ** (-0.5)
EXP2_SCALE = SCALE * math.log2(math.e)
MASKED = -1e30
NT = (((1,), (1,)), ((), ()))
NN = (((1,), (0,)), ((), ()))
TN = (((0,), (0,)), ((), ()))
SWAP = [(0, 1), (1, 0)]
BF16 = jnp.bfloat16
F32 = jnp.float32
IN_HBM = pl.BlockSpec(memory_space=pl.ANY)
IN_SMEM = pl.BlockSpec(memory_space=pltpu.SMEM)
IN_VMEM = pl.BlockSpec(memory_space=pltpu.VMEM)


def dot(a, b, dims):
    return lax.dot_general(a, b, dims, preferred_element_type=F32)


def near(value):
    return pltpu.with_memory_space_constraint(value, pltpu.VMEM)


def lanes(start, size):
    return pl.ds(pl.multiple_of(start, HD), size)


def call(kernel, in_specs, outs, operands, scratch=(), flops=0, exps=0, moved=1 << 20, room=4):
    out_specs = [IN_HBM if isinstance(o, jax.ShapeDtypeStruct) else IN_VMEM for o in outs]
    operands = [near(a) if spec is IN_VMEM else a for a, spec in zip(operands, in_specs)]
    return pl.pallas_call(
        kernel,
        in_specs=list(in_specs),
        out_specs=out_specs,
        out_shape=list(outs),
        scratch_shapes=list(scratch),
        cost_estimate=pl.CostEstimate(flops=flops, transcendentals=exps, bytes_accessed=moved),
        compiler_params=pltpu.CompilerParams(vmem_limit_bytes=room << 20),
    )(*operands)


def run_copies(copies):
    for copy in copies:
        copy.start()
    for copy in copies:
        copy.wait()


def pack_kernel(x_ref, out_ref, sems):
    run_copies(
        [
            pltpu.make_async_copy(
                x_ref.at[:, pl.ds((y * 4 + z) * FEAT, FEAT)], out_ref.at[z, y], sems.at[4 * z + y]
            )
            for z in range(4)
            for y in range(4)
        ]
    )


def pack(layer_input):
    return call(
        pack_kernel, [IN_HBM], [pltpu.VMEM((4, 4, BLK, FEAT), BF16)], [layer_input],
        [pltpu.SemaphoreType.DMA((16,))], moved=2 << 20,
    )[0]


def other_kernel(info, q_ref, do_ref, out_ref, sems):
    cols = lanes((1 - info[1]) * HALF, HALF)
    run_copies(
        [
            pltpu.make_async_copy(ref.at[:, cols], out_ref.at[i], sems.at[i])
            for i, ref in enumerate((q_ref, do_ref))
        ]
    )


def other_heads(info, queries, out_grad):
    return call(
        other_kernel, [IN_SMEM, IN_HBM, IN_HBM],
        [pltpu.VMEM((2, BLK, HALF), BF16)], [info, queries, out_grad],
        [pltpu.SemaphoreType.DMA((2,))], moved=1 << 20,
    )[0]


def side_parity(core, side):
    return core if side == 0 else 1 - core


def first_place(core, side, small):
    return 4 if small else side_parity(core, side)


def gather_keys(core, sources, which, start, buf):
    for j, kv in enumerate(sources):
        for side in range(2):
            buf[2 * j + side_parity(core, side)] = kv[side, which, :, lanes(start, HD)]


def write_bias(info, side, small, bias_ref):
    chip, core = info[0], info[1]
    win = 2 if small else WIN
    k_pos = (2 * chip - 4 + first_place(core, side, small)) * BLK + lax.broadcasted_iota(
        jnp.int32, (win * BLK, BLK), 0
    )
    lane = lax.broadcasted_iota(jnp.int32, (1, BLK), 1)
    q_pos = (2 * chip + side_parity(core, side)) * BLK + lane
    begin = jnp.zeros_like(q_pos)
    end = jnp.int32(0)
    for sample in range(8):
        end = end + info[2 + sample]
        begin = jnp.where(end <= q_pos, end, begin)
    allowed = (k_pos >= begin) & (k_pos <= q_pos)
    bias_ref[side, : win * BLK] = jnp.where(allowed, 0.0, MASKED)


def masked(raw, bias):
    return raw * EXP2_SCALE + jnp.concatenate([bias, bias], axis=1)


class Heads:
    def __init__(self, core, own_ref, oth_ref, which, group):
        self.own, self.oth, self.which = own_ref, oth_ref, which
        self.own_start = core * HALF + group * WIDTH
        self.oth_start = group * WIDTH

    def pair(self, side, pair):
        if side == 0:
            two = self.own[:, lanes(self.own_start + pair * COLS, COLS)]
        else:
            two = self.oth[self.which, :, lanes(self.oth_start + pair * COLS, COLS)]
        return jnp.concatenate([two[:, :HD], two[:, HD:]], axis=0)


def window_rows(core, side, small):
    return lanes(first_place(core, side, small) * BLK, (2 if small else WIN) * BLK)


def window(buf, core, side, small):
    win = 2 if small else WIN
    return buf[pl.ds(first_place(core, side, small), win)].reshape(win * BLK, HD)


def probs_body(small, core, group, q, do, k_buf, stat_ref, bias_ref, dv_acc):
    win = 2 if small else WIN

    def raw_scores(step):
        side, pair = divmod(step, PAIRS)
        return dot(window(k_buf, core, side, small), q.pair(side, pair), NT)

    following = raw_scores(0)
    for step in range(2 * PAIRS):
        side, pair = divmod(step, PAIRS)
        raw = following
        if step + 1 < 2 * PAIRS:
            following = raw_scores(step + 1)
        scores = masked(raw, bias_ref[side, : win * BLK])
        peak = jnp.max(scores, axis=0, keepdims=True)
        exponent = jnp.exp2(scores - peak)
        over = 1.0 / jnp.sum(exponent, axis=0, keepdims=True)
        stat_ref[group, 0, step : step + 1] = peak
        stat_ref[group, 1, step : step + 1] = over
        probs = (exponent * over).astype(BF16)
        dv_acc[window_rows(core, side, small), :] += dot(probs, do.pair(side, pair), NN)


def probs_kernel(
    info, q_own, do_own, others, kv_two, kv_one, kv_here,
    dv_two, dv_one, dv_here, stat_ref, bias_ref,
    k_buf, dv_acc,
):
    chip, core = info[0], info[1]
    for small in (True, False):
        @pl.when((chip == 0) == small)
        def _():
            for side in range(2):
                write_bias(info, side, small, bias_ref)

            def group_step(group, carry):
                gather_keys(core, (kv_two, kv_one, kv_here), 0, group * HD, k_buf)
                dv_acc[...] = jnp.zeros_like(dv_acc)
                q = Heads(core, q_own, others, 0, group)
                do = Heads(core, do_own, others, 1, group)
                probs_body(small, core, group, q, do, k_buf, stat_ref, bias_ref, dv_acc)
                for j, part in enumerate((dv_two, dv_one, dv_here)):
                    for side in range(2):
                        rows = lanes((2 * j + side_parity(core, side)) * BLK, BLK)
                        part[side, :, lanes(group * HD, HD)] = dv_acc[rows, :].astype(part.dtype)
                return carry

            lax.fori_loop(0, 2, group_step, 0)


def scores_body(small, core, q, do, k_buf, v_buf, k_t, stat_ref, bias_ref, dk_acc, dq_refs, at):
    win = 2 if small else WIN

    def products(step):
        side, pair = divmod(step, PAIRS)
        raw = dot(window(k_buf, core, side, small), q.pair(side, pair), NT)
        return raw, dot(window(v_buf, core, side, small), do.pair(side, pair), NT)

    following = products(0)
    for step in range(2 * PAIRS):
        side, pair = divmod(step, PAIRS)
        raw, dprobs = following
        if step + 1 < 2 * PAIRS:
            following = products(step + 1)
        rows = window_rows(core, side, small)
        peak, over = stat_ref[0, step : step + 1], stat_ref[1, step : step + 1]
        scores = masked(raw, bias_ref[side, : win * BLK])
        probs = jnp.exp2(scores - peak) * over
        delta = jnp.sum(probs * dprobs, axis=0, keepdims=True)
        dscores = (probs * (dprobs - delta)).astype(BF16)
        dk_acc[rows, :] += dot(dscores, q.pair(side, pair), NN)
        dq_t = dot(k_t[:, rows], dscores, NN) * SCALE
        for i in range(2):
            start = at + (2 * pair + i) * HD
            dq = dq_t[:, i * BLK : (i + 1) * BLK].T.astype(BF16)
            dq_refs[side][:, start : start + HD] = dq


def scores_kernel(group, info, q_own, do_own, others, kv_two, kv_one, kv_here, stat_ref, bias_ref, *refs):
    chip, core = info[0], info[1]
    if group == 0:
        dq_own, dq_oth, dk_acc, k_buf, v_buf, k_t = refs
    else:
        past_own, past_oth, past_dk, dq_own, dq_oth, dk_two, dk_one, dk_here = refs[:8]
        k_buf, v_buf, k_t, dk_acc = refs[8:]
        dq_own[:, :WIDTH] = past_own[...]
        dq_oth[:, :WIDTH] = past_oth[...]
    gather_keys(core, (kv_two, kv_one, kv_here), 0, group * HD, k_buf)
    gather_keys(core, (kv_two, kv_one, kv_here), 1, group * HD, v_buf)
    k_t[...] = k_buf[...].reshape(SPAN * BLK, HD).T
    dk_acc[...] = jnp.zeros_like(dk_acc)
    q = Heads(core, q_own, others, 0, group)
    do = Heads(core, do_own, others, 1, group)
    stat = stat_ref.at[group]
    for small in (True, False):
        @pl.when((chip == 0) == small)
        def _():
            scores_body(
                small, core, q, do, k_buf, v_buf, k_t, stat, bias_ref, dk_acc,
                (dq_own, dq_oth), group * WIDTH,
            )
    if group == 1:
        for j, part in enumerate((dk_two, dk_one, dk_here)):
            for side in range(2):
                rows = lanes((2 * j + side_parity(core, side)) * BLK, BLK)
                part[side, :, :HD] = (past_dk[rows, :] * SCALE).astype(part.dtype)
                part[side, :, HD:] = (dk_acc[rows, :] * SCALE).astype(part.dtype)


PARTS = [pltpu.VMEM((2, BLK, COLS), kind) for kind in (BF16, BF16, F32)]
KEYS = pltpu.VMEM((SPAN, BLK, HD), BF16)
TURNED = pltpu.VMEM((HD, SPAN * BLK), BF16)
TOTAL = pltpu.VMEM((SPAN * BLK, HD), F32)
PRODUCT = 2 * 16 * 2 * BLK * WIN * BLK * HD


def attention_probs(operands):
    stats = pltpu.VMEM((2, 2, 2 * PAIRS, 2 * BLK), F32)
    bias = pltpu.VMEM((2, WIN * BLK, BLK), F32)
    return call(
        probs_kernel, [IN_SMEM] + [IN_VMEM] * 6, PARTS + [stats, bias], operands,
        [KEYS, TOTAL], flops=2 * PRODUCT, exps=PRODUCT // 256, moved=4 << 20, room=16,
    )


def attention_scores(group, past, stats, bias, operands):
    def kernel(*refs):
        scores_kernel(group, *refs)

    wide = WIDTH * (group + 1)
    outs = [pltpu.VMEM((BLK, wide), BF16)] * 2 + ([TOTAL] if group == 0 else PARTS)
    scratch = [KEYS, KEYS, TURNED] + ([] if group == 0 else [TOTAL])
    return call(
        kernel, [IN_SMEM] + [IN_VMEM] * (8 + len(past)), outs,
        [*operands, stats, bias, *past], scratch,
        flops=2 * PRODUCT, exps=PRODUCT // 512, moved=4 << 20, room=16,
    )


def weight_kernel(info, x_own, x_oth, *refs):
    dv, out_ref = refs[:-1], refs[-1]
    z = info[2 + 8]
    sources = [lax.rem(z + 4 - back, 4) for back in range(4)]
    dv_rows = jnp.concatenate([dv[back][side] for back in range(4) for side in range(2)], axis=0)
    for y in range(4):
        x_rows = jnp.concatenate(
            [x[source, y] for source in sources for x in (x_own, x_oth)], axis=0
        )
        out_ref[y * FEAT : (y + 1) * FEAT] = dot(x_rows, dv_rows, TN).astype(BF16)


def weight_part(info, x_own, x_oth, dv):
    return call(
        weight_kernel, [IN_SMEM] + [IN_VMEM] * 6,
        [pltpu.VMEM((4 * FEAT, COLS), BF16)], [info, x_own, x_oth, *dv],
        flops=2 * 4 * FEAT * COLS * 8 * BLK, moved=6 << 20, room=16,
    )[0]


def weight_sum_kernel(got, out_ref):
    for side in range(2):
        total = got[side].astype(F32)
        for source in range(1, 16):
            total = total + got[2 * source + side].astype(F32)
        out_ref[:, side * COLS : (side + 1) * COLS] = total * (1.0 / math.sqrt(16 * LEN))


def weight_sum(got):
    return pl.pallas_call(
        weight_sum_kernel,
        in_specs=[IN_VMEM],
        out_specs=IN_VMEM,
        out_shape=jax.ShapeDtypeStruct((64, HK * HD), F32),
        compiler_params=pltpu.CompilerParams(vmem_limit_bytes=4 << 20),
        name="weight_sum",
    )(near(got))


def sum_kernel(here, one, two, out_ref):
    out_ref[...] = (here[...] + one[...].astype(F32) + two[...].astype(F32)).astype(BF16)


def part_sum(parts):
    return call(sum_kernel, [IN_VMEM] * 3, [pltpu.VMEM((2, BLK, COLS), BF16)], parts)[0]


def finish_kernel(info, dq_own, dq_got, dk, dv, got, query_grad, key_grad, value_grad, sems):
    core = info[1]
    keep, other = lanes(core * HALF, HALF), lanes((1 - core) * HALF, HALF)
    keep_kv, other_kv = lanes(core * COLS, COLS), lanes((1 - core) * COLS, COLS)
    moves = [
        (dq_own, query_grad.at[:, keep]),
        (dq_got, query_grad.at[:, other]),
        (dk.at[0], key_grad.at[:, keep_kv]),
        (got.at[0], key_grad.at[:, other_kv]),
        (dv.at[0], value_grad.at[:, keep_kv]),
        (got.at[1], value_grad.at[:, other_kv]),
    ]
    run_copies(
        [pltpu.make_async_copy(a, b, sems.at[i]) for i, (a, b) in enumerate(moves)]
    )


def finish(info, dq_own, dq_got, dk, dv, got):
    outs = [jax.ShapeDtypeStruct((BLK, width * HD), BF16) for width in (HQ, HK, HK)]
    return call(
        finish_kernel, [IN_SMEM] + [IN_VMEM] * 5, outs,
        [info, dq_own, dq_got, dk, dv, got], [pltpu.SemaphoreType.DMA((6,))], moved=2 << 20,
    )


def exchange(value, axes):
    return lax.all_to_all(value, axes, 0, 0, tiled=True)


def shards(queries, key_states, value_states, out_grad, layer_input, lengths):
    chip, core, depth = lax.axis_index("x"), lax.axis_index("core"), lax.axis_index("z")
    queries, out_grad = queries[0], out_grad[0]
    info = jnp.concatenate(
        [jnp.stack([chip, core]).astype(jnp.int32), lengths[0], depth.reshape(1).astype(jnp.int32)]
    )

    def pairs(a, b, which, width):
        cut = [lax.dynamic_slice(v, (0, which * width), (BLK, width)) for v in (a, b)]
        return jnp.stack(cut)

    kv_keep = pairs(key_states[0], value_states[0], core, COLS)
    kv_send = pairs(key_states[0], value_states[0], 1 - core, COLS)
    kv_here = jnp.stack([kv_keep, lax.ppermute(kv_send, "core", SWAP)])
    kv_two = lax.ppermute(kv_here, "x", [(0, 2), (1, 3)])
    kv_one = lax.ppermute(kv_here, "x", [(0, 1), (1, 2), (2, 3)])

    others = lax.ppermute(other_heads(info, queries, out_grad), "core", SWAP)

    x_own = exchange(pack(layer_input[0]), "z")
    x_oth = lax.ppermute(x_own, "core", SWAP)

    operands = (info, queries, out_grad, others, kv_two, kv_one, kv_here)
    dv_two, dv_one, dv_here, stats, bias = attention_probs(operands)
    past = ()
    for group in range(2):
        past = attention_scores(group, past, stats, bias, operands)
    dq_own, dq_oth, dk_two, dk_one, dk_here = past

    def summed(here, one, two):
        one = lax.ppermute(one, "x", [(1, 0), (2, 1), (3, 2)])
        two = lax.ppermute(two, "x", [(2, 0), (3, 1)])
        return part_sum([here, one, two])

    dv = summed(dv_here, dv_one, dv_two)
    dv_z = [dv] + [
        lax.ppermute(dv, "z", [(i, (i + away) % 4) for i in range(4)]) for away in (1, 2, 3)
    ]
    weight = weight_part(info, x_own, x_oth, dv_z)
    weight = weight_sum(exchange(weight.reshape(32, 64, COLS), ("y", "x", "core")))

    dk = summed(dk_here, dk_one, dk_two)
    dq_got = lax.ppermute(dq_oth, "core", SWAP)
    got = lax.ppermute(jnp.stack([dk[1], dv[1]]), "core", SWAP)
    query_grad, key_grad, value_grad = finish(info, dq_own, dq_got, dk, dv, got)
    return query_grad[None], key_grad[None], value_grad[None], weight


def solution(mesh):
    whole = Mesh(mesh.devices.reshape(4, 4, 4, 2), ("y", "z", "x", "core"))
    rows = P(("y", "z"), ("x", "core"), None)
    return jax.shard_map(
        shards,
        mesh=whole,
        in_specs=(rows,) * 5 + (P(("y", "z"), None),),
        out_specs=(rows,) * 3 + (P(("y", "z", "x", "core"), None),),
        check_vma=False,
    )
```

time: 140 us -> 124 us (0.89)
  waiting for transfers between devices: 64.9 us -> 39.1 us
  blocking collectives: 12.9 us -> 31.7 us
  local copies, waits for them, and re-layouts: 15.8 us -> 8.93 us
  matrix products: 3.06 us -> 0 us
  other arithmetic: 2.68 us -> 0.15 us
  Pallas kernels: 15.2 us -> 17.4 us
    all_to_all x5 -> x1, waiting for transfers between devices: 64.4 us -> 0.01 us  [exchange(): return lax.all_to_all(value, axes, 0, 0, tiled=True)]
    ppermute x2 -> x12, waiting for transfers between devices: 0.51 us -> 39.1 us  [the longest x2 12.2 us: summed(): one = lax.ppermute(one, 'x', [(1, 0), (2, 1), (3, 2)])]
    all_to_all x1, blocking collectives: 12.9 us -> 31.7 us  [exchange(): return lax.all_to_all(value, axes, 0, 0, tiled=True)]
    ppermute x2 -> x12, starting transfers between devices: 0.24 us -> 16.7 us  [the longest x1 4.64 us: shards(): kv_two = lax.ppermute(kv_here, 'x', [(0, 2), (1, 3)])]
    all_to_all x5 -> x1, starting transfers between devices: 22.3 us -> 6.59 us  [exchange(): return lax.all_to_all(value, axes, 0, 0, tiled=True)]
    another operation x2 -> x0, local copies, waits for them, and re-layouts: 5.46 us -> none  [shards(): layer_input[0].reshape(BLK, 4, 4, D // 16)]
    unnamed x16 -> x38, local copies, waits for them, and re-layouts: 4.02 us -> 8.9 us
    dot_general x2 -> x0, matrix products: 3.06 us -> none  [dot(): return lax.dot_general(a, b, dims, preferred_element_type=jnp.float32)]
  transfers between devices with their start and end apart: 9 -> 15, of which waited for: 6 -> 11; matrix products, arithmetic and copies ran while one was open for 10% -> 0% of each run, Pallas kernels for 11% -> 11%
where the time goes in v2:
time: 124 us; the launch traced here: 122 us
  waiting for transfers between devices  39.1 us (32%)
  blocking collectives  31.7 us (26%)
  starting transfers between devices  23.7 us (19%)
  Pallas kernels  17.4 us (14%)
  local copies, waits for them, and re-layouts  8.93 us (7%)
    all_to_all x1, blocking collectives, exchange(): return lax.all_to_all(value, axes, 0, 0, tiled=True)  31.7 us
    pallas_call x9, Pallas kernels, call(): pl.pallas_call(kernel, in_specs=list(in_specs), out_specs=out_specs, out_...  16.6 us
    ppermute x2, waiting for transfers between devices, summed(): one = lax.ppermute(one, 'x', [(1, 0), (2, 1), (3, 2)])  12.2 us
    ppermute x2, waiting for transfers between devices, summed(): two = lax.ppermute(two, 'x', [(2, 0), (3, 1)])  9.11 us
    unnamed x38, local copies, waits for them, and re-layouts  8.9 us
    ppermute x3, waiting for transfers between devices, shards(): lax.ppermute(dv, 'z', [(i, (i + away) % 4) for i in range(4)])  6.88 us
    all_to_all x1, starting transfers between devices, exchange(): return lax.all_to_all(value, axes, 0, 0, tiled=True)  6.59 us
    ppermute x1, waiting for transfers between devices, shards(): kv_two = lax.ppermute(kv_here, 'x', [(0, 2), (1, 3)])  5.02 us
  transfers between devices with their start and end apart: 15, of which 11 were waited for; matrix products, arithmetic and copies ran while one was open for 0% of the time, Pallas kernels for 11%

profile of v2, /device:TPU:0, one launch (start us, length us, event | category | flops | bytes accessed | tf_op | source)
XLA Modules:
  0.0 121.8 jit_solution(2695266097790983932)
XLA Ops:
  0.6 0.0 copy-start.5
  0.6 1.6 %copy-done.5 = bf16[1,128,8192]{2,1,0:T(8,128)(2,1)S(1)} copy-done((bf16[1,128,8192]{2,1,0:T(8,128)(2,1)S(1)}, bf16[1,128,8192]{2,1,0:T(8,128)(2,1)}, u32[]{:S(2)}) %copy-start.5) | copy-done | bytes 2097176
  2.2 0.5 shard_map.100
  2.7 0.0 copy-start.18
  2.7 0.0 copy-start
  2.7 0.0 copy-start.16
  2.7 0.0 copy-start.17
  2.7 31.7 %all_to_all.10.x_own = bf16[4,4,128,512]{3,2,1,0:T(8,128)(2,1)S(1)} all-to-all(bf16[4,4,128,512]{3,2,1,0:T(8,128)(2,1)S(1)} %shard_map.100), channel_id=1, replica_groups=mesh['y'=4,'z'=4,'x'=4,'core'=2] {'z'}, dimensions={0} | all-to-all | bytes 4194304 | tf_op jit(solution)/shard_map/all_to_all | solution.py:379
  34.4 0.0 collective-permute-start.10
  34.4 0.0 copy-done.18
  34.4 0.1 pad_add_fusion.info.refs_0_
  34.5 0.0 copy-done
  34.5 1.2 %copy-done.1 = bf16[1,128,4096]{2,1,0:T(8,128)(2,1)S(1)} copy-done((bf16[1,128,4096]{2,1,0:T(8,128)(2,1)S(1)}, bf16[1,128,4096]{2,1,0:T(8,128)(2,1)}, u32[]{:S(2)}) %copy-start.1) | copy-done | bytes 1048600
  35.7 1.6 %shard_map.93 = bf16[2,128,2048]{2,1,0:T(8,128)(2,1)} custom-call(s32[11]{0:T(128)S(1)} %pad_add_fusion.info.refs_0_, bf16[128,4096]{1,0:T(8,128)(2,1)S(1)} %bitcast.14, bf16[128,4096]{1,0:T(8,128)(2,1)S(1)} %bitcast.18), custom_call_target="tpu_custom_call" | custom-call | bytes 1048576 | tf_op jit(solution)/shard_map/pallas_call | solution.py:54
  37.4 0.6 collective-permute-start
  37.9 0.0 copy-done.16
  37.9 0.0 copy-done.17
  38.0 0.1 collective-permute-start.1
  38.1 2.5 %collective-permute-done.1 = bf16[2,128,256]{2,1,0:T(8,128)(2,1)S(1)} collective-permute-done((bf16[2,128,256]{2,1,0:T(8,128)(2,1)S(1)}, bf16[2,128,256]{2,1,0:T(8,128)(2,1)S(1)}, u32[]{:S(2)}, u32[]{:S(2)}) %collective-permute-start.1) | collective-permute-done | bytes 131104 | tf_op jit(solution)/shard_map/ppermute | solution.py:395
  40.7 3.4 %collective-permute-start.3 = (bf16[2,2,128,256]{3,2,1,0:T(8,128)(2,1)S(1)}, bf16[2,2,128,256]{3,2,1,0:T(8,128)(2,1)S(1)}, u32[]{:S(2)}, u32[]{:S(2)}) collective-permute-start(bf16[2,2,128,256]{3,2,1,0:T(8,128)(2,1)S(1)} %pad_maximum_fusion.kv_here.refs_6_), channel_id=1, source_target_pairs={{0,2},{2,4},{4,6},{1,3},{3,5},{5,7},{8,10},{10,12},{12,14},{9,11},... | collective-permute-start | bytes 786440 | tf_op jit(solution)/shard_map/ppermute | solution.py:397
  44.1 4.6 %collective-permute-start.2 = (bf16[2,2,128,256]{3,2,1,0:T(8,128)(2,1)S(1)}, bf16[2,2,128,256]{3,2,1,0:T(8,128)(2,1)S(1)}, u32[]{:S(2)}, u32[]{:S(2)}) collective-permute-start(bf16[2,2,128,256]{3,2,1,0:T(8,128)(2,1)S(1)} %pad_maximum_fusion.kv_here.refs_6_), channel_id=1, source_target_pairs={{0,4},{2,6},{1,5},{3,7},{8,12},{10,14},{9,13},{11,15},{16,20},{18,... | collective-permute-start | bytes 786440 | tf_op jit(solution)/shard_map/ppermute | solution.py:396
  48.7 2.0 %collective-permute-done.3.kv_one.refs_5_ = bf16[2,2,128,256]{3,2,1,0:T(8,128)(2,1)S(1)} collective-permute-done((bf16[2,2,128,256]{3,2,1,0:T(8,128)(2,1)S(1)}, bf16[2,2,128,256]{3,2,1,0:T(8,128)(2,1)S(1)}, u32[]{:S(2)}, u32[]{:S(2)}) %collective-permute-start.3) | collective-permute-done | bytes 262176 | tf_op jit(solution)/shard_map/ppermute | solution.py:397
  50.7 5.0 %collective-permute-done.2.kv_two.refs_4_ = bf16[2,2,128,256]{3,2,1,0:T(8,128)(2,1)S(1)} collective-permute-done((bf16[2,2,128,256]{3,2,1,0:T(8,128)(2,1)S(1)}, bf16[2,2,128,256]{3,2,1,0:T(8,128)(2,1)S(1)}, u32[]{:S(2)}, u32[]{:S(2)}) %collective-permute-start.2) | collective-permute-done | bytes 262176 | tf_op jit(solution)/shard_map/ppermute | solution.py:396
  55.8 0.0 collective-permute-done.others.refs_3_
  55.8 1.3 %copy-done.2 = bf16[1,128,4096]{2,1,0:T(8,128)(2,1)S(1)} copy-done((bf16[1,128,4096]{2,1,0:T(8,128)(2,1)S(1)}, bf16[1,128,4096]{2,1,0:T(8,128)(2,1)}, u32[]{:S(2)}) %copy-start.2) | copy-done | bytes 1048600
  57.1 3.6 %shard_map.94 = (bf16[2,128,256]{2,1,0:T(8,128)(2,1)S(1)}, bf16[2,128,256]{2,1,0:T(8,128)(2,1)S(1)}, f32[2,128,256]{2,1,0:T(8,128)S(1)}, f32[2,2,8,256]{3,2,1,0:T(8,128)S(1)}, f32[2,640,128]{2,1,0:T(8,128)S(1)}) custom-call(s32[11]{0:T(128)S(1)} %pad_add_fusion.info.refs_0_, bf16[128,4096]{1,0:T(8,128)(2,1)S(1)} %bitcast.15, bf16[128,4096]{1,0:T(8,128)(2,1)S(1)} %bitcast.19, ...), custom_call_target="tpu_custom_call" | custom-call | flops 1342177280 | bytes 4194304 | tf_op jit(solution)/shard_map/pallas_call | solution.py:54
  60.7 0.0 copy-done.8
  60.7 0.0 copy-done.11
  60.7 0.0 copy-start.6
  60.7 0.0 copy-start.14
  60.7 1.3 %collective-permute-start.7 = (bf16[2,128,256]{2,1,0:T(8,128)(2,1)S(1)}, bf16[2,128,256]{2,1,0:T(8,128)(2,1)S(1)}, u32[]{:S(2)}, u32[]{:S(2)}) collective-permute-start(bf16[2,128,256]{2,1,0:T(8,128)(2,1)S(1)} %get-tuple-element.31), channel_id=1, source_target_pairs={{2,0},{4,2},{6,4},{3,1},{5,3},{7,5},{10,8},{12,10},{14,12},{11,9},... | collective-permute-start | bytes 393224 | tf_op jit(solution)/shard_map/ppermute | solution.py:412
  62.0 1.3 %collective-permute-start.8 = (bf16[2,128,256]{2,1,0:T(8,128)(2,1)S(1)}, bf16[2,128,256]{2,1,0:T(8,128)(2,1)S(1)}, u32[]{:S(2)}, u32[]{:S(2)}) collective-permute-start(bf16[2,128,256]{2,1,0:T(8,128)(2,1)S(1)} %get-tuple-element.32), channel_id=1, source_target_pairs={{4,0},{6,2},{5,1},{7,3},{12,8},{14,10},{13,9},{15,11},{20,16},{22,... | collective-permute-start | bytes 393224 | tf_op jit(solution)/shard_map/ppermute | solution.py:413
  63.3 4.3 %collective-permute-done.7.one = bf16[2,128,256]{2,1,0:T(8,128)(2,1)S(1)} collective-permute-done((bf16[2,128,256]{2,1,0:T(8,128)(2,1)S(1)}, bf16[2,128,256]{2,1,0:T(8,128)(2,1)S(1)}, u32[]{:S(2)}, u32[]{:S(2)}) %collective-permute-start.7) | collective-permute-done | bytes 131104 | tf_op jit(solution)/shard_map/ppermute | solution.py:412
  67.6 6.0 %collective-permute-done.8.two = bf16[2,128,256]{2,1,0:T(8,128)(2,1)S(1)} collective-permute-done((bf16[2,128,256]{2,1,0:T(8,128)(2,1)S(1)}, bf16[2,128,256]{2,1,0:T(8,128)(2,1)S(1)}, u32[]{:S(2)}, u32[]{:S(2)}) %collective-permute-start.8) | collective-permute-done | bytes 131104 | tf_op jit(solution)/shard_map/ppermute | solution.py:413
  73.7 1.2 %collective-permute-start.13 = (bf16[2,128,256]{2,1,0:T(8,128)(2,1)S(1)}, bf16[2,128,256]{2,1,0:T(8,128)(2,1)S(1)}, u32[]{:S(2)}, u32[]{:S(2)}) collective-permute-start(bf16[2,128,256]{2,1,0:T(8,128)(2,1)S(1)} %shard_map.98.dv.refs_0_), channel_id=1, source_target_pairs={{0,24},{8,0},{16,8},{24,16},{1,25},{9,1},{17,9},{25,17},{2,26},{10... | collective-permute-start | bytes 393224 | tf_op jit(solution)/shard_map/ppermute | solution.py:418
  74.9 1.5 %collective-permute-start.12 = (bf16[2,128,256]{2,1,0:T(8,128)(2,1)S(1)}, bf16[2,128,256]{2,1,0:T(8,128)(2,1)S(1)}, u32[]{:S(2)}, u32[]{:S(2)}) collective-permute-start(bf16[2,128,256]{2,1,0:T(8,128)(2,1)S(1)} %shard_map.98.dv.refs_0_), channel_id=1, source_target_pairs={{0,16},{8,24},{16,0},{24,8},{1,17},{9,25},{17,1},{25,9},{2,18},{10... | collective-permute-start | bytes 393224 | tf_op jit(solution)/shard_map/ppermute | solution.py:418
  76.4 0.0 collective-permute-start.11
  76.4 3.1 %collective-permute-done.13.refs_3_ = bf16[2,128,256]{2,1,0:T(8,128)(2,1)S(1)} collective-permute-done((bf16[2,128,256]{2,1,0:T(8,128)(2,1)S(1)}, bf16[2,128,256]{2,1,0:T(8,128)(2,1)S(1)}, u32[]{:S(2)}, u32[]{:S(2)}) %collective-permute-start.13) | collective-permute-done | bytes 131104 | tf_op jit(solution)/shard_map/ppermute | solution.py:418
  79.5 2.4 %collective-permute-done.12.refs_2_ = bf16[2,128,256]{2,1,0:T(8,128)(2,1)S(1)} collective-permute-done((bf16[2,128,256]{2,1,0:T(8,128)(2,1)S(1)}, bf16[2,128,256]{2,1,0:T(8,128)(2,1)S(1)}, u32[]{:S(2)}, u32[]{:S(2)}) %collective-permute-start.12) | collective-permute-done | bytes 131104 | tf_op jit(solution)/shard_map/ppermute | solution.py:418
  81.8 1.4 %collective-permute-done.11.refs_1_ = bf16[2,128,256]{2,1,0:T(8,128)(2,1)S(1)} collective-permute-done((bf16[2,128,256]{2,1,0:T(8,128)(2,1)S(1)}, bf16[2,128,256]{2,1,0:T(8,128)(2,1)S(1)}, u32[]{:S(2)}, u32[]{:S(2)}) %collective-permute-start.11) | collective-permute-done | bytes 131104 | tf_op jit(solution)/shard_map/ppermute | solution.py:418
  83.3 0.0 copy-done.6
  83.3 0.0 collective-permute-done.10.x_oth
  83.3 2.9 %shard_map.101 = bf16[2048,256]{1,0:T(8,128)(2,1)S(1)} custom-call(s32[11]{0:T(128)S(1)} %pad_add_fusion.info.refs_0_, bf16[4,4,128,512]{3,2,1,0:T(8,128)(2,1)S(1)} %all_to_all.10.x_own, bf16[4,4,128,512]{3,2,1,0:T(8,128)(2,1)} %collective-permute-done.10.x_oth, bf16[2,128,256]{2,1,0:T(8,128)(2,1)S(1)} %shard_map.98.dv.refs_0_, ...), custom_call_target="tpu_custom_call" | custom-call | flops 1073741824 | bytes 6291456 | tf_op jit(solution)/shard_map/pallas_call | solution.py:54
  86.2 0.0 copy-done.14
  86.2 1.0 copy-done.4
  87.2 6.6 %all-to-all-start.1 = ((bf16[32,64,256]{2,1,0:T(8,128)(2,1)}), bf16[32,64,256]{2,1,0:T(8,128)(2,1)S(1)}, u32[]{:S(2)}, u32[]{:S(2)}) async-start(bf16[32,64,256]{2,1,0:T(8,128)(2,1)} %bitcast.22), calls=%async_computation.1 | async-start | bytes 2097152 | tf_op jit(solution)/shard_map/all_to_all | solution.py:379
  93.8 0.0 copy-start.7
  93.8 1.1 copy-done.7
  94.9 0.9 copy-done.9
  95.8 0.9 copy-done.12
  96.8 0.8 copy-done.15
  97.5 3.2 %shard_map.95 = (bf16[128,1024]{1,0:T(8,128)(2,1)S(1)}, bf16[128,1024]{1,0:T(8,128)(2,1)S(1)}, f32[768,128]{1,0:T(8,128)S(1)}) custom-call(s32[11]{0:T(128)S(1)} %pad_add_fusion.info.refs_0_, bf16[128,4096]{1,0:T(8,128)(2,1)S(1)} %bitcast.16, bf16[128,4096]{1,0:T(8,128)(2,1)S(1)} %bitcast.20, bf16[2,128,2048]{2,1,0:T(8,128)(2,1)} %collective-permute-done.others.refs_3_, ...), custom_call_target="tpu_custom_call" | custom-call | flops 1342177280 | bytes 4194304 | tf_op jit(solution)/shard_map/pallas_call | solution.py:54
  100.8 3.1 %shard_map.96 = (bf16[128,2048]{1,0:T(8,128)(2,1)S(1)}, bf16[128,2048]{1,0:T(8,128)(2,1)S(1)}, bf16[2,128,256]{2,1,0:T(8,128)(2,1)S(1)}, bf16[2,128,256]{2,1,0:T(8,128)(2,1)S(1)}, f32[2,128,256]{2,1,0:T(8,128)S(1)}) custom-call(s32[11]{0:T(128)S(1)} %pad_add_fusion.info.refs_0_, bf16[128,4096]{1,0:T(8,128)(2,1)S(1)} %bitcast.17, ...), custom_call_target="tpu_custom_call" | custom-call | flops 1342177280 | bytes 4194304 | tf_op jit(solution)/shard_map/pallas_call | solution.py:54
  103.9 0.4 collective-permute-start.4
  104.2 1.3 %collective-permute-start.5 = (bf16[2,128,256]{2,1,0:T(8,128)(2,1)S(1)}, bf16[2,128,256]{2,1,0:T(8,128)(2,1)S(1)}, u32[]{:S(2)}, u32[]{:S(2)}) collective-permute-start(bf16[2,128,256]{2,1,0:T(8,128)(2,1)S(1)} %get-tuple-element.28), channel_id=1, source_target_pairs={{2,0},{4,2},{6,4},{3,1},{5,3},{7,5},{10,8},{12,10},{14,12},{11,9},... | collective-permute-start | bytes 393224 | tf_op jit(solution)/shard_map/ppermute | solution.py:412
  105.5 1.3 %collective-permute-start.6 = (bf16[2,128,256]{2,1,0:T(8,128)(2,1)S(1)}, bf16[2,128,256]{2,1,0:T(8,128)(2,1)S(1)}, u32[]{:S(2)}, u32[]{:S(2)}) collective-permute-start(bf16[2,128,256]{2,1,0:T(8,128)(2,1)S(1)} %get-tuple-element.29), channel_id=1, source_target_pairs={{4,0},{6,2},{5,1},{7,3},{12,8},{14,10},{13,9},{15,11},{20,16},{22,... | collective-permute-start | bytes 393224 | tf_op jit(solution)/shard_map/ppermute | solution.py:413
  106.8 7.9 %collective-permute-done.5.one = bf16[2,128,256]{2,1,0:T(8,128)(2,1)S(1)} collective-permute-done((bf16[2,128,256]{2,1,0:T(8,128)(2,1)S(1)}, bf16[2,128,256]{2,1,0:T(8,128)(2,1)S(1)}, u32[]{:S(2)}, u32[]{:S(2)}) %collective-permute-start.5) | collective-permute-done | bytes 131104 | tf_op jit(solution)/shard_map/ppermute | solution.py:412
  114.8 3.1 %collective-permute-done.6.two = bf16[2,128,256]{2,1,0:T(8,128)(2,1)S(1)} collective-permute-done((bf16[2,128,256]{2,1,0:T(8,128)(2,1)S(1)}, bf16[2,128,256]{2,1,0:T(8,128)(2,1)S(1)}, u32[]{:S(2)}, u32[]{:S(2)}) %collective-permute-start.6) | collective-permute-done | bytes 131104 | tf_op jit(solution)/shard_map/ppermute | solution.py:413
  118.0 0.1 collective-permute-start.9
  118.1 1.3 %collective-permute-done.9.got = bf16[2,128,256]{2,1,0:T(8,128)(2,1)S(1)} collective-permute-done((bf16[2,128,256]{2,1,0:T(8,128)(2,1)S(1)}, bf16[2,128,256]{2,1,0:T(8,128)(2,1)S(1)}, u32[]{:S(2)}, u32[]{:S(2)}) %collective-permute-start.9) | collective-permute-done | bytes 131104 | tf_op jit(solution)/shard_map/ppermute | solution.py:425
  119.4 0.0 collective-permute-done.4.dq_got
  119.4 1.6 %shard_map.99 = (bf16[128,4096]{1,0:T(8,128)(2,1)}, bf16[128,512]{1,0:T(8,128)(2,1)}, bf16[128,512]{1,0:T(8,128)(2,1)}) custom-call(s32[11]{0:T(128)S(1)} %pad_add_fusion.info.refs_0_, bf16[128,2048]{1,0:T(8,128)(2,1)S(1)} %get-tuple-element.25.dq_own, bf16[128,2048]{1,0:T(8,128)(2,1)S(1)} %collective-permute-done.4.dq_got, ...), custom_call_target="tpu_custom_call" | custom-call | bytes 2097152 | tf_op jit(solution)/shard_map/pallas_call | solution.py:54
  121.0 0.0 all-to-all-done.1.got
  121.0 0.8 weight_sum.1
  (23 shorter events, 0.2 us)
Async XLA Ops:
  0.6 1.6 %copy-start.5 = (bf16[1,128,8192]{2,1,0:T(8,128)(2,1)S(1)}, bf16[1,128,8192]{2,1,0:T(8,128)(2,1)}, u32[]{:S(2)}) copy-start(bf16[1,128,8192]{2,1,0:T(8,128)(2,1)} %param.10) | copy-start | bytes 6291460
  2.7 31.7 %copy-start.18 = (s32[1,8]{1,0:T(1,128)S(1)}, s32[1,8]{1,0:T(1,128)}, u32[]{:S(2)}) copy-start(s32[1,8]{1,0:T(1,128)} %param.11) | copy-start | bytes 100
  2.7 31.8 %copy-start = (bf16[1,128,4096]{2,1,0:T(8,128)(2,1)S(1)}, bf16[1,128,4096]{2,1,0:T(8,128)(2,1)}, u32[]{:S(2)}) copy-start(bf16[1,128,4096]{2,1,0:T(8,128)(2,1)} %param.6) | copy-start | bytes 3145732
  2.7 35.2 %copy-start.16 = (bf16[1,128,512]{2,1,0:T(8,128)(2,1)S(1)}, bf16[1,128,512]{2,1,0:T(8,128)(2,1)}, u32[]{:S(2)}) copy-start(bf16[1,128,512]{2,1,0:T(8,128)(2,1)} %param.8) | copy-start | bytes 393220
  2.7 35.2 %copy-start.17 = (bf16[1,128,512]{2,1,0:T(8,128)(2,1)S(1)}, bf16[1,128,512]{2,1,0:T(8,128)(2,1)}, u32[]{:S(2)}) copy-start(bf16[1,128,512]{2,1,0:T(8,128)(2,1)} %param.7) | copy-start | bytes 393220
  34.4 48.8 %collective-permute-start.10 = (bf16[4,4,128,512]{3,2,1,0:T(8,128)(2,1)S(1)}, bf16[4,4,128,512]{3,2,1,0:T(8,128)(2,1)}, u32[]{:S(2)}, u32[]{:S(2)}) collective-permute-start(bf16[4,4,128,512]{3,2,1,0:T(8,128)(2,1)S(1)} %all_to_all.10.x_own), channel_id=1, source_target_pairs={{0,1},{1,0},{2,3},{3,2},{4,5},{5,4},{6,7},{7,6},{8,9},{9,8},{10,11... | collective-permute-start | bytes 6291464 | tf_op jit(solution)/shard_map/ppermute | solution.py:402
  34.5 1.2 %copy-start.1 = (bf16[1,128,4096]{2,1,0:T(8,128)(2,1)S(1)}, bf16[1,128,4096]{2,1,0:T(8,128)(2,1)}, u32[]{:S(2)}) copy-start(bf16[1,128,4096]{2,1,0:T(8,128)(2,1)} %param.9) | copy-start | bytes 3145732
  37.4 18.4 %collective-permute-start = (bf16[2,128,2048]{2,1,0:T(8,128)(2,1)}, bf16[2,128,2048]{2,1,0:T(8,128)(2,1)}, u32[]{:S(2)}, u32[]{:S(2)}) collective-permute-start(bf16[2,128,2048]{2,1,0:T(8,128)(2,1)} %shard_map.93), channel_id=1, source_target_pairs={{0,1},{1,0},{2,3},{3,2},{4,5},{5,4},{6,7},{7,6},{8,9},{9,8},{10,11... | collective-permute-start | bytes 3145736 | tf_op jit(solution)/shard_map/ppermute | solution.py:399
  38.0 2.6 %collective-permute-start.1 = (bf16[2,128,256]{2,1,0:T(8,128)(2,1)S(1)}, bf16[2,128,256]{2,1,0:T(8,128)(2,1)S(1)}, u32[]{:S(2)}, u32[]{:S(2)}) collective-permute-start(bf16[2,128,256]{2,1,0:T(8,128)(2,1)S(1)} %pad_maximum_fusion.1), channel_id=1, source_target_pairs={{0,1},{1,0},{2,3},{3,2},{4,5},{5,4},{6,7},{7,6},{8,9},{9,8},{10,11... | collective-permute-start | bytes 393224 | tf_op jit(solution)/shard_map/ppermute | solution.py:395
  40.7 10.1 %collective-permute-start.3 = (bf16[2,2,128,256]{3,2,1,0:T(8,128)(2,1)S(1)}, bf16[2,2,128,256]{3,2,1,0:T(8,128)(2,1)S(1)}, u32[]{:S(2)}, u32[]{:S(2)}) collective-permute-start(bf16[2,2,128,256]{3,2,1,0:T(8,128)(2,1)S(1)} %pad_maximum_fusion.kv_here.refs_6_), channel_id=1, source_target_pairs={{0,2},{2,4},{4,6},{1,3},{3,5},{5,7},{8,10},{10,12},{12,14},{9,11},... | collective-permute-start | bytes 786440 | tf_op jit(solution)/shard_map/ppermute | solution.py:397
  44.1 11.7 %collective-permute-start.2 = (bf16[2,2,128,256]{3,2,1,0:T(8,128)(2,1)S(1)}, bf16[2,2,128,256]{3,2,1,0:T(8,128)(2,1)S(1)}, u32[]{:S(2)}, u32[]{:S(2)}) collective-permute-start(bf16[2,2,128,256]{3,2,1,0:T(8,128)(2,1)S(1)} %pad_maximum_fusion.kv_here.refs_6_), channel_id=1, source_target_pairs={{0,4},{2,6},{1,5},{3,7},{8,12},{10,14},{9,13},{11,15},{16,20},{18,... | collective-permute-start | bytes 786440 | tf_op jit(solution)/shard_map/ppermute | solution.py:396
  50.7 9.9 %copy-start.8 = (bf16[2,2,128,256]{3,2,1,0:T(8,128)(2,1)}, bf16[2,2,128,256]{3,2,1,0:T(8,128)(2,1)S(1)}, u32[]{:S(2)}) copy-start(bf16[2,2,128,256]{3,2,1,0:T(8,128)(2,1)S(1)} %collective-permute-done.3.kv_one.refs_5_) | copy-start | bytes 786436
  55.8 4.9 %copy-start.11 = (bf16[2,2,128,256]{3,2,1,0:T(8,128)(2,1)}, bf16[2,2,128,256]{3,2,1,0:T(8,128)(2,1)S(1)}, u32[]{:S(2)}) copy-start(bf16[2,2,128,256]{3,2,1,0:T(8,128)(2,1)S(1)} %collective-permute-done.2.kv_two.refs_4_) | copy-start | bytes 786436
  55.8 1.3 %copy-start.2 = (bf16[1,128,4096]{2,1,0:T(8,128)(2,1)S(1)}, bf16[1,128,4096]{2,1,0:T(8,128)(2,1)}, u32[]{:S(2)}) copy-start(bf16[1,128,4096]{2,1,0:T(8,128)(2,1)} %param.9) | copy-start | bytes 3145732
  60.7 22.6 %copy-start.6 = (f32[2,640,128]{2,1,0:T(8,128)}, f32[2,640,128]{2,1,0:T(8,128)S(1)}, u32[]{:S(2)}) copy-start(f32[2,640,128]{2,1,0:T(8,128)S(1)} %get-tuple-element.21.refs_8_) | copy-start | bytes 1966084
  60.7 25.5 %copy-start.14 = (f32[2,2,8,256]{3,2,1,0:T(8,128)}, f32[2,2,8,256]{3,2,1,0:T(8,128)S(1)}, u32[]{:S(2)}) copy-start(f32[2,2,8,256]{3,2,1,0:T(8,128)S(1)} %get-tuple-element.20.refs_7_) | copy-start | bytes 98308
  60.7 6.9 %collective-permute-start.7 = (bf16[2,128,256]{2,1,0:T(8,128)(2,1)S(1)}, bf16[2,128,256]{2,1,0:T(8,128)(2,1)S(1)}, u32[]{:S(2)}, u32[]{:S(2)}) collective-permute-start(bf16[2,128,256]{2,1,0:T(8,128)(2,1)S(1)} %get-tuple-element.31), channel_id=1, source_target_pairs={{2,0},{4,2},{6,4},{3,1},{5,3},{7,5},{10,8},{12,10},{14,12},{11,9},... | collective-permute-start | bytes 393224 | tf_op jit(solution)/shard_map/ppermute | solution.py:412
  62.0 11.6 %collective-permute-start.8 = (bf16[2,128,256]{2,1,0:T(8,128)(2,1)S(1)}, bf16[2,128,256]{2,1,0:T(8,128)(2,1)S(1)}, u32[]{:S(2)}, u32[]{:S(2)}) collective-permute-start(bf16[2,128,256]{2,1,0:T(8,128)(2,1)S(1)} %get-tuple-element.32), channel_id=1, source_target_pairs={{4,0},{6,2},{5,1},{7,3},{12,8},{14,10},{13,9},{15,11},{20,16},{22,... | collective-permute-start | bytes 393224 | tf_op jit(solution)/shard_map/ppermute | solution.py:413
  73.7 5.8 %collective-permute-start.13 = (bf16[2,128,256]{2,1,0:T(8,128)(2,1)S(1)}, bf16[2,128,256]{2,1,0:T(8,128)(2,1)S(1)}, u32[]{:S(2)}, u32[]{:S(2)}) collective-permute-start(bf16[2,128,256]{2,1,0:T(8,128)(2,1)S(1)} %shard_map.98.dv.refs_0_), channel_id=1, source_target_pairs={{0,24},{8,0},{16,8},{24,16},{1,25},{9,1},{17,9},{25,17},{2,26},{10... | collective-permute-start | bytes 393224 | tf_op jit(solution)/shard_map/ppermute | solution.py:418
  74.9 6.9 %collective-permute-start.12 = (bf16[2,128,256]{2,1,0:T(8,128)(2,1)S(1)}, bf16[2,128,256]{2,1,0:T(8,128)(2,1)S(1)}, u32[]{:S(2)}, u32[]{:S(2)}) collective-permute-start(bf16[2,128,256]{2,1,0:T(8,128)(2,1)S(1)} %shard_map.98.dv.refs_0_), channel_id=1, source_target_pairs={{0,16},{8,24},{16,0},{24,8},{1,17},{9,25},{17,1},{25,9},{2,18},{10... | collective-permute-start | bytes 393224 | tf_op jit(solution)/shard_map/ppermute | solution.py:418
  76.4 6.9 %collective-permute-start.11 = (bf16[2,128,256]{2,1,0:T(8,128)(2,1)S(1)}, bf16[2,128,256]{2,1,0:T(8,128)(2,1)S(1)}, u32[]{:S(2)}, u32[]{:S(2)}) collective-permute-start(bf16[2,128,256]{2,1,0:T(8,128)(2,1)S(1)} %shard_map.98.dv.refs_0_), channel_id=1, source_target_pairs={{0,8},{8,16},{16,24},{24,0},{1,9},{9,17},{17,25},{25,1},{2,10},{10... | collective-permute-start | bytes 393224 | tf_op jit(solution)/shard_map/ppermute | solution.py:418
  86.2 1.0 copy-start.4
  87.2 6.6 %copy-start.3 = (bf16[1,128,4096]{2,1,0:T(8,128)(2,1)S(1)}, bf16[1,128,4096]{2,1,0:T(8,128)(2,1)}, u32[]{:S(2)}) copy-start(bf16[1,128,4096]{2,1,0:T(8,128)(2,1)} %param.9) | copy-start | bytes 3145732
  87.2 33.9 %all-to-all-start.1 = ((bf16[32,64,256]{2,1,0:T(8,128)(2,1)}), bf16[32,64,256]{2,1,0:T(8,128)(2,1)S(1)}, u32[]{:S(2)}, u32[]{:S(2)}) async-start(bf16[32,64,256]{2,1,0:T(8,128)(2,1)} %bitcast.22), calls=%async_computation.1 | async-start | bytes 2097152 | tf_op jit(solution)/shard_map/all_to_all | solution.py:379
  93.8 1.1 copy-start.7
  94.9 0.9 copy-start.9
  95.8 0.9 copy-start.12
  96.8 0.8 copy-start.15
  97.5 3.3 %copy-start.10 = (bf16[2,2,128,256]{3,2,1,0:T(8,128)(2,1)S(1)}, bf16[2,2,128,256]{3,2,1,0:T(8,128)(2,1)}, u32[]{:S(2)}) copy-start(bf16[2,2,128,256]{3,2,1,0:T(8,128)(2,1)} %copy-done.8) | copy-start | bytes 786436
  97.5 3.3 %copy-start.13 = (bf16[2,2,128,256]{3,2,1,0:T(8,128)(2,1)S(1)}, bf16[2,2,128,256]{3,2,1,0:T(8,128)(2,1)}, u32[]{:S(2)}) copy-start(bf16[2,2,128,256]{3,2,1,0:T(8,128)(2,1)} %copy-done.11) | copy-start | bytes 786436
  103.9 15.5 %collective-permute-start.4 = (bf16[128,2048]{1,0:T(8,128)(2,1)S(1)}, bf16[128,2048]{1,0:T(8,128)(2,1)S(1)}, u32[]{:S(2)}, u32[]{:S(2)}) collective-permute-start(bf16[128,2048]{1,0:T(8,128)(2,1)S(1)} %get-tuple-element.26), channel_id=1, source_target_pairs={{0,1},{1,0},{2,3},{3,2},{4,5},{5,4},{6,7},{7,6},{8,9},{9,8},{10,11... | collective-permute-start | bytes 1572872 | tf_op jit(solution)/shard_map/ppermute | solution.py:424
  104.2 10.6 %collective-permute-start.5 = (bf16[2,128,256]{2,1,0:T(8,128)(2,1)S(1)}, bf16[2,128,256]{2,1,0:T(8,128)(2,1)S(1)}, u32[]{:S(2)}, u32[]{:S(2)}) collective-permute-start(bf16[2,128,256]{2,1,0:T(8,128)(2,1)S(1)} %get-tuple-element.28), channel_id=1, source_target_pairs={{2,0},{4,2},{6,4},{3,1},{5,3},{7,5},{10,8},{12,10},{14,12},{11,9},... | collective-permute-start | bytes 393224 | tf_op jit(solution)/shard_map/ppermute | solution.py:412
  105.5 12.3 %collective-permute-start.6 = (bf16[2,128,256]{2,1,0:T(8,128)(2,1)S(1)}, bf16[2,128,256]{2,1,0:T(8,128)(2,1)S(1)}, u32[]{:S(2)}, u32[]{:S(2)}) collective-permute-start(bf16[2,128,256]{2,1,0:T(8,128)(2,1)S(1)} %get-tuple-element.29), channel_id=1, source_target_pairs={{4,0},{6,2},{5,1},{7,3},{12,8},{14,10},{13,9},{15,11},{20,16},{22,... | collective-permute-start | bytes 393224 | tf_op jit(solution)/shard_map/ppermute | solution.py:413
  118.0 1.4 %collective-permute-start.9 = (bf16[2,128,256]{2,1,0:T(8,128)(2,1)S(1)}, bf16[2,128,256]{2,1,0:T(8,128)(2,1)S(1)}, u32[]{:S(2)}, u32[]{:S(2)}) collective-permute-start(bf16[2,128,256]{2,1,0:T(8,128)(2,1)S(1)} %pad_maximum_fusion.2), channel_id=1, source_target_pairs={{0,1},{1,0},{2,3},{3,2},{4,5},{5,4},{6,7},{7,6},{8,9},{9,8},{10,11... | collective-permute-start | bytes 393224 | tf_op jit(solution)/shard_map/ppermute | solution.py:425

commit v3 on v2

v3 whole, which is shorter than its diff:
```python
import math

import jax
import jax.numpy as jnp
from jax import lax
from jax.experimental import pallas as pl
from jax.experimental.pallas import tpu as pltpu
from jax.sharding import Mesh, PartitionSpec as P


D = 8192
HQ = 32
HK = 4
HD = 128
LEN = 1024
BLK = 128
SPAN = 6
WIN = 5
GROUP = HQ // HK
PAIRS = GROUP // 2
WIDTH = GROUP * HD
HALF = HQ * HD // 2
COLS = 2 * HD
FEAT = D // 16
SCALE = HD ** (-0.5)
EXP2_SCALE = SCALE * math.log2(math.e)
MASKED = -1e30
NT = (((1,), (1,)), ((), ()))
NN = (((1,), (0,)), ((), ()))
TN = (((0,), (0,)), ((), ()))
SWAP = [(0, 1), (1, 0)]
BF16 = jnp.bfloat16
F32 = jnp.float32
IN_HBM = pl.BlockSpec(memory_space=pltpu.HBM)
IN_SMEM = pl.BlockSpec(memory_space=pltpu.SMEM)
IN_VMEM = pl.BlockSpec(memory_space=pltpu.VMEM)
ANYWHERE = pl.BlockSpec(memory_space=pltpu.VMEM)


def dot(a, b, dims):
    return lax.dot_general(a, b, dims, preferred_element_type=F32)


def near(value):
    return pltpu.with_memory_space_constraint(value, pltpu.VMEM)


def far(value):
    return pltpu.with_memory_space_constraint(value, pltpu.HBM)


def lanes(start, size):
    return pl.ds(pl.multiple_of(start, HD), size)


def call(kernel, in_specs, outs, operands, scratch=(), flops=0, exps=0, moved=1 << 20, room=4, aliases=None):
    out_specs = [IN_HBM if isinstance(o, jax.ShapeDtypeStruct) else IN_VMEM for o in outs]
    place = {id(IN_VMEM): near, id(IN_HBM): far}
    operands = [place.get(id(spec), lambda a: a)(a) for a, spec in zip(operands, in_specs)]
    return pl.pallas_call(
        kernel,
        in_specs=list(in_specs),
        out_specs=out_specs,
        out_shape=list(outs),
        scratch_shapes=list(scratch),
        cost_estimate=pl.CostEstimate(flops=flops, transcendentals=exps, bytes_accessed=moved),
        compiler_params=pltpu.CompilerParams(vmem_limit_bytes=room << 20),
        input_output_aliases=aliases or {},
    )(*operands)


def run_copies(copies):
    for copy in copies:
        copy.start()
    for copy in copies:
        copy.wait()


def pack_kernel(x_ref, out_ref, sems):
    run_copies(
        [
            pltpu.make_async_copy(
                x_ref.at[:, pl.ds((y * 4 + z) * FEAT, FEAT)], out_ref.at[z, y], sems.at[4 * z + y]
            )
            for z in range(4)
            for y in range(4)
        ]
    )


def pack(layer_input):
    return call(
        pack_kernel, [IN_HBM], [pltpu.VMEM((4, 4, BLK, FEAT), BF16)], [layer_input],
        [pltpu.SemaphoreType.DMA((16,))], moved=2 << 20,
    )[0]


def other_kernel(info, q_ref, do_ref, out_ref, sems):
    cols = lanes((1 - info[1]) * HALF, HALF)
    run_copies(
        [
            pltpu.make_async_copy(ref.at[:, cols], out_ref.at[i], sems.at[i])
            for i, ref in enumerate((q_ref, do_ref))
        ]
    )


def other_heads(info, queries, out_grad):
    return call(
        other_kernel, [IN_SMEM, IN_HBM, IN_HBM],
        [pltpu.VMEM((2, BLK, HALF), BF16)], [info, queries, out_grad],
        [pltpu.SemaphoreType.DMA((2,))], moved=1 << 20,
    )[0]


def side_parity(core, side):
    return core if side == 0 else 1 - core


def first_place(core, side, small):
    return 4 if small else side_parity(core, side)


def gather_keys(core, sources, which, group, buf):
    for j, kv in enumerate(sources):
        for side in range(2):
            place = 2 * j + side_parity(core, side)
            buf[group, place] = kv[side, which, :, group * HD : (group + 1) * HD]


def write_bias(info, side, small, bias_ref):
    chip, core = info[0], info[1]
    win = 2 if small else WIN
    k_pos = (2 * chip - 4 + first_place(core, side, small)) * BLK + lax.broadcasted_iota(
        jnp.int32, (win * BLK, BLK), 0
    )
    lane = lax.broadcasted_iota(jnp.int32, (1, BLK), 1)
    q_pos = (2 * chip + side_parity(core, side)) * BLK + lane
    begin = jnp.zeros_like(q_pos)
    end = jnp.int32(0)
    for sample in range(8):
        end = end + info[2 + sample]
        begin = jnp.where(end <= q_pos, end, begin)
    allowed = (k_pos >= begin) & (k_pos <= q_pos)
    bias_ref[side, : win * BLK] = jnp.where(allowed, 0.0, MASKED)


def masked(raw, bias):
    return raw * EXP2_SCALE + jnp.concatenate([bias, bias], axis=1)


def head_pair(own, oth, which, step):
    group, side, pair = place_of(step)
    start = group * WIDTH + pair * COLS
    two = (own if side == 0 else oth)[which, :, start : start + COLS]
    return jnp.concatenate([two[:, :HD], two[:, HD:]], axis=0)


STEPS = 4 * PAIRS


def place_of(step):
    group, rest = divmod(step, 2 * PAIRS)
    return group, 1 - rest // PAIRS, rest % PAIRS


def load_own(core, q_hbm, do_hbm, own, sems):
    cols = lanes(core * HALF, HALF)
    copies = [
        pltpu.make_async_copy(ref.at[:, cols], own.at[i], sems.at[i])
        for i, ref in enumerate((q_hbm, do_hbm))
    ]
    for copy in copies:
        copy.start()
    return copies


def window_rows(core, side, small):
    return lanes(first_place(core, side, small) * BLK, (2 if small else WIN) * BLK)


def window(buf, group, core, side, small):
    win = 2 if small else WIN
    return buf[group, pl.ds(first_place(core, side, small), win)].reshape(win * BLK, HD)


def store_parts(core, acc, parts, scale):
    for group in range(2):
        for j, part in enumerate(parts):
            for side in range(2):
                rows = lanes((2 * j + side_parity(core, side)) * BLK, BLK)
                cut = acc[group, rows, :]
                cut = cut if scale is None else cut * scale
                part[side, :, group * HD : (group + 1) * HD] = cut.astype(part.dtype)


def probs_body(small, core, own, others, loads, k_buf, stat_ref, bias_ref, dv_acc):
    win = 2 if small else WIN

    def raw_scores(step):
        if step == PAIRS:
            for load in loads:
                load.wait()
        group, side, _ = place_of(step)
        return dot(window(k_buf, group, core, side, small), head_pair(own, others, 0, step), NT)

    following = raw_scores(0)
    for step in range(STEPS):
        group, side, _ = place_of(step)
        raw = following
        if step + 1 < STEPS:
            following = raw_scores(step + 1)
        scores = masked(raw, bias_ref[side, : win * BLK])
        peak = jnp.max(scores, axis=0, keepdims=True)
        exponent = jnp.exp2(scores - peak)
        over = 1.0 / jnp.sum(exponent, axis=0, keepdims=True)
        stat_ref[0, step : step + 1] = peak
        stat_ref[1, step : step + 1] = over
        probs = (exponent * over).astype(BF16)
        dv_acc[group, window_rows(core, side, small), :] += dot(
            probs, head_pair(own, others, 1, step), NN
        )


def probs_kernel(
    info, q_hbm, do_hbm, others, kv_two, kv_one, kv_here,
    dv_two, dv_one, dv_here, stat_ref, bias_ref,
    k_buf, dv_acc, own, sems,
):
    chip, core = info[0], info[1]
    loads = load_own(core, q_hbm, do_hbm, own, sems)
    for group in range(2):
        gather_keys(core, (kv_two, kv_one, kv_here), 0, group, k_buf)
    dv_acc[...] = jnp.zeros_like(dv_acc)
    for small in (True, False):
        @pl.when((chip == 0) == small)
        def _():
            for side in range(2):
                write_bias(info, side, small, bias_ref)
            probs_body(small, core, own, others, loads, k_buf, stat_ref, bias_ref, dv_acc)
    store_parts(core, dv_acc, (dv_two, dv_one, dv_here), None)


def scores_body(
    small, core, own, others, loads, k_buf, v_buf, k_t, stat_ref, bias_ref, dk_acc, dq_buf
):
    win = 2 if small else WIN

    def products(step):
        if step == PAIRS:
            for load in loads:
                load.wait()
        group, side, _ = place_of(step)
        raw = dot(window(k_buf, group, core, side, small), head_pair(own, others, 0, step), NT)
        grad = dot(window(v_buf, group, core, side, small), head_pair(own, others, 1, step), NT)
        return raw, grad

    following = products(0)
    for step in range(STEPS):
        group, side, pair = place_of(step)
        raw, dprobs = following
        if step + 1 < STEPS:
            following = products(step + 1)
        rows = window_rows(core, side, small)
        peak, over = stat_ref[0, step : step + 1], stat_ref[1, step : step + 1]
        scores = masked(raw, bias_ref[side, : win * BLK])
        probs = jnp.exp2(scores - peak) * over
        delta = jnp.sum(probs * dprobs, axis=0, keepdims=True)
        dscores = (probs * (dprobs - delta)).astype(BF16)
        dk_acc[group, rows, :] += dot(dscores, head_pair(own, others, 0, step), NN)
        dq_t = dot(k_t[group, :, rows], dscores, NN) * SCALE
        for i in range(2):
            start = group * WIDTH + (2 * pair + i) * HD
            dq = dq_t[:, i * BLK : (i + 1) * BLK].T.astype(BF16)
            dq_buf[side, :, start : start + HD] = dq


def scores_kernel(
    info, q_hbm, do_hbm, others, kv_two, kv_one, kv_here, stat_ref, bias_ref,
    dq_hbm, sent_hbm, dk_two, dk_one, dk_here,
    k_buf, v_buf, k_t, dk_acc, own, sems, dq_buf, out_sems,
):
    chip, core = info[0], info[1]
    loads = load_own(core, q_hbm, do_hbm, own, sems)
    targets = (dq_hbm.at[:, lanes(core * HALF, HALF)], sent_hbm)
    stores = [
        pltpu.make_async_copy(dq_buf.at[side], target, out_sems.at[side])
        for side, target in enumerate(targets)
    ]
    for group in range(2):
        gather_keys(core, (kv_two, kv_one, kv_here), 0, group, k_buf)
        gather_keys(core, (kv_two, kv_one, kv_here), 1, group, v_buf)
        k_t[group] = k_buf[group].reshape(SPAN * BLK, HD).T
    dk_acc[...] = jnp.zeros_like(dk_acc)
    for small in (True, False):
        @pl.when((chip == 0) == small)
        def _():
            scores_body(
                small, core, own, others, loads, k_buf, v_buf, k_t, stat_ref, bias_ref, dk_acc,
                dq_buf,
            )
    for store in stores:
        store.start()
    store_parts(core, dk_acc, (dk_two, dk_one, dk_here), SCALE)
    for store in stores:
        store.wait()


PARTS = [pltpu.VMEM((2, BLK, COLS), kind) for kind in (BF16, BF16, F32)]
KEYS = pltpu.VMEM((2, SPAN, BLK, HD), BF16)
TURNED = pltpu.VMEM((2, HD, SPAN * BLK), BF16)
TOTAL = pltpu.VMEM((2, SPAN * BLK, HD), F32)
OWN = [pltpu.VMEM((2, BLK, HALF), BF16), pltpu.SemaphoreType.DMA((2,))]
PRODUCT = 2 * 16 * 2 * BLK * WIN * BLK * HD
OPERANDS = [IN_SMEM, IN_HBM, IN_HBM] + [IN_VMEM] * 4


def attention_probs(operands):
    stats = pltpu.VMEM((2, STEPS, 2 * BLK), F32)
    bias = pltpu.VMEM((2, WIN * BLK, BLK), F32)
    return call(
        probs_kernel, OPERANDS, PARTS + [stats, bias], operands,
        [KEYS, TOTAL] + OWN, flops=2 * PRODUCT, exps=PRODUCT // 256, moved=4 << 20, room=16,
    )


def attention_scores(operands, stats, bias):
    return call(
        scores_kernel, OPERANDS[:3] + [ANYWHERE] * 4 + [IN_VMEM] * 2,
        [jax.ShapeDtypeStruct((BLK, width), BF16) for width in (2 * HALF, HALF)] + PARTS,
        [*operands, stats, bias],
        [KEYS, KEYS, TURNED, TOTAL] + OWN
        + [pltpu.VMEM((2, BLK, HALF), BF16), pltpu.SemaphoreType.DMA((2,))],
        flops=4 * PRODUCT, exps=PRODUCT // 256, moved=4 << 20, room=16,
    )


def weight_kernel(info, x_own, x_oth, *refs):
    dv, out_ref = refs[:-1], refs[-1]
    z = info[2 + 8]
    sources = [lax.rem(z + 4 - back, 4) for back in range(4)]
    dv_rows = jnp.concatenate([dv[back][side] for back in range(4) for side in range(2)], axis=0)
    for y in range(4):
        x_rows = jnp.concatenate(
            [x[source, y] for source in sources for x in (x_own, x_oth)], axis=0
        )
        out_ref[y * FEAT : (y + 1) * FEAT] = dot(x_rows, dv_rows, TN).astype(BF16)


def weight_part(info, x_own, x_oth, dv):
    return call(
        weight_kernel, [IN_SMEM] + [IN_VMEM] * 6,
        [pltpu.VMEM((4 * FEAT, COLS), BF16)], [info, x_own, x_oth, *dv],
        flops=2 * 4 * FEAT * COLS * 8 * BLK, moved=6 << 20, room=16,
    )[0]


def weight_sum_kernel(got, out_ref):
    for side in range(2):
        total = got[side].astype(F32)
        for source in range(1, 16):
            total = total + got[2 * source + side].astype(F32)
        out_ref[:, side * COLS : (side + 1) * COLS] = total * (1.0 / math.sqrt(16 * LEN))


def weight_sum(got):
    return pl.pallas_call(
        weight_sum_kernel,
        in_specs=[IN_VMEM],
        out_specs=IN_VMEM,
        out_shape=jax.ShapeDtypeStruct((64, HK * HD), F32),
        compiler_params=pltpu.CompilerParams(vmem_limit_bytes=4 << 20),
        name="weight_sum",
    )(near(got))


def sum_kernel(here, one, two, out_ref):
    out_ref[...] = (here[...] + one[...].astype(F32) + two[...].astype(F32)).astype(BF16)


def part_sum(parts):
    return call(sum_kernel, [IN_VMEM] * 3, [pltpu.VMEM((2, BLK, COLS), BF16)], parts)[0]


def finish_kernel(info, dq_kept, dq_got, dk, dv, got, query_grad, key_grad, value_grad, sems):
    core = info[1]
    other = lanes((1 - core) * HALF, HALF)
    keep_kv, other_kv = lanes(core * COLS, COLS), lanes((1 - core) * COLS, COLS)
    moves = [
        (dq_got, query_grad.at[:, other]),
        (dk.at[0], key_grad.at[:, keep_kv]),
        (got.at[0], key_grad.at[:, other_kv]),
        (dv.at[0], value_grad.at[:, keep_kv]),
        (got.at[1], value_grad.at[:, other_kv]),
    ]
    run_copies(
        [pltpu.make_async_copy(a, b, sems.at[i]) for i, (a, b) in enumerate(moves)]
    )


def finish(info, dq_kept, dq_got, dk, dv, got):
    outs = [jax.ShapeDtypeStruct((BLK, width * HD), BF16) for width in (HQ, HK, HK)]
    return call(
        finish_kernel, [IN_SMEM, IN_HBM] + [ANYWHERE] * 4, outs,
        [info, dq_kept, dq_got, dk, dv, got], [pltpu.SemaphoreType.DMA((5,))], moved=2 << 20,
        aliases={1: 0},
    )


def exchange(value, axes):
    return lax.all_to_all(value, axes, 0, 0, tiled=True)


def shards(queries, key_states, value_states, out_grad, layer_input, lengths):
    chip, core, depth = lax.axis_index("x"), lax.axis_index("core"), lax.axis_index("z")
    queries, out_grad = queries[0], out_grad[0]
    info = jnp.concatenate(
        [jnp.stack([chip, core]).astype(jnp.int32), lengths[0], depth.reshape(1).astype(jnp.int32)]
    )

    def pairs(a, b, which, width):
        cut = [lax.dynamic_slice(v, (0, which * width), (BLK, width)) for v in (a, b)]
        return jnp.stack(cut)

    kv_keep = pairs(key_states[0], value_states[0], core, COLS)
    kv_send = pairs(key_states[0], value_states[0], 1 - core, COLS)
    kv_here = jnp.stack([kv_keep, lax.ppermute(kv_send, "core", SWAP)])
    kv_two = lax.ppermute(kv_here, "x", [(0, 2), (1, 3)])
    kv_one = lax.ppermute(kv_here, "x", [(0, 1), (1, 2), (2, 3)])

    others = lax.ppermute(other_heads(info, queries, out_grad), "core", SWAP)

    x_own = exchange(pack(layer_input[0]), "z")
    x_oth = lax.ppermute(x_own, "core", SWAP)

    operands = (info, queries, out_grad, others, kv_two, kv_one, kv_here)
    dv_two, dv_one, dv_here, stats, bias = attention_probs(operands)
    dq_kept, dq_sent, dk_two, dk_one, dk_here = attention_scores(operands, stats, bias)

    def summed(here, one, two):
        one = lax.ppermute(one, "x", [(1, 0), (2, 1), (3, 2)])
        two = lax.ppermute(two, "x", [(2, 0), (3, 1)])
        return part_sum([here, one, two])

    dv = summed(dv_here, dv_one, dv_two)
    dv_z = [dv] + [
        lax.ppermute(dv, "z", [(i, (i + away) % 4) for i in range(4)]) for away in (1, 2, 3)
    ]
    weight = weight_part(info, x_own, x_oth, dv_z)
    weight = weight_sum(exchange(weight.reshape(32, 64, COLS), ("y", "x", "core")))

    dk = summed(dk_here, dk_one, dk_two)
    dq_got = lax.ppermute(dq_sent, "core", SWAP)
    got = lax.ppermute(jnp.stack([dk[1], dv[1]]), "core", SWAP)
    query_grad, key_grad, value_grad = finish(info, dq_kept, dq_got, dk, dv, got)
    return query_grad[None], key_grad[None], value_grad[None], weight


def solution(mesh):
    whole = Mesh(mesh.devices.reshape(4, 4, 4, 2), ("y", "z", "x", "core"))
    rows = P(("y", "z"), ("x", "core"), None)
    return jax.shard_map(
        shards,
        mesh=whole,
        in_specs=(rows,) * 5 + (P(("y", "z"), None),),
        out_specs=(rows,) * 3 + (P(("y", "z", "x", "core"), None),),
        check_vma=False,
    )
```

time: 124 us -> 117 us (0.944)
  local copies, waits for them, and re-layouts: 8.93 us -> 0.89 us
  Pallas kernels: 17.4 us -> 19.6 us
    unnamed x38 -> x18, local copies, waits for them, and re-layouts: 8.9 us -> 0.86 us
    pallas_call x9 -> x8, Pallas kernels: 16.6 us -> 18.8 us  [call(): pl.pallas_call(kernel, in_specs=list(in_specs), out_specs=out_specs, out_...]
where the time goes in v3:
time: 117 us; the launch traced here: 115 us
  waiting for transfers between devices  38.4 us (33%)
  blocking collectives  31.5 us (27%)
  starting transfers between devices  24.1 us (21%)
  Pallas kernels  19.6 us (17%)
    all_to_all x1, blocking collectives, exchange(): return lax.all_to_all(value, axes, 0, 0, tiled=True)  31.5 us
    pallas_call x8, Pallas kernels, call(): pl.pallas_call(kernel, in_specs=list(in_specs), out_specs=out_specs, out_...  18.8 us
    ppermute x2, waiting for transfers between devices, summed(): one = lax.ppermute(one, 'x', [(1, 0), (2, 1), (3, 2)])  12.6 us
    ppermute x2, waiting for transfers between devices, summed(): two = lax.ppermute(two, 'x', [(2, 0), (3, 1)])  8.03 us
    all_to_all x1, starting transfers between devices, exchange(): return lax.all_to_all(value, axes, 0, 0, tiled=True)  7.03 us
    ppermute x3, waiting for transfers between devices, shards(): lax.ppermute(dv, 'z', [(i, (i + away) % 4) for i in range(4)])  6.41 us
    ppermute x1, waiting for transfers between devices, shards(): kv_two = lax.ppermute(kv_here, 'x', [(0, 2), (1, 3)])  4.79 us
    ppermute x1, starting transfers between devices, shards(): kv_two = lax.ppermute(kv_here, 'x', [(0, 2), (1, 3)])  4.64 us
  transfers between devices with their start and end apart: 15, of which 11 were waited for; matrix products, arithmetic and copies ran while one was open for 0% of the time, Pallas kernels for 11%

profile of v3, /device:TPU:0, one launch (start us, length us, event | category | flops | bytes accessed | tf_op | source)
XLA Modules:
  0.0 115.5 jit_solution(9000857111498514797)
XLA Ops:
  0.6 1.8 %shard_map.99 = bf16[4,4,128,512]{3,2,1,0:T(8,128)(2,1)S(1)} custom-call(bf16[128,8192]{1,0:T(8,128)(2,1)} %bitcast.14), custom_call_target="tpu_custom_call" | custom-call | bytes 2097152 | tf_op jit(solution)/shard_map/pallas_call | solution.py:60
  2.4 0.0 copy-start.8
  2.4 31.5 %all_to_all.10.x_own = bf16[4,4,128,512]{3,2,1,0:T(8,128)(2,1)S(1)} all-to-all(bf16[4,4,128,512]{3,2,1,0:T(8,128)(2,1)S(1)} %shard_map.99), channel_id=1, replica_groups=mesh['y'=4,'z'=4,'x'=4,'core'=2] {'z'}, dimensions={0} | all-to-all | bytes 4194304 | tf_op jit(solution)/shard_map/all_to_all | solution.py:411
  34.0 0.0 copy-start.6
  34.0 0.0 copy-start.7
  34.0 0.0 collective-permute-start.10
  34.0 0.0 copy-done.8
  34.0 0.1 pad_add_fusion.info
  34.0 1.8 %shard_map.93 = bf16[2,128,2048]{2,1,0:T(8,128)(2,1)S(1)} custom-call(s32[11]{0:T(128)S(1)} %pad_add_fusion.info, bf16[128,4096]{1,0:T(8,128)(2,1)} %bitcast.15, bf16[128,4096]{1,0:T(8,128)(2,1)} %bitcast.18), custom_call_target="tpu_custom_call" | custom-call | bytes 1048576 | tf_op jit(solution)/shard_map/pallas_call | solution.py:60
  35.8 0.6 collective-permute-start
  36.4 0.0 copy-done.6
  36.4 0.0 copy-done.7
  36.4 0.1 collective-permute-start.1
  36.6 3.2 %collective-permute-done.1 = bf16[2,128,256]{2,1,0:T(8,128)(2,1)S(1)} collective-permute-done((bf16[2,128,256]{2,1,0:T(8,128)(2,1)S(1)}, bf16[2,128,256]{2,1,0:T(8,128)(2,1)S(1)}, u32[]{:S(2)}, u32[]{:S(2)}) %collective-permute-start.1) | collective-permute-done | bytes 131104 | tf_op jit(solution)/shard_map/ppermute | solution.py:427
  39.8 3.4 %collective-permute-start.3 = (bf16[2,2,128,256]{3,2,1,0:T(8,128)(2,1)S(1)}, bf16[2,2,128,256]{3,2,1,0:T(8,128)(2,1)S(1)}, u32[]{:S(2)}, u32[]{:S(2)}) collective-permute-start(bf16[2,2,128,256]{3,2,1,0:T(8,128)(2,1)S(1)} %pad_maximum_fusion.kv_here), channel_id=1, source_target_pairs={{0,2},{2,4},{4,6},{1,3},{3,5},{5,7},{8,10},{10,12},{12,14},{9,11},... | collective-permute-start | bytes 786440 | tf_op jit(solution)/shard_map/ppermute | solution.py:429
  43.3 4.6 %collective-permute-start.2 = (bf16[2,2,128,256]{3,2,1,0:T(8,128)(2,1)S(1)}, bf16[2,2,128,256]{3,2,1,0:T(8,128)(2,1)S(1)}, u32[]{:S(2)}, u32[]{:S(2)}) collective-permute-start(bf16[2,2,128,256]{3,2,1,0:T(8,128)(2,1)S(1)} %pad_maximum_fusion.kv_here), channel_id=1, source_target_pairs={{0,4},{2,6},{1,5},{3,7},{8,12},{10,14},{9,13},{11,15},{16,20},{18,... | collective-permute-start | bytes 786440 | tf_op jit(solution)/shard_map/ppermute | solution.py:428
  47.9 2.0 %collective-permute-done.3.kv_one = bf16[2,2,128,256]{3,2,1,0:T(8,128)(2,1)S(1)} collective-permute-done((bf16[2,2,128,256]{3,2,1,0:T(8,128)(2,1)S(1)}, bf16[2,2,128,256]{3,2,1,0:T(8,128)(2,1)S(1)}, u32[]{:S(2)}, u32[]{:S(2)}) %collective-permute-start.3) | collective-permute-done | bytes 262176 | tf_op jit(solution)/shard_map/ppermute | solution.py:429
  49.9 0.0 copy-start
  49.9 4.8 %collective-permute-done.2.kv_two = bf16[2,2,128,256]{3,2,1,0:T(8,128)(2,1)S(1)} collective-permute-done((bf16[2,2,128,256]{3,2,1,0:T(8,128)(2,1)S(1)}, bf16[2,2,128,256]{3,2,1,0:T(8,128)(2,1)S(1)}, u32[]{:S(2)}, u32[]{:S(2)}) %collective-permute-start.2) | collective-permute-done | bytes 262176 | tf_op jit(solution)/shard_map/ppermute | solution.py:428
  54.7 0.0 copy-start.2
  54.7 0.0 collective-permute-done.others
  54.7 4.2 %shard_map.94 = (bf16[2,128,256]{2,1,0:T(8,128)(2,1)S(1)}, bf16[2,128,256]{2,1,0:T(8,128)(2,1)S(1)}, f32[2,128,256]{2,1,0:T(8,128)S(1)}, f32[2,16,256]{2,1,0:T(8,128)S(1)}, f32[2,640,128]{2,1,0:T(8,128)S(1)}) custom-call(s32[11]{0:T(128)S(1)} %pad_add_fusion.info, bf16[128,4096]{1,0:T(8,128)(2,1)} %bitcast.16, bf16[128,4096]{1,0:T(8,128)(2,1)} %bitcast.19, ...), custom_call_target="tpu_custom_call" | custom-call | flops 1342177280 | bytes 4194304 | tf_op jit(solution)/shard_map/pallas_call | solution.py:60
  59.0 0.0 copy-done
  59.0 0.0 copy-done.2
  59.0 0.0 copy-start.4
  59.0 0.8 copy-done.4
  59.8 1.3 %collective-permute-start.7 = (bf16[2,128,256]{2,1,0:T(8,128)(2,1)S(1)}, bf16[2,128,256]{2,1,0:T(8,128)(2,1)S(1)}, u32[]{:S(2)}, u32[]{:S(2)}) collective-permute-start(bf16[2,128,256]{2,1,0:T(8,128)(2,1)S(1)} %get-tuple-element.25), channel_id=1, source_target_pairs={{2,0},{4,2},{6,4},{3,1},{5,3},{7,5},{10,8},{12,10},{14,12},{11,9},... | collective-permute-start | bytes 393224 | tf_op jit(solution)/shard_map/ppermute | solution.py:441
  61.1 1.3 %collective-permute-start.8 = (bf16[2,128,256]{2,1,0:T(8,128)(2,1)S(1)}, bf16[2,128,256]{2,1,0:T(8,128)(2,1)S(1)}, u32[]{:S(2)}, u32[]{:S(2)}) collective-permute-start(bf16[2,128,256]{2,1,0:T(8,128)(2,1)S(1)} %get-tuple-element.26), channel_id=1, source_target_pairs={{4,0},{6,2},{5,1},{7,3},{12,8},{14,10},{13,9},{15,11},{20,16},{22,... | collective-permute-start | bytes 393224 | tf_op jit(solution)/shard_map/ppermute | solution.py:442
  62.4 4.3 %collective-permute-done.7.one = bf16[2,128,256]{2,1,0:T(8,128)(2,1)S(1)} collective-permute-done((bf16[2,128,256]{2,1,0:T(8,128)(2,1)S(1)}, bf16[2,128,256]{2,1,0:T(8,128)(2,1)S(1)}, u32[]{:S(2)}, u32[]{:S(2)}) %collective-permute-start.7) | collective-permute-done | bytes 131104 | tf_op jit(solution)/shard_map/ppermute | solution.py:441
  66.7 5.1 %collective-permute-done.8.two = bf16[2,128,256]{2,1,0:T(8,128)(2,1)S(1)} collective-permute-done((bf16[2,128,256]{2,1,0:T(8,128)(2,1)S(1)}, bf16[2,128,256]{2,1,0:T(8,128)(2,1)S(1)}, u32[]{:S(2)}, u32[]{:S(2)}) %collective-permute-start.8) | collective-permute-done | bytes 131104 | tf_op jit(solution)/shard_map/ppermute | solution.py:442
  71.8 1.2 %collective-permute-start.13 = (bf16[2,128,256]{2,1,0:T(8,128)(2,1)S(1)}, bf16[2,128,256]{2,1,0:T(8,128)(2,1)S(1)}, u32[]{:S(2)}, u32[]{:S(2)}) collective-permute-start(bf16[2,128,256]{2,1,0:T(8,128)(2,1)S(1)} %shard_map.97.dv.refs_0_), channel_id=1, source_target_pairs={{0,24},{8,0},{16,8},{24,16},{1,25},{9,1},{17,9},{25,17},{2,26},{10... | collective-permute-start | bytes 393224 | tf_op jit(solution)/shard_map/ppermute | solution.py:447
  73.0 1.5 %collective-permute-start.12 = (bf16[2,128,256]{2,1,0:T(8,128)(2,1)S(1)}, bf16[2,128,256]{2,1,0:T(8,128)(2,1)S(1)}, u32[]{:S(2)}, u32[]{:S(2)}) collective-permute-start(bf16[2,128,256]{2,1,0:T(8,128)(2,1)S(1)} %shard_map.97.dv.refs_0_), channel_id=1, source_target_pairs={{0,16},{8,24},{16,0},{24,8},{1,17},{9,25},{17,1},{25,9},{2,18},{10... | collective-permute-start | bytes 393224 | tf_op jit(solution)/shard_map/ppermute | solution.py:447
  74.5 0.0 collective-permute-start.11
  74.5 2.6 %collective-permute-done.13.refs_3_ = bf16[2,128,256]{2,1,0:T(8,128)(2,1)S(1)} collective-permute-done((bf16[2,128,256]{2,1,0:T(8,128)(2,1)S(1)}, bf16[2,128,256]{2,1,0:T(8,128)(2,1)S(1)}, u32[]{:S(2)}, u32[]{:S(2)}) %collective-permute-start.13) | collective-permute-done | bytes 131104 | tf_op jit(solution)/shard_map/ppermute | solution.py:447
  77.0 2.5 %collective-permute-done.12.refs_2_ = bf16[2,128,256]{2,1,0:T(8,128)(2,1)S(1)} collective-permute-done((bf16[2,128,256]{2,1,0:T(8,128)(2,1)S(1)}, bf16[2,128,256]{2,1,0:T(8,128)(2,1)S(1)}, u32[]{:S(2)}, u32[]{:S(2)}) %collective-permute-start.12) | collective-permute-done | bytes 131104 | tf_op jit(solution)/shard_map/ppermute | solution.py:447
  79.5 1.4 %collective-permute-done.11.refs_1_ = bf16[2,128,256]{2,1,0:T(8,128)(2,1)S(1)} collective-permute-done((bf16[2,128,256]{2,1,0:T(8,128)(2,1)S(1)}, bf16[2,128,256]{2,1,0:T(8,128)(2,1)S(1)}, u32[]{:S(2)}, u32[]{:S(2)}) %collective-permute-start.11) | collective-permute-done | bytes 131104 | tf_op jit(solution)/shard_map/ppermute | solution.py:447
  80.9 0.0 collective-permute-done.10.x_oth
  80.9 3.9 %shard_map.100 = bf16[2048,256]{1,0:T(8,128)(2,1)} custom-call(s32[11]{0:T(128)S(1)} %pad_add_fusion.info, bf16[4,4,128,512]{3,2,1,0:T(8,128)(2,1)S(1)} %all_to_all.10.x_own, bf16[4,4,128,512]{3,2,1,0:T(8,128)(2,1)} %collective-permute-done.10.x_oth, bf16[2,128,256]{2,1,0:T(8,128)(2,1)S(1)} %shard_map.97.dv.refs_0_, ...), custom_call_target="tpu_custom_call" | custom-call | flops 1073741824 | bytes 6291456 | tf_op jit(solution)/shard_map/pallas_call | solution.py:60
  84.8 0.0 copy-start.1
  84.8 0.0 copy-start.3
  84.8 0.0 copy-start.5
  84.8 7.0 %all-to-all-start.1 = ((bf16[32,64,256]{2,1,0:T(8,128)(2,1)}), bf16[32,64,256]{2,1,0:T(8,128)(2,1)S(1)}, u32[]{:S(2)}, u32[]{:S(2)}) async-start(bf16[32,64,256]{2,1,0:T(8,128)(2,1)} %bitcast.12), calls=%async_computation.1 | async-start | bytes 2097152 | tf_op jit(solution)/shard_map/all_to_all | solution.py:411
  91.8 0.0 copy-done.1
  91.8 0.0 copy-done.3
  91.8 0.0 copy-done.5
  91.9 5.6 %shard_map.95 = (bf16[128,4096]{1,0:T(8,128)(2,1)}, bf16[128,2048]{1,0:T(8,128)(2,1)S(1)}, bf16[2,128,256]{2,1,0:T(8,128)(2,1)S(1)}, bf16[2,128,256]{2,1,0:T(8,128)(2,1)S(1)}, f32[2,128,256]{2,1,0:T(8,128)S(1)}) custom-call(s32[11]{0:T(128)S(1)} %pad_add_fusion.info, bf16[128,4096]{1,0:T(8,128)(2,1)} %bitcast.17, bf16[128,4096]{1,0:T(8,128)(2,1)} %bitcast.20, ...), custom_call_target="tpu_custom_call" | custom-call | flops 2684354560 | bytes 4194304 | tf_op jit(solution)/shard_map/pallas_call | solution.py:60
  97.5 0.4 collective-permute-start.4
  97.8 1.3 %collective-permute-start.5 = (bf16[2,128,256]{2,1,0:T(8,128)(2,1)S(1)}, bf16[2,128,256]{2,1,0:T(8,128)(2,1)S(1)}, u32[]{:S(2)}, u32[]{:S(2)}) collective-permute-start(bf16[2,128,256]{2,1,0:T(8,128)(2,1)S(1)} %get-tuple-element.22), channel_id=1, source_target_pairs={{2,0},{4,2},{6,4},{3,1},{5,3},{7,5},{10,8},{12,10},{14,12},{11,9},... | collective-permute-start | bytes 393224 | tf_op jit(solution)/shard_map/ppermute | solution.py:441
  99.1 1.3 %collective-permute-start.6 = (bf16[2,128,256]{2,1,0:T(8,128)(2,1)S(1)}, bf16[2,128,256]{2,1,0:T(8,128)(2,1)S(1)}, u32[]{:S(2)}, u32[]{:S(2)}) collective-permute-start(bf16[2,128,256]{2,1,0:T(8,128)(2,1)S(1)} %get-tuple-element.23), channel_id=1, source_target_pairs={{4,0},{6,2},{5,1},{7,3},{12,8},{14,10},{13,9},{15,11},{20,16},{22,... | collective-permute-start | bytes 393224 | tf_op jit(solution)/shard_map/ppermute | solution.py:442
  100.4 8.3 %collective-permute-done.5.one = bf16[2,128,256]{2,1,0:T(8,128)(2,1)S(1)} collective-permute-done((bf16[2,128,256]{2,1,0:T(8,128)(2,1)S(1)}, bf16[2,128,256]{2,1,0:T(8,128)(2,1)S(1)}, u32[]{:S(2)}, u32[]{:S(2)}) %collective-permute-start.5) | collective-permute-done | bytes 131104 | tf_op jit(solution)/shard_map/ppermute | solution.py:441
  108.7 3.0 %collective-permute-done.6.two = bf16[2,128,256]{2,1,0:T(8,128)(2,1)S(1)} collective-permute-done((bf16[2,128,256]{2,1,0:T(8,128)(2,1)S(1)}, bf16[2,128,256]{2,1,0:T(8,128)(2,1)S(1)}, u32[]{:S(2)}, u32[]{:S(2)}) %collective-permute-start.6) | collective-permute-done | bytes 131104 | tf_op jit(solution)/shard_map/ppermute | solution.py:442
  111.8 0.1 collective-permute-start.9
  111.9 1.3 %collective-permute-done.9.got = bf16[2,128,256]{2,1,0:T(8,128)(2,1)S(1)} collective-permute-done((bf16[2,128,256]{2,1,0:T(8,128)(2,1)S(1)}, bf16[2,128,256]{2,1,0:T(8,128)(2,1)S(1)}, u32[]{:S(2)}, u32[]{:S(2)}) %collective-permute-start.9) | collective-permute-done | bytes 131104 | tf_op jit(solution)/shard_map/ppermute | solution.py:454
  113.2 0.0 collective-permute-done.4.dq_got
  113.2 1.5 %shard_map.98 = (bf16[128,4096]{1,0:T(8,128)(2,1)}, bf16[128,512]{1,0:T(8,128)(2,1)}, bf16[128,512]{1,0:T(8,128)(2,1)}) custom-call(s32[11]{0:T(128)S(1)} %pad_add_fusion.info, bf16[128,4096]{1,0:T(8,128)(2,1)} %get-tuple-element.19.dq_kept, bf16[128,2048]{1,0:T(8,128)(2,1)S(1)} %collective-permute-done.4.dq_got, ...), custom_call_target="tpu_custom_call", output_to_operand_aliasing={{0}: (1, {})} | custom-call | bytes 2097152 | tf_op jit(solution)/shard_map/pallas_call | solution.py:60
  114.7 0.0 all-to-all-done.1.got
  114.7 0.8 weight_sum.1
  (9 shorter events, 0.2 us)
Async XLA Ops:
  2.4 31.6 %copy-start.8 = (s32[1,8]{1,0:T(1,128)S(1)}, s32[1,8]{1,0:T(1,128)}, u32[]{:S(2)}) copy-start(s32[1,8]{1,0:T(1,128)} %param.11) | copy-start | bytes 100
  34.0 2.4 %copy-start.6 = (bf16[1,128,512]{2,1,0:T(8,128)(2,1)S(1)}, bf16[1,128,512]{2,1,0:T(8,128)(2,1)}, u32[]{:S(2)}) copy-start(bf16[1,128,512]{2,1,0:T(8,128)(2,1)} %param.8) | copy-start | bytes 393220
  34.0 2.4 %copy-start.7 = (bf16[1,128,512]{2,1,0:T(8,128)(2,1)S(1)}, bf16[1,128,512]{2,1,0:T(8,128)(2,1)}, u32[]{:S(2)}) copy-start(bf16[1,128,512]{2,1,0:T(8,128)(2,1)} %param.7) | copy-start | bytes 393220
  34.0 46.9 %collective-permute-start.10 = (bf16[4,4,128,512]{3,2,1,0:T(8,128)(2,1)S(1)}, bf16[4,4,128,512]{3,2,1,0:T(8,128)(2,1)}, u32[]{:S(2)}, u32[]{:S(2)}) collective-permute-start(bf16[4,4,128,512]{3,2,1,0:T(8,128)(2,1)S(1)} %all_to_all.10.x_own), channel_id=1, source_target_pairs={{0,1},{1,0},{2,3},{3,2},{4,5},{5,4},{6,7},{7,6},{8,9},{9,8},{10,11... | collective-permute-start | bytes 6291464 | tf_op jit(solution)/shard_map/ppermute | solution.py:434
  35.8 18.9 %collective-permute-start = (bf16[2,128,2048]{2,1,0:T(8,128)(2,1)S(1)}, bf16[2,128,2048]{2,1,0:T(8,128)(2,1)}, u32[]{:S(2)}, u32[]{:S(2)}) collective-permute-start(bf16[2,128,2048]{2,1,0:T(8,128)(2,1)S(1)} %shard_map.93), channel_id=1, source_target_pairs={{0,1},{1,0},{2,3},{3,2},{4,5},{5,4},{6,7},{7,6},{8,9},{9,8},{10,11... | collective-permute-start | bytes 3145736 | tf_op jit(solution)/shard_map/ppermute | solution.py:431
  36.4 3.4 %collective-permute-start.1 = (bf16[2,128,256]{2,1,0:T(8,128)(2,1)S(1)}, bf16[2,128,256]{2,1,0:T(8,128)(2,1)S(1)}, u32[]{:S(2)}, u32[]{:S(2)}) collective-permute-start(bf16[2,128,256]{2,1,0:T(8,128)(2,1)S(1)} %pad_maximum_fusion.1), channel_id=1, source_target_pairs={{0,1},{1,0},{2,3},{3,2},{4,5},{5,4},{6,7},{7,6},{8,9},{9,8},{10,11... | collective-permute-start | bytes 393224 | tf_op jit(solution)/shard_map/ppermute | solution.py:427
  39.8 10.1 %collective-permute-start.3 = (bf16[2,2,128,256]{3,2,1,0:T(8,128)(2,1)S(1)}, bf16[2,2,128,256]{3,2,1,0:T(8,128)(2,1)S(1)}, u32[]{:S(2)}, u32[]{:S(2)}) collective-permute-start(bf16[2,2,128,256]{3,2,1,0:T(8,128)(2,1)S(1)} %pad_maximum_fusion.kv_here), channel_id=1, source_target_pairs={{0,2},{2,4},{4,6},{1,3},{3,5},{5,7},{8,10},{10,12},{12,14},{9,11},... | collective-permute-start | bytes 786440 | tf_op jit(solution)/shard_map/ppermute | solution.py:429
  43.3 11.4 %collective-permute-start.2 = (bf16[2,2,128,256]{3,2,1,0:T(8,128)(2,1)S(1)}, bf16[2,2,128,256]{3,2,1,0:T(8,128)(2,1)S(1)}, u32[]{:S(2)}, u32[]{:S(2)}) collective-permute-start(bf16[2,2,128,256]{3,2,1,0:T(8,128)(2,1)S(1)} %pad_maximum_fusion.kv_here), channel_id=1, source_target_pairs={{0,4},{2,6},{1,5},{3,7},{8,12},{10,14},{9,13},{11,15},{16,20},{18,... | collective-permute-start | bytes 786440 | tf_op jit(solution)/shard_map/ppermute | solution.py:428
  49.9 9.0 %copy-start = (bf16[2,2,128,256]{3,2,1,0:T(8,128)(2,1)}, bf16[2,2,128,256]{3,2,1,0:T(8,128)(2,1)S(1)}, u32[]{:S(2)}) copy-start(bf16[2,2,128,256]{3,2,1,0:T(8,128)(2,1)S(1)} %collective-permute-done.3.kv_one) | copy-start | bytes 786436
  54.7 4.3 %copy-start.2 = (bf16[2,2,128,256]{3,2,1,0:T(8,128)(2,1)}, bf16[2,2,128,256]{3,2,1,0:T(8,128)(2,1)S(1)}, u32[]{:S(2)}) copy-start(bf16[2,2,128,256]{3,2,1,0:T(8,128)(2,1)S(1)} %collective-permute-done.2.kv_two) | copy-start | bytes 786436
  59.0 0.8 copy-start.4
  59.8 6.8 %collective-permute-start.7 = (bf16[2,128,256]{2,1,0:T(8,128)(2,1)S(1)}, bf16[2,128,256]{2,1,0:T(8,128)(2,1)S(1)}, u32[]{:S(2)}, u32[]{:S(2)}) collective-permute-start(bf16[2,128,256]{2,1,0:T(8,128)(2,1)S(1)} %get-tuple-element.25), channel_id=1, source_target_pairs={{2,0},{4,2},{6,4},{3,1},{5,3},{7,5},{10,8},{12,10},{14,12},{11,9},... | collective-permute-start | bytes 393224 | tf_op jit(solution)/shard_map/ppermute | solution.py:441
  61.1 10.6 %collective-permute-start.8 = (bf16[2,128,256]{2,1,0:T(8,128)(2,1)S(1)}, bf16[2,128,256]{2,1,0:T(8,128)(2,1)S(1)}, u32[]{:S(2)}, u32[]{:S(2)}) collective-permute-start(bf16[2,128,256]{2,1,0:T(8,128)(2,1)S(1)} %get-tuple-element.26), channel_id=1, source_target_pairs={{4,0},{6,2},{5,1},{7,3},{12,8},{14,10},{13,9},{15,11},{20,16},{22,... | collective-permute-start | bytes 393224 | tf_op jit(solution)/shard_map/ppermute | solution.py:442
  71.8 5.3 %collective-permute-start.13 = (bf16[2,128,256]{2,1,0:T(8,128)(2,1)S(1)}, bf16[2,128,256]{2,1,0:T(8,128)(2,1)S(1)}, u32[]{:S(2)}, u32[]{:S(2)}) collective-permute-start(bf16[2,128,256]{2,1,0:T(8,128)(2,1)S(1)} %shard_map.97.dv.refs_0_), channel_id=1, source_target_pairs={{0,24},{8,0},{16,8},{24,16},{1,25},{9,1},{17,9},{25,17},{2,26},{10... | collective-permute-start | bytes 393224 | tf_op jit(solution)/shard_map/ppermute | solution.py:447
  73.0 6.5 %collective-permute-start.12 = (bf16[2,128,256]{2,1,0:T(8,128)(2,1)S(1)}, bf16[2,128,256]{2,1,0:T(8,128)(2,1)S(1)}, u32[]{:S(2)}, u32[]{:S(2)}) collective-permute-start(bf16[2,128,256]{2,1,0:T(8,128)(2,1)S(1)} %shard_map.97.dv.refs_0_), channel_id=1, source_target_pairs={{0,16},{8,24},{16,0},{24,8},{1,17},{9,25},{17,1},{25,9},{2,18},{10... | collective-permute-start | bytes 393224 | tf_op jit(solution)/shard_map/ppermute | solution.py:447
  74.5 6.4 %collective-permute-start.11 = (bf16[2,128,256]{2,1,0:T(8,128)(2,1)S(1)}, bf16[2,128,256]{2,1,0:T(8,128)(2,1)S(1)}, u32[]{:S(2)}, u32[]{:S(2)}) collective-permute-start(bf16[2,128,256]{2,1,0:T(8,128)(2,1)S(1)} %shard_map.97.dv.refs_0_), channel_id=1, source_target_pairs={{0,8},{8,16},{16,24},{24,0},{1,9},{9,17},{17,25},{25,1},{2,10},{10... | collective-permute-start | bytes 393224 | tf_op jit(solution)/shard_map/ppermute | solution.py:447
  84.8 7.0 %copy-start.1 = (bf16[2,2,128,256]{3,2,1,0:T(8,128)(2,1)S(1)}, bf16[2,2,128,256]{3,2,1,0:T(8,128)(2,1)}, u32[]{:S(2)}) copy-start(bf16[2,2,128,256]{3,2,1,0:T(8,128)(2,1)} %copy-done) | copy-start | bytes 786436
  84.8 7.1 %copy-start.3 = (bf16[2,2,128,256]{3,2,1,0:T(8,128)(2,1)S(1)}, bf16[2,2,128,256]{3,2,1,0:T(8,128)(2,1)}, u32[]{:S(2)}) copy-start(bf16[2,2,128,256]{3,2,1,0:T(8,128)(2,1)} %copy-done.2) | copy-start | bytes 786436
  84.8 7.1 %copy-start.5 = (f32[2,640,128]{2,1,0:T(8,128)S(1)}, f32[2,640,128]{2,1,0:T(8,128)}, u32[]{:S(2)}) copy-start(f32[2,640,128]{2,1,0:T(8,128)} %copy-done.4) | copy-start | bytes 1966084
  84.8 29.9 %all-to-all-start.1 = ((bf16[32,64,256]{2,1,0:T(8,128)(2,1)}), bf16[32,64,256]{2,1,0:T(8,128)(2,1)S(1)}, u32[]{:S(2)}, u32[]{:S(2)}) async-start(bf16[32,64,256]{2,1,0:T(8,128)(2,1)} %bitcast.12), calls=%async_computation.1 | async-start | bytes 2097152 | tf_op jit(solution)/shard_map/all_to_all | solution.py:411
  97.5 15.7 %collective-permute-start.4 = (bf16[128,2048]{1,0:T(8,128)(2,1)S(1)}, bf16[128,2048]{1,0:T(8,128)(2,1)S(1)}, u32[]{:S(2)}, u32[]{:S(2)}) collective-permute-start(bf16[128,2048]{1,0:T(8,128)(2,1)S(1)} %get-tuple-element.20), channel_id=1, source_target_pairs={{0,1},{1,0},{2,3},{3,2},{4,5},{5,4},{6,7},{7,6},{8,9},{9,8},{10,11... | collective-permute-start | bytes 1572872 | tf_op jit(solution)/shard_map/ppermute | solution.py:453
  97.8 10.9 %collective-permute-start.5 = (bf16[2,128,256]{2,1,0:T(8,128)(2,1)S(1)}, bf16[2,128,256]{2,1,0:T(8,128)(2,1)S(1)}, u32[]{:S(2)}, u32[]{:S(2)}) collective-permute-start(bf16[2,128,256]{2,1,0:T(8,128)(2,1)S(1)} %get-tuple-element.22), channel_id=1, source_target_pairs={{2,0},{4,2},{6,4},{3,1},{5,3},{7,5},{10,8},{12,10},{14,12},{11,9},... | collective-permute-start | bytes 393224 | tf_op jit(solution)/shard_map/ppermute | solution.py:441
  99.1 12.6 %collective-permute-start.6 = (bf16[2,128,256]{2,1,0:T(8,128)(2,1)S(1)}, bf16[2,128,256]{2,1,0:T(8,128)(2,1)S(1)}, u32[]{:S(2)}, u32[]{:S(2)}) collective-permute-start(bf16[2,128,256]{2,1,0:T(8,128)(2,1)S(1)} %get-tuple-element.23), channel_id=1, source_target_pairs={{4,0},{6,2},{5,1},{7,3},{12,8},{14,10},{13,9},{15,11},{20,16},{22,... | collective-permute-start | bytes 393224 | tf_op jit(solution)/shard_map/ppermute | solution.py:442
  111.8 1.4 %collective-permute-start.9 = (bf16[2,128,256]{2,1,0:T(8,128)(2,1)S(1)}, bf16[2,128,256]{2,1,0:T(8,128)(2,1)S(1)}, u32[]{:S(2)}, u32[]{:S(2)}) collective-permute-start(bf16[2,128,256]{2,1,0:T(8,128)(2,1)S(1)} %pad_maximum_fusion.2), channel_id=1, source_target_pairs={{0,1},{1,0},{2,3},{3,2},{4,5},{5,4},{6,7},{7,6},{8,9},{9,8},{10,11... | collective-permute-start | bytes 393224 | tf_op jit(solution)/shard_map/ppermute | solution.py:454

commit v4 on v3

--- a/solution.py
+++ b/solution.py
@@ -54,7 +54,9 @@
 
 
 def call(kernel, in_specs, outs, operands, scratch=(), flops=0, exps=0, moved=1 << 20, room=4, aliases=None):
-    out_specs = [IN_HBM if isinstance(o, jax.ShapeDtypeStruct) else IN_VMEM for o in outs]
+    out_specs = [
+        IN_HBM if getattr(o, "memory_space", None) != pltpu.VMEM else IN_VMEM for o in outs
+    ]
     place = {id(IN_VMEM): near, id(IN_HBM): far}
     operands = [place.get(id(spec), lambda a: a)(a) for a, spec in zip(operands, in_specs)]
     return pl.pallas_call(
@@ -76,27 +78,33 @@
         copy.wait()
 
 
-def pack_kernel(x_ref, out_ref, sems):
-    run_copies(
-        [
-            pltpu.make_async_copy(
-                x_ref.at[:, pl.ds((y * 4 + z) * FEAT, FEAT)], out_ref.at[z, y], sems.at[4 * z + y]
-            )
-            for z in range(4)
-            for y in range(4)
-        ]
-    )
+def pack_kernel(x_ref, out_ref, buf, load_sems, store_sems):
+    loads, stores = [], []
+    for z in range(4):
+        for y in range(4):
+            cols = pl.ds((y * 4 + z) * FEAT, FEAT)
+            at = buf.at[z, y]
+            loads.append(pltpu.make_async_copy(x_ref.at[:, cols], at, load_sems.at[4 * z + y]))
+            stores.append(pltpu.make_async_copy(at, out_ref.at[z, y], store_sems.at[4 * z + y]))
+    for load in loads:
+        load.start()
+    for load, store in zip(loads, stores):
+        load.wait()
+        store.start()
+    for store in stores:
+        store.wait()
 
 
 def pack(layer_input):
-    return call(
-        pack_kernel, [IN_HBM], [pltpu.VMEM((4, 4, BLK, FEAT), BF16)], [layer_input],
-        [pltpu.SemaphoreType.DMA((16,))], moved=2 << 20,
+    shape = (4, 4, BLK, FEAT)
+    return call(
+        pack_kernel, [IN_HBM], [pltpu.HBM(shape, BF16)], [layer_input],
+        [pltpu.VMEM(shape, BF16)] + [pltpu.SemaphoreType.DMA((16,))] * 2, moved=4 << 20,
     )[0]
 
 
-def other_kernel(info, q_ref, do_ref, out_ref, sems):
-    cols = lanes((1 - info[1]) * HALF, HALF)
+def other_kernel(q_ref, do_ref, out_ref, sems):
+    cols = lanes((1 - lax.axis_index("core")) * HALF, HALF)
     run_copies(
         [
             pltpu.make_async_copy(ref.at[:, cols], out_ref.at[i], sems.at[i])
@@ -105,10 +113,10 @@
     )
 
 
-def other_heads(info, queries, out_grad):
-    return call(
-        other_kernel, [IN_SMEM, IN_HBM, IN_HBM],
-        [pltpu.VMEM((2, BLK, HALF), BF16)], [info, queries, out_grad],
+def other_heads(queries, out_grad):
+    return call(
+        other_kernel, [IN_HBM, IN_HBM],
+        [pltpu.VMEM((2, BLK, HALF), BF16)], [queries, out_grad],
         [pltpu.SemaphoreType.DMA((2,))], moved=1 << 20,
     )[0]
 
@@ -128,8 +136,7 @@
             buf[group, place] = kv[side, which, :, group * HD : (group + 1) * HD]
 
 
-def write_bias(info, side, small, bias_ref):
-    chip, core = info[0], info[1]
+def write_bias(lengths, chip, core, side, small, bias_ref):
     win = 2 if small else WIN
     k_pos = (2 * chip - 4 + first_place(core, side, small)) * BLK + lax.broadcasted_iota(
         jnp.int32, (win * BLK, BLK), 0
@@ -139,7 +146,7 @@
     begin = jnp.zeros_like(q_pos)
     end = jnp.int32(0)
     for sample in range(8):
-        end = end + info[2 + sample]
+        end = end + lengths[0, sample]
         begin = jnp.where(end <= q_pos, end, begin)
     allowed = (k_pos >= begin) & (k_pos <= q_pos)
     bias_ref[side, : win * BLK] = jnp.where(allowed, 0.0, MASKED)
@@ -223,11 +230,11 @@
 
 
 def probs_kernel(
-    info, q_hbm, do_hbm, others, kv_two, kv_one, kv_here,
+    lengths, q_hbm, do_hbm, others, kv_two, kv_one, kv_here,
     dv_two, dv_one, dv_here, stat_ref, bias_ref,
     k_buf, dv_acc, own, sems,
 ):
-    chip, core = info[0], info[1]
+    chip, core = lax.axis_index("x"), lax.axis_index("core")
     loads = load_own(core, q_hbm, do_hbm, own, sems)
     for group in range(2):
         gather_keys(core, (kv_two, kv_one, kv_here), 0, group, k_buf)
@@ -236,13 +243,13 @@
         @pl.when((chip == 0) == small)
         def _():
             for side in range(2):
-                write_bias(info, side, small, bias_ref)
+                write_bias(lengths, chip, core, side, small, bias_ref)
             probs_body(small, core, own, others, loads, k_buf, stat_ref, bias_ref, dv_acc)
     store_parts(core, dv_acc, (dv_two, dv_one, dv_here), None)
 
 
 def scores_body(
-    small, core, own, others, loads, k_buf, v_buf, k_t, stat_ref, bias_ref, dk_acc, dq_buf
+    small, core, own, others, loads, k_buf, v_buf, k_t, stat_ref, bias_ref, dk_acc, dq_refs
 ):
     win = 2 if small else WIN
 
@@ -272,21 +279,17 @@
         for i in range(2):
             start = group * WIDTH + (2 * pair + i) * HD
             dq = dq_t[:, i * BLK : (i + 1) * BLK].T.astype(BF16)
-            dq_buf[side, :, start : start + HD] = dq
+            dq_refs[side][:, start : start + HD] = dq
 
 
 def scores_kernel(
-    info, q_hbm, do_hbm, others, kv_two, kv_one, kv_here, stat_ref, bias_ref,
-    dq_hbm, sent_hbm, dk_two, dk_one, dk_here,
-    k_buf, v_buf, k_t, dk_acc, own, sems, dq_buf, out_sems,
+    lengths, q_hbm, do_hbm, others, kv_two, kv_one, kv_here, stat_ref, bias_ref,
+    dq_hbm, dq_sent, dk_two, dk_one, dk_here,
+    k_buf, v_buf, k_t, dk_acc, own, sems, dq_buf, out_sem,
 ):
-    chip, core = info[0], info[1]
+    chip, core = lax.axis_index("x"), lax.axis_index("core")
     loads = load_own(core, q_hbm, do_hbm, own, sems)
-    targets = (dq_hbm.at[:, lanes(core * HALF, HALF)], sent_hbm)
-    stores = [
-        pltpu.make_async_copy(dq_buf.at[side], target, out_sems.at[side])
-        for side, target in enumerate(targets)
-    ]
+    store = pltpu.make_async_copy(dq_buf, dq_hbm.at[:, lanes(core * HALF, HALF)], out_sem)
     for group in range(2):
         gather_keys(core, (kv_two, kv_one, kv_here), 0, group, k_buf)
         gather_keys(core, (kv_two, kv_one, kv_here), 1, group, v_buf)
@@ -297,13 +300,11 @@
         def _():
             scores_body(
                 small, core, own, others, loads, k_buf, v_buf, k_t, stat_ref, bias_ref, dk_acc,
-                dq_buf,
+                (dq_buf, dq_sent),
             )
-    for store in stores:
-        store.start()
+    store.start()
     store_parts(core, dk_acc, (dk_two, dk_one, dk_here), SCALE)
-    for store in stores:
-        store.wait()
+    store.wait()
 
 
 PARTS = [pltpu.VMEM((2, BLK, COLS), kind) for kind in (BF16, BF16, F32)]
@@ -327,31 +328,42 @@
 def attention_scores(operands, stats, bias):
     return call(
         scores_kernel, OPERANDS[:3] + [ANYWHERE] * 4 + [IN_VMEM] * 2,
-        [jax.ShapeDtypeStruct((BLK, width), BF16) for width in (2 * HALF, HALF)] + PARTS,
-        [*operands, stats, bias],
+        [jax.ShapeDtypeStruct((BLK, 2 * HALF), BF16), pltpu.VMEM((BLK, HALF), BF16)] + PARTS,
+        [*operands[:-1], far(operands[-1]), stats, bias],
         [KEYS, KEYS, TURNED, TOTAL] + OWN
-        + [pltpu.VMEM((2, BLK, HALF), BF16), pltpu.SemaphoreType.DMA((2,))],
+        + [pltpu.VMEM((BLK, HALF), BF16), pltpu.SemaphoreType.DMA(())],
         flops=4 * PRODUCT, exps=PRODUCT // 256, moved=4 << 20, room=16,
     )
 
 
-def weight_kernel(info, x_own, x_oth, *refs):
-    dv, out_ref = refs[:-1], refs[-1]
-    z = info[2 + 8]
+def weight_rows(z, x, dv, side, y):
     sources = [lax.rem(z + 4 - back, 4) for back in range(4)]
-    dv_rows = jnp.concatenate([dv[back][side] for back in range(4) for side in range(2)], axis=0)
+    x_rows = jnp.concatenate([x[source, y] for source in sources], axis=0)
+    return dot(x_rows, jnp.concatenate([ref[side] for ref in dv], axis=0), TN)
+
+
+def weight_own_kernel(x, *refs):
+    z = lax.axis_index("z")
     for y in range(4):
-        x_rows = jnp.concatenate(
-            [x[source, y] for source in sources for x in (x_own, x_oth)], axis=0
-        )
-        out_ref[y * FEAT : (y + 1) * FEAT] = dot(x_rows, dv_rows, TN).astype(BF16)
-
-
-def weight_part(info, x_own, x_oth, dv):
-    return call(
-        weight_kernel, [IN_SMEM] + [IN_VMEM] * 6,
-        [pltpu.VMEM((4 * FEAT, COLS), BF16)], [info, x_own, x_oth, *dv],
-        flops=2 * 4 * FEAT * COLS * 8 * BLK, moved=6 << 20, room=16,
+        refs[-1][y * FEAT : (y + 1) * FEAT] = weight_rows(z, x, refs[:-1], 0, y)
+
+
+def weight_all_kernel(x, past, *refs):
+    z = lax.axis_index("z")
+    for y in range(4):
+        rows = slice(y * FEAT, (y + 1) * FEAT)
+        refs[-1][rows] = (past[rows] + weight_rows(z, x, refs[:-1], 1, y)).astype(BF16)
+
+
+def weight_part(x_own, x_oth, dv):
+    flops = 4 * FEAT * COLS * 8 * BLK
+    past = call(
+        weight_own_kernel, [IN_VMEM] * 5, [pltpu.VMEM((4 * FEAT, COLS), F32)],
+        [x_own, *dv], flops=flops, moved=4 << 20, room=12,
+    )[0]
+    return call(
+        weight_all_kernel, [IN_VMEM] * 6, [pltpu.VMEM((4 * FEAT, COLS), BF16)],
+        [x_oth, past, *dv], flops=flops, moved=4 << 20, room=12,
     )[0]
 
 
@@ -382,8 +394,8 @@
     return call(sum_kernel, [IN_VMEM] * 3, [pltpu.VMEM((2, BLK, COLS), BF16)], parts)[0]
 
 
-def finish_kernel(info, dq_kept, dq_got, dk, dv, got, query_grad, key_grad, value_grad, sems):
-    core = info[1]
+def finish_kernel(dq_kept, dq_got, dk, dv, got, query_grad, key_grad, value_grad, sems):
+    core = lax.axis_index("core")
     other = lanes((1 - core) * HALF, HALF)
     keep_kv, other_kv = lanes(core * COLS, COLS), lanes((1 - core) * COLS, COLS)
     moves = [
@@ -398,12 +410,12 @@
     )
 
 
-def finish(info, dq_kept, dq_got, dk, dv, got):
+def finish(dq_kept, dq_got, dk, dv, got):
     outs = [jax.ShapeDtypeStruct((BLK, width * HD), BF16) for width in (HQ, HK, HK)]
     return call(
-        finish_kernel, [IN_SMEM, IN_HBM] + [ANYWHERE] * 4, outs,
-        [info, dq_kept, dq_got, dk, dv, got], [pltpu.SemaphoreType.DMA((5,))], moved=2 << 20,
-        aliases={1: 0},
+        finish_kernel, [IN_HBM] + [ANYWHERE] * 4, outs,
+        [dq_kept, dq_got, dk, dv, got], [pltpu.SemaphoreType.DMA((5,))], moved=2 << 20,
+        aliases={0: 0},
     )
 
 
@@ -412,11 +424,8 @@
 
 
 def shards(queries, key_states, value_states, out_grad, layer_input, lengths):
-    chip, core, depth = lax.axis_index("x"), lax.axis_index("core"), lax.axis_index("z")
+    core = lax.axis_index("core")
     queries, out_grad = queries[0], out_grad[0]
-    info = jnp.concatenate(
-        [jnp.stack([chip, core]).astype(jnp.int32), lengths[0], depth.reshape(1).astype(jnp.int32)]
-    )
 
     def pairs(a, b, which, width):
         cut = [lax.dynamic_slice(v, (0, which * width), (BLK, width)) for v in (a, b)]
@@ -428,12 +437,12 @@
     kv_two = lax.ppermute(kv_here, "x", [(0, 2), (1, 3)])
     kv_one = lax.ppermute(kv_here, "x", [(0, 1), (1, 2), (2, 3)])
 
-    others = lax.ppermute(other_heads(info, queries, out_grad), "core", SWAP)
+    others = lax.ppermute(other_heads(queries, out_grad), "core", SWAP)
 
     x_own = exchange(pack(layer_input[0]), "z")
     x_oth = lax.ppermute(x_own, "core", SWAP)
 
-    operands = (info, queries, out_grad, others, kv_two, kv_one, kv_here)
+    operands = (lengths, queries, out_grad, others, kv_two, kv_one, kv_here)
     dv_two, dv_one, dv_here, stats, bias = attention_probs(operands)
     dq_kept, dq_sent, dk_two, dk_one, dk_here = attention_scores(operands, stats, bias)
 
@@ -446,13 +455,13 @@
     dv_z = [dv] + [
         lax.ppermute(dv, "z", [(i, (i + away) % 4) for i in range(4)]) for away in (1, 2, 3)
     ]
-    weight = weight_part(info, x_own, x_oth, dv_z)
+    weight = weight_part(x_own, x_oth, dv_z)
     weight = weight_sum(exchange(weight.reshape(32, 64, COLS), ("y", "x", "core")))
 
     dk = summed(dk_here, dk_one, dk_two)
     dq_got = lax.ppermute(dq_sent, "core", SWAP)
     got = lax.ppermute(jnp.stack([dk[1], dv[1]]), "core", SWAP)
-    query_grad, key_grad, value_grad = finish(info, dq_kept, dq_got, dk, dv, got)
+    query_grad, key_grad, value_grad = finish(dq_kept, dq_got, dk, dv, got)
     return query_grad[None], key_grad[None], value_grad[None], weight
 
 

time: 117 us -> 120 us (1.026)
  waiting for transfers between devices: 38.4 us -> 41.1 us
    ppermute x1, waiting for transfers between devices: 2.01 us -> 4.79 us  [shards(): kv_one = lax.ppermute(kv_here, 'x', [(0, 1), (1, 2), (2, 3)])]
    ppermute x2, waiting for transfers between devices: 12.6 us -> 14.9 us  [summed(): one = lax.ppermute(one, 'x', [(1, 0), (2, 1), (3, 2)])]
    ppermute x2, waiting for transfers between devices: 8.03 us -> 6.59 us  [summed(): two = lax.ppermute(two, 'x', [(2, 0), (3, 1)])]
    pallas_call x8 -> x9, Pallas kernels: 18.8 us -> 18.9 us  [call(): pl.pallas_call(kernel, in_specs=list(in_specs), out_specs=out_specs, out_...]
  transfers between devices with their start and end apart: 15 -> 15, of which waited for: 11 -> 10; matrix products, arithmetic and copies ran while one was open for 0% -> 0% of each run, Pallas kernels for 11% -> 11%
where the time goes in v4:
time: 120 us; the launch traced here: 118 us
  waiting for transfers between devices  41.1 us (34%)
  blocking collectives  31.8 us (26%)
  starting transfers between devices  24.6 us (20%)
  Pallas kernels  19.7 us (16%)
    all_to_all x1, blocking collectives, exchange(): return lax.all_to_all(value, axes, 0, 0, tiled=True)  31.8 us
    pallas_call x9, Pallas kernels, call(): pl.pallas_call(kernel, in_specs=list(in_specs), out_specs=out_specs, out_...  18.9 us
    ppermute x2, waiting for transfers between devices, summed(): one = lax.ppermute(one, 'x', [(1, 0), (2, 1), (3, 2)])  14.9 us
    all_to_all x1, starting transfers between devices, exchange(): return lax.all_to_all(value, axes, 0, 0, tiled=True)  7.38 us
    ppermute x2, waiting for transfers between devices, summed(): two = lax.ppermute(two, 'x', [(2, 0), (3, 1)])  6.59 us
    ppermute x3, waiting for transfers between devices, shards(): lax.ppermute(dv, 'z', [(i, (i + away) % 4) for i in range(4)])  5.45 us
    ppermute x1, starting transfers between devices, shards(): kv_two = lax.ppermute(kv_here, 'x', [(0, 2), (1, 3)])  4.94 us
    ppermute x1, waiting for transfers between devices, shards(): kv_one = lax.ppermute(kv_here, 'x', [(0, 1), (1, 2), (2, 3)])  4.79 us
  transfers between devices with their start and end apart: 15, of which 10 were waited for; matrix products, arithmetic and copies ran while one was open for 0% of the time, Pallas kernels for 11%

profile of v4, /device:TPU:0, one launch (start us, length us, event | category | flops | bytes accessed | tf_op | source)
XLA Modules:
  0.0 118.2 jit_solution(3218860589486228384)
XLA Ops:
  0.6 2.6 %shard_map.99 = bf16[4,4,128,512]{3,2,1,0:T(8,128)(2,1)} custom-call(bf16[128,8192]{1,0:T(8,128)(2,1)} %bitcast.10), custom_call_target="tpu_custom_call" | custom-call | bytes 4194304 | tf_op jit(solution)/shard_map/pallas_call | solution.py:62
  3.3 31.8 %all_to_all.10.x = bf16[4,4,128,512]{3,2,1,0:T(8,128)(2,1)S(1)} all-to-all(bf16[4,4,128,512]{3,2,1,0:T(8,128)(2,1)} %shard_map.99), channel_id=1, replica_groups=mesh['y'=4,'z'=4,'x'=4,'core'=2] {'z'}, dimensions={0} | all-to-all | bytes 4194304 | tf_op jit(solution)/shard_map/all_to_all | solution.py:423
  35.0 0.0 copy-start.6
  35.0 0.0 copy-start.7
  35.0 0.0 collective-permute-start.10
  35.0 0.0 copy-start.5
  35.0 1.3 %shard_map.93 = bf16[2,128,2048]{2,1,0:T(8,128)(2,1)S(1)} custom-call(bf16[128,4096]{1,0:T(8,128)(2,1)} %bitcast.11, bf16[128,4096]{1,0:T(8,128)(2,1)} %bitcast.14), custom_call_target="tpu_custom_call" | custom-call | bytes 1048576 | tf_op jit(solution)/shard_map/pallas_call | solution.py:62
  36.3 0.5 collective-permute-start
  36.9 0.0 copy-done.6
  36.9 0.0 copy-done.7
  36.9 0.1 collective-permute-start.1
  37.0 3.8 %collective-permute-done.1 = bf16[2,128,256]{2,1,0:T(8,128)(2,1)S(1)} collective-permute-done((bf16[2,128,256]{2,1,0:T(8,128)(2,1)S(1)}, bf16[2,128,256]{2,1,0:T(8,128)(2,1)S(1)}, u32[]{:S(2)}, u32[]{:S(2)}) %collective-permute-start.1) | collective-permute-done | bytes 131104 | tf_op jit(solution)/shard_map/ppermute | solution.py:436
  40.9 0.0 copy-start
  40.9 4.9 %collective-permute-start.2 = (bf16[2,2,128,256]{3,2,1,0:T(8,128)(2,1)S(1)}, bf16[2,2,128,256]{3,2,1,0:T(8,128)(2,1)S(1)}, u32[]{:S(2)}, u32[]{:S(2)}) collective-permute-start(bf16[2,2,128,256]{3,2,1,0:T(8,128)(2,1)S(1)} %pad_maximum_fusion.kv_here), channel_id=1, source_target_pairs={{0,4},{2,6},{1,5},{3,7},{8,12},{10,14},{9,13},{11,15},{16,20},{18,... | collective-permute-start | bytes 786440 | tf_op jit(solution)/shard_map/ppermute | solution.py:437
  45.9 2.5 %collective-permute-start.3 = (bf16[2,2,128,256]{3,2,1,0:T(8,128)(2,1)S(1)}, bf16[2,2,128,256]{3,2,1,0:T(8,128)(2,1)S(1)}, u32[]{:S(2)}, u32[]{:S(2)}) collective-permute-start(bf16[2,2,128,256]{3,2,1,0:T(8,128)(2,1)S(1)} %pad_maximum_fusion.kv_here), channel_id=1, source_target_pairs={{0,2},{2,4},{4,6},{1,3},{3,5},{5,7},{8,10},{10,12},{12,14},{9,11},... | collective-permute-start | bytes 786440 | tf_op jit(solution)/shard_map/ppermute | solution.py:438
  48.4 4.2 %collective-permute-done.2.kv_two = bf16[2,2,128,256]{3,2,1,0:T(8,128)(2,1)S(1)} collective-permute-done((bf16[2,2,128,256]{3,2,1,0:T(8,128)(2,1)S(1)}, bf16[2,2,128,256]{3,2,1,0:T(8,128)(2,1)S(1)}, u32[]{:S(2)}, u32[]{:S(2)}) %collective-permute-start.2) | collective-permute-done | bytes 262176 | tf_op jit(solution)/shard_map/ppermute | solution.py:437
  52.6 0.0 copy-start.1
  52.6 4.8 %collective-permute-done.3.kv_one = bf16[2,2,128,256]{3,2,1,0:T(8,128)(2,1)S(1)} collective-permute-done((bf16[2,2,128,256]{3,2,1,0:T(8,128)(2,1)S(1)}, bf16[2,2,128,256]{3,2,1,0:T(8,128)(2,1)S(1)}, u32[]{:S(2)}, u32[]{:S(2)}) %collective-permute-start.3) | collective-permute-done | bytes 262176 | tf_op jit(solution)/shard_map/ppermute | solution.py:438
  57.4 0.0 copy-start.3
  57.4 0.0 collective-permute-done.others
  57.4 0.0 copy-done.5
  57.4 4.3 %shard_map.94 = (bf16[2,128,256]{2,1,0:T(8,128)(2,1)S(1)}, bf16[2,128,256]{2,1,0:T(8,128)(2,1)S(1)}, f32[2,128,256]{2,1,0:T(8,128)S(1)}, f32[2,16,256]{2,1,0:T(8,128)S(1)}, f32[2,640,128]{2,1,0:T(8,128)S(1)}) custom-call(s32[1,8]{1,0:T(1,128)S(1)} %copy-done.5, bf16[128,4096]{1,0:T(8,128)(2,1)} %bitcast.12, bf16[128,4096]{1,0:T(8,128)(2,1)} %bitcast.15, ...), custom_call_target="tpu_custom_call" | custom-call | flops 1342177280 | bytes 4194304 | tf_op jit(solution)/shard_map/pallas_call | solution.py:62
  61.7 0.0 copy-done
  61.7 0.0 copy-done.1
  61.7 0.0 copy-done.3
  61.7 1.3 %collective-permute-start.7 = (bf16[2,128,256]{2,1,0:T(8,128)(2,1)S(1)}, bf16[2,128,256]{2,1,0:T(8,128)(2,1)S(1)}, u32[]{:S(2)}, u32[]{:S(2)}) collective-permute-start(bf16[2,128,256]{2,1,0:T(8,128)(2,1)S(1)} %get-tuple-element.25), channel_id=1, source_target_pairs={{2,0},{4,2},{6,4},{3,1},{5,3},{7,5},{10,8},{12,10},{14,12},{11,9},... | collective-permute-start | bytes 393224 | tf_op jit(solution)/shard_map/ppermute | solution.py:450
  63.0 1.3 %collective-permute-start.8 = (bf16[2,128,256]{2,1,0:T(8,128)(2,1)S(1)}, bf16[2,128,256]{2,1,0:T(8,128)(2,1)S(1)}, u32[]{:S(2)}, u32[]{:S(2)}) collective-permute-start(bf16[2,128,256]{2,1,0:T(8,128)(2,1)S(1)} %get-tuple-element.26), channel_id=1, source_target_pairs={{4,0},{6,2},{5,1},{7,3},{12,8},{14,10},{13,9},{15,11},{20,16},{22,... | collective-permute-start | bytes 393224 | tf_op jit(solution)/shard_map/ppermute | solution.py:451
  64.3 6.6 %collective-permute-done.7.one = bf16[2,128,256]{2,1,0:T(8,128)(2,1)S(1)} collective-permute-done((bf16[2,128,256]{2,1,0:T(8,128)(2,1)S(1)}, bf16[2,128,256]{2,1,0:T(8,128)(2,1)S(1)}, u32[]{:S(2)}, u32[]{:S(2)}) %collective-permute-start.7) | collective-permute-done | bytes 131104 | tf_op jit(solution)/shard_map/ppermute | solution.py:450
  70.9 3.5 %collective-permute-done.8.two = bf16[2,128,256]{2,1,0:T(8,128)(2,1)S(1)} collective-permute-done((bf16[2,128,256]{2,1,0:T(8,128)(2,1)S(1)}, bf16[2,128,256]{2,1,0:T(8,128)(2,1)S(1)}, u32[]{:S(2)}, u32[]{:S(2)}) %collective-permute-start.8) | collective-permute-done | bytes 131104 | tf_op jit(solution)/shard_map/ppermute | solution.py:451
  74.4 0.6 collective-permute-start.11
  75.1 2.1 %collective-permute-start.12 = (bf16[2,128,256]{2,1,0:T(8,128)(2,1)S(1)}, bf16[2,128,256]{2,1,0:T(8,128)(2,1)S(1)}, u32[]{:S(2)}, u32[]{:S(2)}) collective-permute-start(bf16[2,128,256]{2,1,0:T(8,128)(2,1)S(1)} %shard_map.97.dv.refs_0_), channel_id=1, source_target_pairs={{0,16},{8,24},{16,0},{24,8},{1,17},{9,25},{17,1},{25,9},{2,18},{10... | collective-permute-start | bytes 393224 | tf_op jit(solution)/shard_map/ppermute | solution.py:456
  77.1 0.8 collective-permute-start.13
  78.0 4.8 %collective-permute-done.11.refs_1_ = bf16[2,128,256]{2,1,0:T(8,128)(2,1)S(1)} collective-permute-done((bf16[2,128,256]{2,1,0:T(8,128)(2,1)S(1)}, bf16[2,128,256]{2,1,0:T(8,128)(2,1)S(1)}, u32[]{:S(2)}, u32[]{:S(2)}) %collective-permute-start.11) | collective-permute-done | bytes 131104 | tf_op jit(solution)/shard_map/ppermute | solution.py:456
  82.8 0.0 collective-permute-done.12.refs_2_
  82.8 0.6 collective-permute-done.13.refs_3_
  83.4 0.8 shard_map.100.past
  84.2 0.0 collective-permute-done.10.x
  84.2 3.3 %shard_map.101 = bf16[2048,256]{1,0:T(8,128)(2,1)} custom-call(bf16[4,4,128,512]{3,2,1,0:T(8,128)(2,1)} %collective-permute-done.10.x, f32[2048,256]{1,0:T(8,128)S(1)} %shard_map.100.past, bf16[2,128,256]{2,1,0:T(8,128)(2,1)S(1)} %shard_map.97.dv.refs_0_, bf16[2,128,256]{2,1,0:T(8,128)(2,1)S(1)} %collective-permute-done.11.refs_1_, ...), custom_call_target="tpu_custom_call" | custom-call | flops 536870912 | bytes 4194304 | tf_op jit(solution)/shard_map/pallas_call | solution.py:62
  87.5 0.0 copy-start.2
  87.5 0.0 copy-start.4
  87.5 7.4 %all-to-all-start.1 = ((bf16[32,64,256]{2,1,0:T(8,128)(2,1)}), bf16[32,64,256]{2,1,0:T(8,128)(2,1)S(1)}, u32[]{:S(2)}, u32[]{:S(2)}) async-start(bf16[32,64,256]{2,1,0:T(8,128)(2,1)} %bitcast.8), calls=%async_computation.1 | async-start | bytes 2097152 | tf_op jit(solution)/shard_map/all_to_all | solution.py:423
  94.9 0.0 copy-done.2
  94.9 0.0 copy-done.4
  94.9 5.7 %shard_map.95 = (bf16[128,4096]{1,0:T(8,128)(2,1)}, bf16[128,2048]{1,0:T(8,128)(2,1)S(1)}, bf16[2,128,256]{2,1,0:T(8,128)(2,1)S(1)}, bf16[2,128,256]{2,1,0:T(8,128)(2,1)S(1)}, f32[2,128,256]{2,1,0:T(8,128)S(1)}) custom-call(s32[1,8]{1,0:T(1,128)S(1)} %copy-done.5, bf16[128,4096]{1,0:T(8,128)(2,1)} %bitcast.13, bf16[128,4096]{1,0:T(8,128)(2,1)} %bitcast.16, ...), custom_call_target="tpu_custom_call" | custom-call | flops 2684354560 | bytes 4194304 | tf_op jit(solution)/shard_map/pallas_call | solution.py:62
  100.6 0.4 collective-permute-start.4
  101.0 1.3 %collective-permute-start.5 = (bf16[2,128,256]{2,1,0:T(8,128)(2,1)S(1)}, bf16[2,128,256]{2,1,0:T(8,128)(2,1)S(1)}, u32[]{:S(2)}, u32[]{:S(2)}) collective-permute-start(bf16[2,128,256]{2,1,0:T(8,128)(2,1)S(1)} %get-tuple-element.22), channel_id=1, source_target_pairs={{2,0},{4,2},{6,4},{3,1},{5,3},{7,5},{10,8},{12,10},{14,12},{11,9},... | collective-permute-start | bytes 393224 | tf_op jit(solution)/shard_map/ppermute | solution.py:450
  102.2 1.3 %collective-permute-start.6 = (bf16[2,128,256]{2,1,0:T(8,128)(2,1)S(1)}, bf16[2,128,256]{2,1,0:T(8,128)(2,1)S(1)}, u32[]{:S(2)}, u32[]{:S(2)}) collective-permute-start(bf16[2,128,256]{2,1,0:T(8,128)(2,1)S(1)} %get-tuple-element.23), channel_id=1, source_target_pairs={{4,0},{6,2},{5,1},{7,3},{12,8},{14,10},{13,9},{15,11},{20,16},{22,... | collective-permute-start | bytes 393224 | tf_op jit(solution)/shard_map/ppermute | solution.py:451
  103.6 8.3 %collective-permute-done.5.one = bf16[2,128,256]{2,1,0:T(8,128)(2,1)S(1)} collective-permute-done((bf16[2,128,256]{2,1,0:T(8,128)(2,1)S(1)}, bf16[2,128,256]{2,1,0:T(8,128)(2,1)S(1)}, u32[]{:S(2)}, u32[]{:S(2)}) %collective-permute-start.5) | collective-permute-done | bytes 131104 | tf_op jit(solution)/shard_map/ppermute | solution.py:450
  111.9 3.1 %collective-permute-done.6.two = bf16[2,128,256]{2,1,0:T(8,128)(2,1)S(1)} collective-permute-done((bf16[2,128,256]{2,1,0:T(8,128)(2,1)S(1)}, bf16[2,128,256]{2,1,0:T(8,128)(2,1)S(1)}, u32[]{:S(2)}, u32[]{:S(2)}) %collective-permute-start.6) | collective-permute-done | bytes 131104 | tf_op jit(solution)/shard_map/ppermute | solution.py:451
  115.0 0.1 collective-permute-start.9
  115.1 1.3 %collective-permute-done.9.got = bf16[2,128,256]{2,1,0:T(8,128)(2,1)S(1)} collective-permute-done((bf16[2,128,256]{2,1,0:T(8,128)(2,1)S(1)}, bf16[2,128,256]{2,1,0:T(8,128)(2,1)S(1)}, u32[]{:S(2)}, u32[]{:S(2)}) %collective-permute-start.9) | collective-permute-done | bytes 131104 | tf_op jit(solution)/shard_map/ppermute | solution.py:463
  116.4 0.0 collective-permute-done.4.dq_got
  116.4 0.9 shard_map.98
  117.4 0.0 all-to-all-done.1.got
  117.4 0.8 weight_sum.1
  (9 shorter events, 0.2 us)
Async XLA Ops:
  35.0 1.8 %copy-start.6 = (bf16[1,128,512]{2,1,0:T(8,128)(2,1)S(1)}, bf16[1,128,512]{2,1,0:T(8,128)(2,1)}, u32[]{:S(2)}) copy-start(bf16[1,128,512]{2,1,0:T(8,128)(2,1)} %param.8) | copy-start | bytes 393220
  35.0 1.8 %copy-start.7 = (bf16[1,128,512]{2,1,0:T(8,128)(2,1)S(1)}, bf16[1,128,512]{2,1,0:T(8,128)(2,1)}, u32[]{:S(2)}) copy-start(bf16[1,128,512]{2,1,0:T(8,128)(2,1)} %param.7) | copy-start | bytes 393220
  35.0 49.2 %collective-permute-start.10 = (bf16[4,4,128,512]{3,2,1,0:T(8,128)(2,1)S(1)}, bf16[4,4,128,512]{3,2,1,0:T(8,128)(2,1)}, u32[]{:S(2)}, u32[]{:S(2)}) collective-permute-start(bf16[4,4,128,512]{3,2,1,0:T(8,128)(2,1)S(1)} %all_to_all.10.x), channel_id=1, source_target_pairs={{0,1},{1,0},{2,3},{3,2},{4,5},{5,4},{6,7},{7,6},{8,9},{9,8},{10,11... | collective-permute-start | bytes 6291464 | tf_op jit(solution)/shard_map/ppermute | solution.py:443
  35.0 22.3 %copy-start.5 = (s32[1,8]{1,0:T(1,128)S(1)}, s32[1,8]{1,0:T(1,128)}, u32[]{:S(2)}) copy-start(s32[1,8]{1,0:T(1,128)} %lengths.3) | copy-start | bytes 100
  36.3 21.1 %collective-permute-start = (bf16[2,128,2048]{2,1,0:T(8,128)(2,1)S(1)}, bf16[2,128,2048]{2,1,0:T(8,128)(2,1)}, u32[]{:S(2)}, u32[]{:S(2)}) collective-permute-start(bf16[2,128,2048]{2,1,0:T(8,128)(2,1)S(1)} %shard_map.93), channel_id=1, source_target_pairs={{0,1},{1,0},{2,3},{3,2},{4,5},{5,4},{6,7},{7,6},{8,9},{9,8},{10,11... | collective-permute-start | bytes 3145736 | tf_op jit(solution)/shard_map/ppermute | solution.py:440
  36.9 4.0 %collective-permute-start.1 = (bf16[2,128,256]{2,1,0:T(8,128)(2,1)S(1)}, bf16[2,128,256]{2,1,0:T(8,128)(2,1)S(1)}, u32[]{:S(2)}, u32[]{:S(2)}) collective-permute-start(bf16[2,128,256]{2,1,0:T(8,128)(2,1)S(1)} %pad_maximum_fusion.1), channel_id=1, source_target_pairs={{0,1},{1,0},{2,3},{3,2},{4,5},{5,4},{6,7},{7,6},{8,9},{9,8},{10,11... | collective-permute-start | bytes 393224 | tf_op jit(solution)/shard_map/ppermute | solution.py:436
  40.9 20.8 %copy-start = (bf16[2,2,128,256]{3,2,1,0:T(8,128)(2,1)}, bf16[2,2,128,256]{3,2,1,0:T(8,128)(2,1)S(1)}, u32[]{:S(2)}) copy-start(bf16[2,2,128,256]{3,2,1,0:T(8,128)(2,1)S(1)} %pad_maximum_fusion.kv_here) | copy-start | bytes 786436
  40.9 11.7 %collective-permute-start.2 = (bf16[2,2,128,256]{3,2,1,0:T(8,128)(2,1)S(1)}, bf16[2,2,128,256]{3,2,1,0:T(8,128)(2,1)S(1)}, u32[]{:S(2)}, u32[]{:S(2)}) collective-permute-start(bf16[2,2,128,256]{3,2,1,0:T(8,128)(2,1)S(1)} %pad_maximum_fusion.kv_here), channel_id=1, source_target_pairs={{0,4},{2,6},{1,5},{3,7},{8,12},{10,14},{9,13},{11,15},{16,20},{18,... | collective-permute-start | bytes 786440 | tf_op jit(solution)/shard_map/ppermute | solution.py:437
  45.9 11.5 %collective-permute-start.3 = (bf16[2,2,128,256]{3,2,1,0:T(8,128)(2,1)S(1)}, bf16[2,2,128,256]{3,2,1,0:T(8,128)(2,1)S(1)}, u32[]{:S(2)}, u32[]{:S(2)}) collective-permute-start(bf16[2,2,128,256]{3,2,1,0:T(8,128)(2,1)S(1)} %pad_maximum_fusion.kv_here), channel_id=1, source_target_pairs={{0,2},{2,4},{4,6},{1,3},{3,5},{5,7},{8,10},{10,12},{12,14},{9,11},... | collective-permute-start | bytes 786440 | tf_op jit(solution)/shard_map/ppermute | solution.py:438
  52.6 9.1 %copy-start.1 = (bf16[2,2,128,256]{3,2,1,0:T(8,128)(2,1)}, bf16[2,2,128,256]{3,2,1,0:T(8,128)(2,1)S(1)}, u32[]{:S(2)}) copy-start(bf16[2,2,128,256]{3,2,1,0:T(8,128)(2,1)S(1)} %collective-permute-done.2.kv_two) | copy-start | bytes 786436
  57.4 4.3 %copy-start.3 = (bf16[2,2,128,256]{3,2,1,0:T(8,128)(2,1)}, bf16[2,2,128,256]{3,2,1,0:T(8,128)(2,1)S(1)}, u32[]{:S(2)}) copy-start(bf16[2,2,128,256]{3,2,1,0:T(8,128)(2,1)S(1)} %collective-permute-done.3.kv_one) | copy-start | bytes 786436
  61.7 9.2 %collective-permute-start.7 = (bf16[2,128,256]{2,1,0:T(8,128)(2,1)S(1)}, bf16[2,128,256]{2,1,0:T(8,128)(2,1)S(1)}, u32[]{:S(2)}, u32[]{:S(2)}) collective-permute-start(bf16[2,128,256]{2,1,0:T(8,128)(2,1)S(1)} %get-tuple-element.25), channel_id=1, source_target_pairs={{2,0},{4,2},{6,4},{3,1},{5,3},{7,5},{10,8},{12,10},{14,12},{11,9},... | collective-permute-start | bytes 393224 | tf_op jit(solution)/shard_map/ppermute | solution.py:450
  63.0 11.4 %collective-permute-start.8 = (bf16[2,128,256]{2,1,0:T(8,128)(2,1)S(1)}, bf16[2,128,256]{2,1,0:T(8,128)(2,1)S(1)}, u32[]{:S(2)}, u32[]{:S(2)}) collective-permute-start(bf16[2,128,256]{2,1,0:T(8,128)(2,1)S(1)} %get-tuple-element.26), channel_id=1, source_target_pairs={{4,0},{6,2},{5,1},{7,3},{12,8},{14,10},{13,9},{15,11},{20,16},{22,... | collective-permute-start | bytes 393224 | tf_op jit(solution)/shard_map/ppermute | solution.py:451
  74.4 8.3 %collective-permute-start.11 = (bf16[2,128,256]{2,1,0:T(8,128)(2,1)S(1)}, bf16[2,128,256]{2,1,0:T(8,128)(2,1)S(1)}, u32[]{:S(2)}, u32[]{:S(2)}) collective-permute-start(bf16[2,128,256]{2,1,0:T(8,128)(2,1)S(1)} %shard_map.97.dv.refs_0_), channel_id=1, source_target_pairs={{0,8},{8,16},{16,24},{24,0},{1,9},{9,17},{17,25},{25,1},{2,10},{10... | collective-permute-start | bytes 393224 | tf_op jit(solution)/shard_map/ppermute | solution.py:456
  75.1 7.7 %collective-permute-start.12 = (bf16[2,128,256]{2,1,0:T(8,128)(2,1)S(1)}, bf16[2,128,256]{2,1,0:T(8,128)(2,1)S(1)}, u32[]{:S(2)}, u32[]{:S(2)}) collective-permute-start(bf16[2,128,256]{2,1,0:T(8,128)(2,1)S(1)} %shard_map.97.dv.refs_0_), channel_id=1, source_target_pairs={{0,16},{8,24},{16,0},{24,8},{1,17},{9,25},{17,1},{25,9},{2,18},{10... | collective-permute-start | bytes 393224 | tf_op jit(solution)/shard_map/ppermute | solution.py:456
  77.1 6.3 %collective-permute-start.13 = (bf16[2,128,256]{2,1,0:T(8,128)(2,1)S(1)}, bf16[2,128,256]{2,1,0:T(8,128)(2,1)S(1)}, u32[]{:S(2)}, u32[]{:S(2)}) collective-permute-start(bf16[2,128,256]{2,1,0:T(8,128)(2,1)S(1)} %shard_map.97.dv.refs_0_), channel_id=1, source_target_pairs={{0,24},{8,0},{16,8},{24,16},{1,25},{9,1},{17,9},{25,17},{2,26},{10... | collective-permute-start | bytes 393224 | tf_op jit(solution)/shard_map/ppermute | solution.py:456
  87.5 7.4 %copy-start.2 = (bf16[2,2,128,256]{3,2,1,0:T(8,128)(2,1)S(1)}, bf16[2,2,128,256]{3,2,1,0:T(8,128)(2,1)}, u32[]{:S(2)}) copy-start(bf16[2,2,128,256]{3,2,1,0:T(8,128)(2,1)} %copy-done.1) | copy-start | bytes 786436
  87.5 7.4 %copy-start.4 = (bf16[2,2,128,256]{3,2,1,0:T(8,128)(2,1)S(1)}, bf16[2,2,128,256]{3,2,1,0:T(8,128)(2,1)}, u32[]{:S(2)}) copy-start(bf16[2,2,128,256]{3,2,1,0:T(8,128)(2,1)} %copy-done.3) | copy-start | bytes 786436
  87.5 29.9 %all-to-all-start.1 = ((bf16[32,64,256]{2,1,0:T(8,128)(2,1)}), bf16[32,64,256]{2,1,0:T(8,128)(2,1)S(1)}, u32[]{:S(2)}, u32[]{:S(2)}) async-start(bf16[32,64,256]{2,1,0:T(8,128)(2,1)} %bitcast.8), calls=%async_computation.1 | async-start | bytes 2097152 | tf_op jit(solution)/shard_map/all_to_all | solution.py:423
  100.6 15.8 %collective-permute-start.4 = (bf16[128,2048]{1,0:T(8,128)(2,1)S(1)}, bf16[128,2048]{1,0:T(8,128)(2,1)S(1)}, u32[]{:S(2)}, u32[]{:S(2)}) collective-permute-start(bf16[128,2048]{1,0:T(8,128)(2,1)S(1)} %get-tuple-element.20), channel_id=1, source_target_pairs={{0,1},{1,0},{2,3},{3,2},{4,5},{5,4},{6,7},{7,6},{8,9},{9,8},{10,11... | collective-permute-start | bytes 1572872 | tf_op jit(solution)/shard_map/ppermute | solution.py:462
  101.0 10.9 %collective-permute-start.5 = (bf16[2,128,256]{2,1,0:T(8,128)(2,1)S(1)}, bf16[2,128,256]{2,1,0:T(8,128)(2,1)S(1)}, u32[]{:S(2)}, u32[]{:S(2)}) collective-permute-start(bf16[2,128,256]{2,1,0:T(8,128)(2,1)S(1)} %get-tuple-element.22), channel_id=1, source_target_pairs={{2,0},{4,2},{6,4},{3,1},{5,3},{7,5},{10,8},{12,10},{14,12},{11,9},... | collective-permute-start | bytes 393224 | tf_op jit(solution)/shard_map/ppermute | solution.py:450
  102.2 12.7 %collective-permute-start.6 = (bf16[2,128,256]{2,1,0:T(8,128)(2,1)S(1)}, bf16[2,128,256]{2,1,0:T(8,128)(2,1)S(1)}, u32[]{:S(2)}, u32[]{:S(2)}) collective-permute-start(bf16[2,128,256]{2,1,0:T(8,128)(2,1)S(1)} %get-tuple-element.23), channel_id=1, source_target_pairs={{4,0},{6,2},{5,1},{7,3},{12,8},{14,10},{13,9},{15,11},{20,16},{22,... | collective-permute-start | bytes 393224 | tf_op jit(solution)/shard_map/ppermute | solution.py:451
  115.0 1.4 %collective-permute-start.9 = (bf16[2,128,256]{2,1,0:T(8,128)(2,1)S(1)}, bf16[2,128,256]{2,1,0:T(8,128)(2,1)S(1)}, u32[]{:S(2)}, u32[]{:S(2)}) collective-permute-start(bf16[2,128,256]{2,1,0:T(8,128)(2,1)S(1)} %pad_maximum_fusion.2), channel_id=1, source_target_pairs={{0,1},{1,0},{2,3},{3,2},{4,5},{5,4},{6,7},{7,6},{8,9},{9,8},{10,11... | collective-permute-start | bytes 393224 | tf_op jit(solution)/shard_map/ppermute | solution.py:463

commit v5 on v4

--- a/solution.py
+++ b/solution.py
@@ -249,7 +249,7 @@
 
 
 def scores_body(
-    small, core, own, others, loads, k_buf, v_buf, k_t, stat_ref, bias_ref, dk_acc, dq_refs
+    small, core, own, others, loads, k_buf, v_buf, k_t, stat_ref, bias_ref, dk_acc, dq_buf
 ):
     win = 2 if small else WIN
 
@@ -279,17 +279,21 @@
         for i in range(2):
             start = group * WIDTH + (2 * pair + i) * HD
             dq = dq_t[:, i * BLK : (i + 1) * BLK].T.astype(BF16)
-            dq_refs[side][:, start : start + HD] = dq
+            dq_buf[side, :, start : start + HD] = dq
 
 
 def scores_kernel(
     lengths, q_hbm, do_hbm, others, kv_two, kv_one, kv_here, stat_ref, bias_ref,
-    dq_hbm, dq_sent, dk_two, dk_one, dk_here,
-    k_buf, v_buf, k_t, dk_acc, own, sems, dq_buf, out_sem,
+    dq_hbm, sent_hbm, dk_two, dk_one, dk_here,
+    k_buf, v_buf, k_t, dk_acc, own, sems, dq_buf, out_sems,
 ):
     chip, core = lax.axis_index("x"), lax.axis_index("core")
     loads = load_own(core, q_hbm, do_hbm, own, sems)
-    store = pltpu.make_async_copy(dq_buf, dq_hbm.at[:, lanes(core * HALF, HALF)], out_sem)
+    targets = (dq_hbm.at[:, lanes(core * HALF, HALF)], sent_hbm)
+    stores = [
+        pltpu.make_async_copy(dq_buf.at[side], target, out_sems.at[side])
+        for side, target in enumerate(targets)
+    ]
     for group in range(2):
         gather_keys(core, (kv_two, kv_one, kv_here), 0, group, k_buf)
         gather_keys(core, (kv_two, kv_one, kv_here), 1, group, v_buf)
@@ -300,11 +304,13 @@
         def _():
             scores_body(
                 small, core, own, others, loads, k_buf, v_buf, k_t, stat_ref, bias_ref, dk_acc,
-                (dq_buf, dq_sent),
+                dq_buf,
             )
-    store.start()
+    for store in stores:
+        store.start()
     store_parts(core, dk_acc, (dk_two, dk_one, dk_here), SCALE)
-    store.wait()
+    for store in stores:
+        store.wait()
 
 
 PARTS = [pltpu.VMEM((2, BLK, COLS), kind) for kind in (BF16, BF16, F32)]
@@ -328,10 +334,10 @@
 def attention_scores(operands, stats, bias):
     return call(
         scores_kernel, OPERANDS[:3] + [ANYWHERE] * 4 + [IN_VMEM] * 2,
-        [jax.ShapeDtypeStruct((BLK, 2 * HALF), BF16), pltpu.VMEM((BLK, HALF), BF16)] + PARTS,
+        [pltpu.HBM((BLK, width), BF16) for width in (2 * HALF, HALF)] + PARTS,
         [*operands[:-1], far(operands[-1]), stats, bias],
         [KEYS, KEYS, TURNED, TOTAL] + OWN
-        + [pltpu.VMEM((BLK, HALF), BF16), pltpu.SemaphoreType.DMA(())],
+        + [pltpu.VMEM((2, BLK, HALF), BF16), pltpu.SemaphoreType.DMA((2,))],
         flops=4 * PRODUCT, exps=PRODUCT // 256, moved=4 << 20, room=16,
     )
 

time: 120 us -> 120 us (level)
  no operation moved by 1% of the time
where the time goes in v5:
time: 120 us; the launch traced here: 118 us
  waiting for transfers between devices  41.1 us (34%)
  blocking collectives  31.8 us (26%)
  starting transfers between devices  24.6 us (20%)
  Pallas kernels  19.9 us (17%)
    all_to_all x1, blocking collectives, exchange(): return lax.all_to_all(value, axes, 0, 0, tiled=True)  31.8 us
    pallas_call x9, Pallas kernels, call(): pl.pallas_call(kernel, in_specs=list(in_specs), out_specs=out_specs, out_...  19.1 us
    ppermute x2, waiting for transfers between devices, summed(): one = lax.ppermute(one, 'x', [(1, 0), (2, 1), (3, 2)])  14.9 us
    all_to_all x1, starting transfers between devices, exchange(): return lax.all_to_all(value, axes, 0, 0, tiled=True)  7.38 us
    ppermute x2, waiting for transfers between devices, summed(): two = lax.ppermute(two, 'x', [(2, 0), (3, 1)])  6.59 us
    ppermute x3, waiting for transfers between devices, shards(): lax.ppermute(dv, 'z', [(i, (i + away) % 4) for i in range(4)])  5.45 us
    ppermute x1, starting transfers between devices, shards(): kv_two = lax.ppermute(kv_here, 'x', [(0, 2), (1, 3)])  4.94 us
    ppermute x1, waiting for transfers between devices, shards(): kv_one = lax.ppermute(kv_here, 'x', [(0, 1), (1, 2), (2, 3)])  4.79 us
  transfers between devices with their start and end apart: 15, of which 10 were waited for; matrix products, arithmetic and copies ran while one was open for 0% of the time, Pallas kernels for 11%

profile of v5, /device:TPU:0, one launch (start us, length us, event | category | flops | bytes accessed | tf_op | source)
XLA Modules:
  0.0 118.4 jit_solution(6869193596127663946)
XLA Ops:
  0.6 2.6 %shard_map.99 = bf16[4,4,128,512]{3,2,1,0:T(8,128)(2,1)} custom-call(bf16[128,8192]{1,0:T(8,128)(2,1)} %bitcast.10), custom_call_target="tpu_custom_call" | custom-call | bytes 4194304 | tf_op jit(solution)/shard_map/pallas_call | solution.py:62
  3.3 31.8 %all_to_all.10.x = bf16[4,4,128,512]{3,2,1,0:T(8,128)(2,1)S(1)} all-to-all(bf16[4,4,128,512]{3,2,1,0:T(8,128)(2,1)} %shard_map.99), channel_id=1, replica_groups=mesh['y'=4,'z'=4,'x'=4,'core'=2] {'z'}, dimensions={0} | all-to-all | bytes 4194304 | tf_op jit(solution)/shard_map/all_to_all | solution.py:429
  35.0 0.0 copy-start.6
  35.0 0.0 copy-start.7
  35.0 0.0 collective-permute-start.10
  35.0 0.0 copy-start.5
  35.0 1.3 %shard_map.93 = bf16[2,128,2048]{2,1,0:T(8,128)(2,1)S(1)} custom-call(bf16[128,4096]{1,0:T(8,128)(2,1)} %bitcast.11, bf16[128,4096]{1,0:T(8,128)(2,1)} %bitcast.14), custom_call_target="tpu_custom_call" | custom-call | bytes 1048576 | tf_op jit(solution)/shard_map/pallas_call | solution.py:62
  36.3 0.5 collective-permute-start
  36.9 0.0 copy-done.6
  36.9 0.0 copy-done.7
  36.9 0.1 collective-permute-start.1
  37.0 3.8 %collective-permute-done.1 = bf16[2,128,256]{2,1,0:T(8,128)(2,1)S(1)} collective-permute-done((bf16[2,128,256]{2,1,0:T(8,128)(2,1)S(1)}, bf16[2,128,256]{2,1,0:T(8,128)(2,1)S(1)}, u32[]{:S(2)}, u32[]{:S(2)}) %collective-permute-start.1) | collective-permute-done | bytes 131104 | tf_op jit(solution)/shard_map/ppermute | solution.py:442
  40.9 0.0 copy-start
  40.9 4.9 %collective-permute-start.2 = (bf16[2,2,128,256]{3,2,1,0:T(8,128)(2,1)S(1)}, bf16[2,2,128,256]{3,2,1,0:T(8,128)(2,1)S(1)}, u32[]{:S(2)}, u32[]{:S(2)}) collective-permute-start(bf16[2,2,128,256]{3,2,1,0:T(8,128)(2,1)S(1)} %pad_maximum_fusion.kv_here), channel_id=1, source_target_pairs={{0,4},{2,6},{1,5},{3,7},{8,12},{10,14},{9,13},{11,15},{16,20},{18,... | collective-permute-start | bytes 786440 | tf_op jit(solution)/shard_map/ppermute | solution.py:443
  45.9 2.5 %collective-permute-start.3 = (bf16[2,2,128,256]{3,2,1,0:T(8,128)(2,1)S(1)}, bf16[2,2,128,256]{3,2,1,0:T(8,128)(2,1)S(1)}, u32[]{:S(2)}, u32[]{:S(2)}) collective-permute-start(bf16[2,2,128,256]{3,2,1,0:T(8,128)(2,1)S(1)} %pad_maximum_fusion.kv_here), channel_id=1, source_target_pairs={{0,2},{2,4},{4,6},{1,3},{3,5},{5,7},{8,10},{10,12},{12,14},{9,11},... | collective-permute-start | bytes 786440 | tf_op jit(solution)/shard_map/ppermute | solution.py:444
  48.4 4.2 %collective-permute-done.2.kv_two = bf16[2,2,128,256]{3,2,1,0:T(8,128)(2,1)S(1)} collective-permute-done((bf16[2,2,128,256]{3,2,1,0:T(8,128)(2,1)S(1)}, bf16[2,2,128,256]{3,2,1,0:T(8,128)(2,1)S(1)}, u32[]{:S(2)}, u32[]{:S(2)}) %collective-permute-start.2) | collective-permute-done | bytes 262176 | tf_op jit(solution)/shard_map/ppermute | solution.py:443
  52.6 0.0 copy-start.1
  52.6 4.8 %collective-permute-done.3.kv_one = bf16[2,2,128,256]{3,2,1,0:T(8,128)(2,1)S(1)} collective-permute-done((bf16[2,2,128,256]{3,2,1,0:T(8,128)(2,1)S(1)}, bf16[2,2,128,256]{3,2,1,0:T(8,128)(2,1)S(1)}, u32[]{:S(2)}, u32[]{:S(2)}) %collective-permute-start.3) | collective-permute-done | bytes 262176 | tf_op jit(solution)/shard_map/ppermute | solution.py:444
  57.4 0.0 copy-start.3
  57.4 0.0 collective-permute-done.others
  57.4 0.0 copy-done.5
  57.4 4.3 %shard_map.94 = (bf16[2,128,256]{2,1,0:T(8,128)(2,1)S(1)}, bf16[2,128,256]{2,1,0:T(8,128)(2,1)S(1)}, f32[2,128,256]{2,1,0:T(8,128)S(1)}, f32[2,16,256]{2,1,0:T(8,128)S(1)}, f32[2,640,128]{2,1,0:T(8,128)S(1)}) custom-call(s32[1,8]{1,0:T(1,128)S(1)} %copy-done.5, bf16[128,4096]{1,0:T(8,128)(2,1)} %bitcast.12, bf16[128,4096]{1,0:T(8,128)(2,1)} %bitcast.15, ...), custom_call_target="tpu_custom_call" | custom-call | flops 1342177280 | bytes 4194304 | tf_op jit(solution)/shard_map/pallas_call | solution.py:62
  61.7 0.0 copy-done
  61.7 0.0 copy-done.1
  61.7 0.0 copy-done.3
  61.7 1.3 %collective-permute-start.7 = (bf16[2,128,256]{2,1,0:T(8,128)(2,1)S(1)}, bf16[2,128,256]{2,1,0:T(8,128)(2,1)S(1)}, u32[]{:S(2)}, u32[]{:S(2)}) collective-permute-start(bf16[2,128,256]{2,1,0:T(8,128)(2,1)S(1)} %get-tuple-element.25), channel_id=1, source_target_pairs={{2,0},{4,2},{6,4},{3,1},{5,3},{7,5},{10,8},{12,10},{14,12},{11,9},... | collective-permute-start | bytes 393224 | tf_op jit(solution)/shard_map/ppermute | solution.py:456
  63.0 1.3 %collective-permute-start.8 = (bf16[2,128,256]{2,1,0:T(8,128)(2,1)S(1)}, bf16[2,128,256]{2,1,0:T(8,128)(2,1)S(1)}, u32[]{:S(2)}, u32[]{:S(2)}) collective-permute-start(bf16[2,128,256]{2,1,0:T(8,128)(2,1)S(1)} %get-tuple-element.26), channel_id=1, source_target_pairs={{4,0},{6,2},{5,1},{7,3},{12,8},{14,10},{13,9},{15,11},{20,16},{22,... | collective-permute-start | bytes 393224 | tf_op jit(solution)/shard_map/ppermute | solution.py:457
  64.3 6.6 %collective-permute-done.7.one = bf16[2,128,256]{2,1,0:T(8,128)(2,1)S(1)} collective-permute-done((bf16[2,128,256]{2,1,0:T(8,128)(2,1)S(1)}, bf16[2,128,256]{2,1,0:T(8,128)(2,1)S(1)}, u32[]{:S(2)}, u32[]{:S(2)}) %collective-permute-start.7) | collective-permute-done | bytes 131104 | tf_op jit(solution)/shard_map/ppermute | solution.py:456
  70.9 3.5 %collective-permute-done.8.two = bf16[2,128,256]{2,1,0:T(8,128)(2,1)S(1)} collective-permute-done((bf16[2,128,256]{2,1,0:T(8,128)(2,1)S(1)}, bf16[2,128,256]{2,1,0:T(8,128)(2,1)S(1)}, u32[]{:S(2)}, u32[]{:S(2)}) %collective-permute-start.8) | collective-permute-done | bytes 131104 | tf_op jit(solution)/shard_map/ppermute | solution.py:457
  74.4 0.6 collective-permute-start.11
  75.1 2.1 %collective-permute-start.12 = (bf16[2,128,256]{2,1,0:T(8,128)(2,1)S(1)}, bf16[2,128,256]{2,1,0:T(8,128)(2,1)S(1)}, u32[]{:S(2)}, u32[]{:S(2)}) collective-permute-start(bf16[2,128,256]{2,1,0:T(8,128)(2,1)S(1)} %shard_map.97.dv.refs_0_), channel_id=1, source_target_pairs={{0,16},{8,24},{16,0},{24,8},{1,17},{9,25},{17,1},{25,9},{2,18},{10... | collective-permute-start | bytes 393224 | tf_op jit(solution)/shard_map/ppermute | solution.py:462
  77.1 0.8 collective-permute-start.13
  78.0 4.8 %collective-permute-done.11.refs_1_ = bf16[2,128,256]{2,1,0:T(8,128)(2,1)S(1)} collective-permute-done((bf16[2,128,256]{2,1,0:T(8,128)(2,1)S(1)}, bf16[2,128,256]{2,1,0:T(8,128)(2,1)S(1)}, u32[]{:S(2)}, u32[]{:S(2)}) %collective-permute-start.11) | collective-permute-done | bytes 131104 | tf_op jit(solution)/shard_map/ppermute | solution.py:462
  82.8 0.0 collective-permute-done.12.refs_2_
  82.8 0.6 collective-permute-done.13.refs_3_
  83.4 0.8 shard_map.100.past
  84.2 0.0 collective-permute-done.10.x
  84.2 3.3 %shard_map.101 = bf16[2048,256]{1,0:T(8,128)(2,1)} custom-call(bf16[4,4,128,512]{3,2,1,0:T(8,128)(2,1)} %collective-permute-done.10.x, f32[2048,256]{1,0:T(8,128)S(1)} %shard_map.100.past, bf16[2,128,256]{2,1,0:T(8,128)(2,1)S(1)} %shard_map.97.dv.refs_0_, bf16[2,128,256]{2,1,0:T(8,128)(2,1)S(1)} %collective-permute-done.11.refs_1_, ...), custom_call_target="tpu_custom_call" | custom-call | flops 536870912 | bytes 4194304 | tf_op jit(solution)/shard_map/pallas_call | solution.py:62
  87.5 0.0 copy-start.2
  87.5 0.0 copy-start.4
  87.5 7.4 %all-to-all-start.1 = ((bf16[32,64,256]{2,1,0:T(8,128)(2,1)}), bf16[32,64,256]{2,1,0:T(8,128)(2,1)S(1)}, u32[]{:S(2)}, u32[]{:S(2)}) async-start(bf16[32,64,256]{2,1,0:T(8,128)(2,1)} %bitcast.8), calls=%async_computation.1 | async-start | bytes 2097152 | tf_op jit(solution)/shard_map/all_to_all | solution.py:429
  94.9 0.0 copy-done.2
  94.9 0.0 copy-done.4
  94.9 5.9 %shard_map.95 = (bf16[128,4096]{1,0:T(8,128)(2,1)}, bf16[128,2048]{1,0:T(8,128)(2,1)}, bf16[2,128,256]{2,1,0:T(8,128)(2,1)S(1)}, bf16[2,128,256]{2,1,0:T(8,128)(2,1)S(1)}, f32[2,128,256]{2,1,0:T(8,128)S(1)}) custom-call(s32[1,8]{1,0:T(1,128)S(1)} %copy-done.5, bf16[128,4096]{1,0:T(8,128)(2,1)} %bitcast.13, bf16[128,4096]{1,0:T(8,128)(2,1)} %bitcast.16, ...), custom_call_target="tpu_custom_call" | custom-call | flops 2684354560 | bytes 4194304 | tf_op jit(solution)/shard_map/pallas_call | solution.py:62
  100.8 0.3 collective-permute-start.4
  101.2 1.3 %collective-permute-start.5 = (bf16[2,128,256]{2,1,0:T(8,128)(2,1)S(1)}, bf16[2,128,256]{2,1,0:T(8,128)(2,1)S(1)}, u32[]{:S(2)}, u32[]{:S(2)}) collective-permute-start(bf16[2,128,256]{2,1,0:T(8,128)(2,1)S(1)} %get-tuple-element.22), channel_id=1, source_target_pairs={{2,0},{4,2},{6,4},{3,1},{5,3},{7,5},{10,8},{12,10},{14,12},{11,9},... | collective-permute-start | bytes 393224 | tf_op jit(solution)/shard_map/ppermute | solution.py:456
  102.4 1.3 %collective-permute-start.6 = (bf16[2,128,256]{2,1,0:T(8,128)(2,1)S(1)}, bf16[2,128,256]{2,1,0:T(8,128)(2,1)S(1)}, u32[]{:S(2)}, u32[]{:S(2)}) collective-permute-start(bf16[2,128,256]{2,1,0:T(8,128)(2,1)S(1)} %get-tuple-element.23), channel_id=1, source_target_pairs={{4,0},{6,2},{5,1},{7,3},{12,8},{14,10},{13,9},{15,11},{20,16},{22,... | collective-permute-start | bytes 393224 | tf_op jit(solution)/shard_map/ppermute | solution.py:457
  103.8 8.3 %collective-permute-done.5.one = bf16[2,128,256]{2,1,0:T(8,128)(2,1)S(1)} collective-permute-done((bf16[2,128,256]{2,1,0:T(8,128)(2,1)S(1)}, bf16[2,128,256]{2,1,0:T(8,128)(2,1)S(1)}, u32[]{:S(2)}, u32[]{:S(2)}) %collective-permute-start.5) | collective-permute-done | bytes 131104 | tf_op jit(solution)/shard_map/ppermute | solution.py:456
  112.1 3.1 %collective-permute-done.6.two = bf16[2,128,256]{2,1,0:T(8,128)(2,1)S(1)} collective-permute-done((bf16[2,128,256]{2,1,0:T(8,128)(2,1)S(1)}, bf16[2,128,256]{2,1,0:T(8,128)(2,1)S(1)}, u32[]{:S(2)}, u32[]{:S(2)}) %collective-permute-start.6) | collective-permute-done | bytes 131104 | tf_op jit(solution)/shard_map/ppermute | solution.py:457
  115.2 0.1 collective-permute-start.9
  115.3 1.3 %collective-permute-done.9.got = bf16[2,128,256]{2,1,0:T(8,128)(2,1)S(1)} collective-permute-done((bf16[2,128,256]{2,1,0:T(8,128)(2,1)S(1)}, bf16[2,128,256]{2,1,0:T(8,128)(2,1)S(1)}, u32[]{:S(2)}, u32[]{:S(2)}) %collective-permute-start.9) | collective-permute-done | bytes 131104 | tf_op jit(solution)/shard_map/ppermute | solution.py:469
  116.7 0.0 collective-permute-done.4.dq_got
  116.7 0.9 shard_map.98
  117.6 0.0 all-to-all-done.1.got
  117.6 0.8 weight_sum.1
  (9 shorter events, 0.2 us)
Async XLA Ops:
  35.0 1.8 %copy-start.6 = (bf16[1,128,512]{2,1,0:T(8,128)(2,1)S(1)}, bf16[1,128,512]{2,1,0:T(8,128)(2,1)}, u32[]{:S(2)}) copy-start(bf16[1,128,512]{2,1,0:T(8,128)(2,1)} %param.8) | copy-start | bytes 393220
  35.0 1.8 %copy-start.7 = (bf16[1,128,512]{2,1,0:T(8,128)(2,1)S(1)}, bf16[1,128,512]{2,1,0:T(8,128)(2,1)}, u32[]{:S(2)}) copy-start(bf16[1,128,512]{2,1,0:T(8,128)(2,1)} %param.7) | copy-start | bytes 393220
  35.0 49.2 %collective-permute-start.10 = (bf16[4,4,128,512]{3,2,1,0:T(8,128)(2,1)S(1)}, bf16[4,4,128,512]{3,2,1,0:T(8,128)(2,1)}, u32[]{:S(2)}, u32[]{:S(2)}) collective-permute-start(bf16[4,4,128,512]{3,2,1,0:T(8,128)(2,1)S(1)} %all_to_all.10.x), channel_id=1, source_target_pairs={{0,1},{1,0},{2,3},{3,2},{4,5},{5,4},{6,7},{7,6},{8,9},{9,8},{10,11... | collective-permute-start | bytes 6291464 | tf_op jit(solution)/shard_map/ppermute | solution.py:449
  35.0 22.3 %copy-start.5 = (s32[1,8]{1,0:T(1,128)S(1)}, s32[1,8]{1,0:T(1,128)}, u32[]{:S(2)}) copy-start(s32[1,8]{1,0:T(1,128)} %lengths.3) | copy-start | bytes 100
  36.3 21.1 %collective-permute-start = (bf16[2,128,2048]{2,1,0:T(8,128)(2,1)S(1)}, bf16[2,128,2048]{2,1,0:T(8,128)(2,1)}, u32[]{:S(2)}, u32[]{:S(2)}) collective-permute-start(bf16[2,128,2048]{2,1,0:T(8,128)(2,1)S(1)} %shard_map.93), channel_id=1, source_target_pairs={{0,1},{1,0},{2,3},{3,2},{4,5},{5,4},{6,7},{7,6},{8,9},{9,8},{10,11... | collective-permute-start | bytes 3145736 | tf_op jit(solution)/shard_map/ppermute | solution.py:446
  36.9 4.0 %collective-permute-start.1 = (bf16[2,128,256]{2,1,0:T(8,128)(2,1)S(1)}, bf16[2,128,256]{2,1,0:T(8,128)(2,1)S(1)}, u32[]{:S(2)}, u32[]{:S(2)}) collective-permute-start(bf16[2,128,256]{2,1,0:T(8,128)(2,1)S(1)} %pad_maximum_fusion.1), channel_id=1, source_target_pairs={{0,1},{1,0},{2,3},{3,2},{4,5},{5,4},{6,7},{7,6},{8,9},{9,8},{10,11... | collective-permute-start | bytes 393224 | tf_op jit(solution)/shard_map/ppermute | solution.py:442
  40.9 20.8 %copy-start = (bf16[2,2,128,256]{3,2,1,0:T(8,128)(2,1)}, bf16[2,2,128,256]{3,2,1,0:T(8,128)(2,1)S(1)}, u32[]{:S(2)}) copy-start(bf16[2,2,128,256]{3,2,1,0:T(8,128)(2,1)S(1)} %pad_maximum_fusion.kv_here) | copy-start | bytes 786436
  40.9 11.7 %collective-permute-start.2 = (bf16[2,2,128,256]{3,2,1,0:T(8,128)(2,1)S(1)}, bf16[2,2,128,256]{3,2,1,0:T(8,128)(2,1)S(1)}, u32[]{:S(2)}, u32[]{:S(2)}) collective-permute-start(bf16[2,2,128,256]{3,2,1,0:T(8,128)(2,1)S(1)} %pad_maximum_fusion.kv_here), channel_id=1, source_target_pairs={{0,4},{2,6},{1,5},{3,7},{8,12},{10,14},{9,13},{11,15},{16,20},{18,... | collective-permute-start | bytes 786440 | tf_op jit(solution)/shard_map/ppermute | solution.py:443
  45.9 11.5 %collective-permute-start.3 = (bf16[2,2,128,256]{3,2,1,0:T(8,128)(2,1)S(1)}, bf16[2,2,128,256]{3,2,1,0:T(8,128)(2,1)S(1)}, u32[]{:S(2)}, u32[]{:S(2)}) collective-permute-start(bf16[2,2,128,256]{3,2,1,0:T(8,128)(2,1)S(1)} %pad_maximum_fusion.kv_here), channel_id=1, source_target_pairs={{0,2},{2,4},{4,6},{1,3},{3,5},{5,7},{8,10},{10,12},{12,14},{9,11},... | collective-permute-start | bytes 786440 | tf_op jit(solution)/shard_map/ppermute | solution.py:444
  52.6 9.1 %copy-start.1 = (bf16[2,2,128,256]{3,2,1,0:T(8,128)(2,1)}, bf16[2,2,128,256]{3,2,1,0:T(8,128)(2,1)S(1)}, u32[]{:S(2)}) copy-start(bf16[2,2,128,256]{3,2,1,0:T(8,128)(2,1)S(1)} %collective-permute-done.2.kv_two) | copy-start | bytes 786436
  57.4 4.3 %copy-start.3 = (bf16[2,2,128,256]{3,2,1,0:T(8,128)(2,1)}, bf16[2,2,128,256]{3,2,1,0:T(8,128)(2,1)S(1)}, u32[]{:S(2)}) copy-start(bf16[2,2,128,256]{3,2,1,0:T(8,128)(2,1)S(1)} %collective-permute-done.3.kv_one) | copy-start | bytes 786436
  61.7 9.2 %collective-permute-start.7 = (bf16[2,128,256]{2,1,0:T(8,128)(2,1)S(1)}, bf16[2,128,256]{2,1,0:T(8,128)(2,1)S(1)}, u32[]{:S(2)}, u32[]{:S(2)}) collective-permute-start(bf16[2,128,256]{2,1,0:T(8,128)(2,1)S(1)} %get-tuple-element.25), channel_id=1, source_target_pairs={{2,0},{4,2},{6,4},{3,1},{5,3},{7,5},{10,8},{12,10},{14,12},{11,9},... | collective-permute-start | bytes 393224 | tf_op jit(solution)/shard_map/ppermute | solution.py:456
  63.0 11.4 %collective-permute-start.8 = (bf16[2,128,256]{2,1,0:T(8,128)(2,1)S(1)}, bf16[2,128,256]{2,1,0:T(8,128)(2,1)S(1)}, u32[]{:S(2)}, u32[]{:S(2)}) collective-permute-start(bf16[2,128,256]{2,1,0:T(8,128)(2,1)S(1)} %get-tuple-element.26), channel_id=1, source_target_pairs={{4,0},{6,2},{5,1},{7,3},{12,8},{14,10},{13,9},{15,11},{20,16},{22,... | collective-permute-start | bytes 393224 | tf_op jit(solution)/shard_map/ppermute | solution.py:457
  74.4 8.3 %collective-permute-start.11 = (bf16[2,128,256]{2,1,0:T(8,128)(2,1)S(1)}, bf16[2,128,256]{2,1,0:T(8,128)(2,1)S(1)}, u32[]{:S(2)}, u32[]{:S(2)}) collective-permute-start(bf16[2,128,256]{2,1,0:T(8,128)(2,1)S(1)} %shard_map.97.dv.refs_0_), channel_id=1, source_target_pairs={{0,8},{8,16},{16,24},{24,0},{1,9},{9,17},{17,25},{25,1},{2,10},{10... | collective-permute-start | bytes 393224 | tf_op jit(solution)/shard_map/ppermute | solution.py:462
  75.1 7.7 %collective-permute-start.12 = (bf16[2,128,256]{2,1,0:T(8,128)(2,1)S(1)}, bf16[2,128,256]{2,1,0:T(8,128)(2,1)S(1)}, u32[]{:S(2)}, u32[]{:S(2)}) collective-permute-start(bf16[2,128,256]{2,1,0:T(8,128)(2,1)S(1)} %shard_map.97.dv.refs_0_), channel_id=1, source_target_pairs={{0,16},{8,24},{16,0},{24,8},{1,17},{9,25},{17,1},{25,9},{2,18},{10... | collective-permute-start | bytes 393224 | tf_op jit(solution)/shard_map/ppermute | solution.py:462
  77.1 6.3 %collective-permute-start.13 = (bf16[2,128,256]{2,1,0:T(8,128)(2,1)S(1)}, bf16[2,128,256]{2,1,0:T(8,128)(2,1)S(1)}, u32[]{:S(2)}, u32[]{:S(2)}) collective-permute-start(bf16[2,128,256]{2,1,0:T(8,128)(2,1)S(1)} %shard_map.97.dv.refs_0_), channel_id=1, source_target_pairs={{0,24},{8,0},{16,8},{24,16},{1,25},{9,1},{17,9},{25,17},{2,26},{10... | collective-permute-start | bytes 393224 | tf_op jit(solution)/shard_map/ppermute | solution.py:462
  87.5 7.4 %copy-start.2 = (bf16[2,2,128,256]{3,2,1,0:T(8,128)(2,1)S(1)}, bf16[2,2,128,256]{3,2,1,0:T(8,128)(2,1)}, u32[]{:S(2)}) copy-start(bf16[2,2,128,256]{3,2,1,0:T(8,128)(2,1)} %copy-done.1) | copy-start | bytes 786436
  87.5 7.4 %copy-start.4 = (bf16[2,2,128,256]{3,2,1,0:T(8,128)(2,1)S(1)}, bf16[2,2,128,256]{3,2,1,0:T(8,128)(2,1)}, u32[]{:S(2)}) copy-start(bf16[2,2,128,256]{3,2,1,0:T(8,128)(2,1)} %copy-done.3) | copy-start | bytes 786436
  87.5 30.1 %all-to-all-start.1 = ((bf16[32,64,256]{2,1,0:T(8,128)(2,1)}), bf16[32,64,256]{2,1,0:T(8,128)(2,1)S(1)}, u32[]{:S(2)}, u32[]{:S(2)}) async-start(bf16[32,64,256]{2,1,0:T(8,128)(2,1)} %bitcast.8), calls=%async_computation.1 | async-start | bytes 2097152 | tf_op jit(solution)/shard_map/all_to_all | solution.py:429
  100.8 15.9 %collective-permute-start.4 = (bf16[128,2048]{1,0:T(8,128)(2,1)}, bf16[128,2048]{1,0:T(8,128)(2,1)S(1)}, u32[]{:S(2)}, u32[]{:S(2)}) collective-permute-start(bf16[128,2048]{1,0:T(8,128)(2,1)} %get-tuple-element.20), channel_id=1, source_target_pairs={{0,1},{1,0},{2,3},{3,2},{4,5},{5,4},{6,7},{7,6},{8,9},{9,8},{10,11... | collective-permute-start | bytes 1572872 | tf_op jit(solution)/shard_map/ppermute | solution.py:468
  101.2 10.9 %collective-permute-start.5 = (bf16[2,128,256]{2,1,0:T(8,128)(2,1)S(1)}, bf16[2,128,256]{2,1,0:T(8,128)(2,1)S(1)}, u32[]{:S(2)}, u32[]{:S(2)}) collective-permute-start(bf16[2,128,256]{2,1,0:T(8,128)(2,1)S(1)} %get-tuple-element.22), channel_id=1, source_target_pairs={{2,0},{4,2},{6,4},{3,1},{5,3},{7,5},{10,8},{12,10},{14,12},{11,9},... | collective-permute-start | bytes 393224 | tf_op jit(solution)/shard_map/ppermute | solution.py:456
  102.4 12.7 %collective-permute-start.6 = (bf16[2,128,256]{2,1,0:T(8,128)(2,1)S(1)}, bf16[2,128,256]{2,1,0:T(8,128)(2,1)S(1)}, u32[]{:S(2)}, u32[]{:S(2)}) collective-permute-start(bf16[2,128,256]{2,1,0:T(8,128)(2,1)S(1)} %get-tuple-element.23), channel_id=1, source_target_pairs={{4,0},{6,2},{5,1},{7,3},{12,8},{14,10},{13,9},{15,11},{20,16},{22,... | collective-permute-start | bytes 393224 | tf_op jit(solution)/shard_map/ppermute | solution.py:457
  115.2 1.4 %collective-permute-start.9 = (bf16[2,128,256]{2,1,0:T(8,128)(2,1)S(1)}, bf16[2,128,256]{2,1,0:T(8,128)(2,1)S(1)}, u32[]{:S(2)}, u32[]{:S(2)}) collective-permute-start(bf16[2,128,256]{2,1,0:T(8,128)(2,1)S(1)} %pad_maximum_fusion.2), channel_id=1, source_target_pairs={{0,1},{1,0},{2,3},{3,2},{4,5},{5,4},{6,7},{7,6},{8,9},{9,8},{10,11... | collective-permute-start | bytes 393224 | tf_op jit(solution)/shard_map/ppermute | solution.py:469

commit v6 on v5

--- a/solution.py
+++ b/solution.py
@@ -171,12 +171,12 @@
     return group, 1 - rest // PAIRS, rest % PAIRS
 
 
-def load_own(core, q_hbm, do_hbm, own, sems):
+def start_loads(core, q_hbm, do_hbm, oth_hbm, kv_hbm, own, oth, kv, sems):
     cols = lanes(core * HALF, HALF)
-    copies = [
-        pltpu.make_async_copy(ref.at[:, cols], own.at[i], sems.at[i])
-        for i, ref in enumerate((q_hbm, do_hbm))
-    ]
+    moves = [(ref, kv.at[i]) for i, ref in enumerate(kv_hbm)]
+    moves += [(oth_hbm.at[i], oth.at[i]) for i in range(2)]
+    moves += [(ref.at[:, cols], own.at[i]) for i, ref in enumerate((q_hbm, do_hbm))]
+    copies = [pltpu.make_async_copy(a, b, sems.at[i]) for i, (a, b) in enumerate(moves)]
     for copy in copies:
         copy.start()
     return copies
@@ -230,15 +230,20 @@
 
 
 def probs_kernel(
-    lengths, q_hbm, do_hbm, others, kv_two, kv_one, kv_here,
+    lengths, q_hbm, do_hbm, oth_hbm, kv_two, kv_one, kv_here,
     dv_two, dv_one, dv_here, stat_ref, bias_ref,
-    k_buf, dv_acc, own, sems,
+    k_buf, dv_acc, own, others, kv, sems,
 ):
     chip, core = lax.axis_index("x"), lax.axis_index("core")
-    loads = load_own(core, q_hbm, do_hbm, own, sems)
+    loads = start_loads(
+        core, q_hbm, do_hbm, oth_hbm, (kv_two, kv_one, kv_here), own, others, kv, sems
+    )
+    dv_acc[...] = jnp.zeros_like(dv_acc)
+    for load in loads[:5]:
+        load.wait()
+    loads = loads[5:]
     for group in range(2):
-        gather_keys(core, (kv_two, kv_one, kv_here), 0, group, k_buf)
-    dv_acc[...] = jnp.zeros_like(dv_acc)
+        gather_keys(core, [kv.at[i] for i in range(3)], 0, group, k_buf)
     for small in (True, False):
         @pl.when((chip == 0) == small)
         def _():
@@ -283,22 +288,28 @@
 
 
 def scores_kernel(
-    lengths, q_hbm, do_hbm, others, kv_two, kv_one, kv_here, stat_ref, bias_ref,
+    lengths, q_hbm, do_hbm, oth_hbm, kv_two, kv_one, kv_here, stat_ref, bias_ref,
     dq_hbm, sent_hbm, dk_two, dk_one, dk_here,
-    k_buf, v_buf, k_t, dk_acc, own, sems, dq_buf, out_sems,
+    k_buf, v_buf, k_t, dk_acc, own, others, kv, sems, dq_buf, out_sems,
 ):
     chip, core = lax.axis_index("x"), lax.axis_index("core")
-    loads = load_own(core, q_hbm, do_hbm, own, sems)
+    loads = start_loads(
+        core, q_hbm, do_hbm, oth_hbm, (kv_two, kv_one, kv_here), own, others, kv, sems
+    )
     targets = (dq_hbm.at[:, lanes(core * HALF, HALF)], sent_hbm)
     stores = [
         pltpu.make_async_copy(dq_buf.at[side], target, out_sems.at[side])
         for side, target in enumerate(targets)
     ]
+    dk_acc[...] = jnp.zeros_like(dk_acc)
+    for load in loads[:5]:
+        load.wait()
+    loads = loads[5:]
+    parts = [kv.at[i] for i in range(3)]
     for group in range(2):
-        gather_keys(core, (kv_two, kv_one, kv_here), 0, group, k_buf)
-        gather_keys(core, (kv_two, kv_one, kv_here), 1, group, v_buf)
+        gather_keys(core, parts, 0, group, k_buf)
+        gather_keys(core, parts, 1, group, v_buf)
         k_t[group] = k_buf[group].reshape(SPAN * BLK, HD).T
-    dk_acc[...] = jnp.zeros_like(dk_acc)
     for small in (True, False):
         @pl.when((chip == 0) == small)
         def _():
@@ -317,25 +328,27 @@
 KEYS = pltpu.VMEM((2, SPAN, BLK, HD), BF16)
 TURNED = pltpu.VMEM((2, HD, SPAN * BLK), BF16)
 TOTAL = pltpu.VMEM((2, SPAN * BLK, HD), F32)
-OWN = [pltpu.VMEM((2, BLK, HALF), BF16), pltpu.SemaphoreType.DMA((2,))]
+ROWS = pltpu.VMEM((2, BLK, HALF), BF16)
+OWN = [ROWS, ROWS, pltpu.VMEM((3, 2, 2, BLK, COLS), BF16), pltpu.SemaphoreType.DMA((7,))]
 PRODUCT = 2 * 16 * 2 * BLK * WIN * BLK * HD
-OPERANDS = [IN_SMEM, IN_HBM, IN_HBM] + [IN_VMEM] * 4
+OPERANDS = [IN_SMEM] + [IN_HBM] * 6
 
 
 def attention_probs(operands):
     stats = pltpu.VMEM((2, STEPS, 2 * BLK), F32)
     bias = pltpu.VMEM((2, WIN * BLK, BLK), F32)
     return call(
-        probs_kernel, OPERANDS, PARTS + [stats, bias], operands,
+        probs_kernel, OPERANDS[:4] + [IN_VMEM] + OPERANDS[5:],
+        PARTS + [stats, bias], operands,
         [KEYS, TOTAL] + OWN, flops=2 * PRODUCT, exps=PRODUCT // 256, moved=4 << 20, room=16,
     )
 
 
 def attention_scores(operands, stats, bias):
     return call(
-        scores_kernel, OPERANDS[:3] + [ANYWHERE] * 4 + [IN_VMEM] * 2,
+        scores_kernel, OPERANDS + [IN_VMEM] * 2,
         [pltpu.HBM((BLK, width), BF16) for width in (2 * HALF, HALF)] + PARTS,
-        [*operands[:-1], far(operands[-1]), stats, bias],
+        [*operands, stats, bias],
         [KEYS, KEYS, TURNED, TOTAL] + OWN
         + [pltpu.VMEM((2, BLK, HALF), BF16), pltpu.SemaphoreType.DMA((2,))],
         flops=4 * PRODUCT, exps=PRODUCT // 256, moved=4 << 20, room=16,
@@ -440,8 +453,8 @@
     kv_keep = pairs(key_states[0], value_states[0], core, COLS)
     kv_send = pairs(key_states[0], value_states[0], 1 - core, COLS)
     kv_here = jnp.stack([kv_keep, lax.ppermute(kv_send, "core", SWAP)])
-    kv_two = lax.ppermute(kv_here, "x", [(0, 2), (1, 3)])
     kv_one = lax.ppermute(kv_here, "x", [(0, 1), (1, 2), (2, 3)])
+    kv_two = lax.ppermute(kv_one, "x", [(1, 2), (2, 3)])
 
     others = lax.ppermute(other_heads(queries, out_grad), "core", SWAP)
 

time: 120 us -> 121 us (level)
  waiting for transfers between devices: 41.1 us -> 46 us
  starting transfers between devices: 24.6 us -> 20.1 us
    ppermute x2, waiting for transfers between devices: 14.9 us -> 23 us  [summed(): one = lax.ppermute(one, 'x', [(1, 0), (2, 1), (3, 2)])]
    ppermute x1, starting transfers between devices: 4.94 us -> 0.67 us  [shards(): kv_two = lax.ppermute(kv_one, 'x', [(1, 2), (2, 3)])]
    ppermute x1, waiting for transfers between devices: 4.18 us -> 0.01 us  [shards(): kv_two = lax.ppermute(kv_one, 'x', [(1, 2), (2, 3)])]
  transfers between devices with their start and end apart: 15 -> 15, of which waited for: 10 -> 9; matrix products, arithmetic and copies ran while one was open for 0% -> 0% of each run, Pallas kernels for 11% -> 12%
where the time goes in v6:
time: 121 us; the launch traced here: 120 us
  waiting for transfers between devices  46 us (38%)
  blocking collectives  31.8 us (26%)
  Pallas kernels  20.7 us (17%)
  starting transfers between devices  20.1 us (17%)
    all_to_all x1, blocking collectives, exchange(): return lax.all_to_all(value, axes, 0, 0, tiled=True)  31.8 us
    ppermute x2, waiting for transfers between devices, summed(): one = lax.ppermute(one, 'x', [(1, 0), (2, 1), (3, 2)])  23 us
    pallas_call x9, Pallas kernels, call(): pl.pallas_call(kernel, in_specs=list(in_specs), out_specs=out_specs, out_...  19.9 us
    ppermute x2, waiting for transfers between devices, summed(): two = lax.ppermute(two, 'x', [(2, 0), (3, 1)])  6.91 us
    all_to_all x1, starting transfers between devices, exchange(): return lax.all_to_all(value, axes, 0, 0, tiled=True)  6.22 us
    ppermute x1, waiting for transfers between devices, shards(): kv_one = lax.ppermute(kv_here, 'x', [(0, 1), (1, 2), (2, 3)])  5.83 us
    ppermute x3, waiting for transfers between devices, shards(): lax.ppermute(dv, 'z', [(i, (i + away) % 4) for i in range(4)])  5.03 us
    ppermute x1, waiting for transfers between devices, shards(): kv_here = jnp.stack([kv_keep, lax.ppermute(kv_send, 'core', SWAP)])  3.82 us
  transfers between devices with their start and end apart: 15, of which 9 were waited for; matrix products, arithmetic and copies ran while one was open for 0% of the time, Pallas kernels for 12%

profile of v6, /device:TPU:0, one launch (start us, length us, event | category | flops | bytes accessed | tf_op | source)
XLA Modules:
  0.0 119.5 jit_solution(11630848220357738754)
XLA Ops:
  0.6 2.6 %shard_map.99 = bf16[4,4,128,512]{3,2,1,0:T(8,128)(2,1)} custom-call(bf16[128,8192]{1,0:T(8,128)(2,1)} %bitcast.10), custom_call_target="tpu_custom_call" | custom-call | bytes 4194304 | tf_op jit(solution)/shard_map/pallas_call | solution.py:62
  3.3 31.8 %all_to_all.10.x = bf16[4,4,128,512]{3,2,1,0:T(8,128)(2,1)S(1)} all-to-all(bf16[4,4,128,512]{3,2,1,0:T(8,128)(2,1)} %shard_map.99), channel_id=1, replica_groups=mesh['y'=4,'z'=4,'x'=4,'core'=2] {'z'}, dimensions={0} | all-to-all | bytes 4194304 | tf_op jit(solution)/shard_map/all_to_all | solution.py:442
  35.0 0.0 copy-start.3
  35.0 0.0 copy-start.4
  35.0 0.0 collective-permute-start.10
  35.0 0.0 copy-start.1
  35.0 1.3 %shard_map.93 = bf16[2,128,2048]{2,1,0:T(8,128)(2,1)S(1)} custom-call(bf16[128,4096]{1,0:T(8,128)(2,1)} %bitcast.11, bf16[128,4096]{1,0:T(8,128)(2,1)} %bitcast.14), custom_call_target="tpu_custom_call" | custom-call | bytes 1048576 | tf_op jit(solution)/shard_map/pallas_call | solution.py:62
  36.3 0.5 collective-permute-start
  36.9 0.0 copy-done.3
  36.9 0.0 copy-done.4
  36.9 0.1 collective-permute-start.1
  37.1 3.8 %collective-permute-done.1 = bf16[2,128,256]{2,1,0:T(8,128)(2,1)S(1)} collective-permute-done((bf16[2,128,256]{2,1,0:T(8,128)(2,1)S(1)}, bf16[2,128,256]{2,1,0:T(8,128)(2,1)S(1)}, u32[]{:S(2)}, u32[]{:S(2)}) %collective-permute-start.1) | collective-permute-done | bytes 131104 | tf_op jit(solution)/shard_map/ppermute | solution.py:455
  40.9 0.0 copy-start.2
  40.9 3.4 %collective-permute-start.2 = (bf16[2,2,128,256]{3,2,1,0:T(8,128)(2,1)S(1)}, bf16[2,2,128,256]{3,2,1,0:T(8,128)(2,1)S(1)}, u32[]{:S(2)}, u32[]{:S(2)}) collective-permute-start(bf16[2,2,128,256]{3,2,1,0:T(8,128)(2,1)S(1)} %pad_maximum_fusion.kv_here), channel_id=1, source_target_pairs={{0,2},{2,4},{4,6},{1,3},{3,5},{5,7},{8,10},{10,12},{12,14},{9,11},... | collective-permute-start | bytes 786440 | tf_op jit(solution)/shard_map/ppermute | solution.py:456
  44.3 5.8 %collective-permute-done.2.kv_one = bf16[2,2,128,256]{3,2,1,0:T(8,128)(2,1)S(1)} collective-permute-done((bf16[2,2,128,256]{3,2,1,0:T(8,128)(2,1)S(1)}, bf16[2,2,128,256]{3,2,1,0:T(8,128)(2,1)S(1)}, u32[]{:S(2)}, u32[]{:S(2)}) %collective-permute-start.2) | collective-permute-done | bytes 262176 | tf_op jit(solution)/shard_map/ppermute | solution.py:456
  50.2 0.0 copy-start.5
  50.2 0.7 collective-permute-start.3
  50.8 0.0 collective-permute-done.3.kv_two
  50.9 0.0 copy-start
  50.9 0.0 collective-permute-done.oth_hbm
  50.9 0.0 copy-done.2
  50.9 0.0 copy-done.5
  50.9 0.0 copy-done.1
  50.9 4.4 %shard_map.94 = (bf16[2,128,256]{2,1,0:T(8,128)(2,1)S(1)}, bf16[2,128,256]{2,1,0:T(8,128)(2,1)S(1)}, f32[2,128,256]{2,1,0:T(8,128)S(1)}, f32[2,16,256]{2,1,0:T(8,128)S(1)}, f32[2,640,128]{2,1,0:T(8,128)S(1)}) custom-call(s32[1,8]{1,0:T(1,128)S(1)} %copy-done.1, bf16[128,4096]{1,0:T(8,128)(2,1)} %bitcast.12, bf16[128,4096]{1,0:T(8,128)(2,1)} %bitcast.15, ...), custom_call_target="tpu_custom_call" | custom-call | flops 1342177280 | bytes 4194304 | tf_op jit(solution)/shard_map/pallas_call | solution.py:62
  55.3 0.0 copy-done
  55.3 1.3 %collective-permute-start.7 = (bf16[2,128,256]{2,1,0:T(8,128)(2,1)S(1)}, bf16[2,128,256]{2,1,0:T(8,128)(2,1)S(1)}, u32[]{:S(2)}, u32[]{:S(2)}) collective-permute-start(bf16[2,128,256]{2,1,0:T(8,128)(2,1)S(1)} %get-tuple-element.25), channel_id=1, source_target_pairs={{2,0},{4,2},{6,4},{3,1},{5,3},{7,5},{10,8},{12,10},{14,12},{11,9},... | collective-permute-start | bytes 393224 | tf_op jit(solution)/shard_map/ppermute | solution.py:469
  56.6 1.3 %collective-permute-start.8 = (bf16[2,128,256]{2,1,0:T(8,128)(2,1)S(1)}, bf16[2,128,256]{2,1,0:T(8,128)(2,1)S(1)}, u32[]{:S(2)}, u32[]{:S(2)}) collective-permute-start(bf16[2,128,256]{2,1,0:T(8,128)(2,1)S(1)} %get-tuple-element.26), channel_id=1, source_target_pairs={{4,0},{6,2},{5,1},{7,3},{12,8},{14,10},{13,9},{15,11},{20,16},{22,... | collective-permute-start | bytes 393224 | tf_op jit(solution)/shard_map/ppermute | solution.py:470
  57.9 14.7 %collective-permute-done.7.one = bf16[2,128,256]{2,1,0:T(8,128)(2,1)S(1)} collective-permute-done((bf16[2,128,256]{2,1,0:T(8,128)(2,1)S(1)}, bf16[2,128,256]{2,1,0:T(8,128)(2,1)S(1)}, u32[]{:S(2)}, u32[]{:S(2)}) %collective-permute-start.7) | collective-permute-done | bytes 131104 | tf_op jit(solution)/shard_map/ppermute | solution.py:469
  72.6 3.8 %collective-permute-done.8.two = bf16[2,128,256]{2,1,0:T(8,128)(2,1)S(1)} collective-permute-done((bf16[2,128,256]{2,1,0:T(8,128)(2,1)S(1)}, bf16[2,128,256]{2,1,0:T(8,128)(2,1)S(1)}, u32[]{:S(2)}, u32[]{:S(2)}) %collective-permute-start.8) | collective-permute-done | bytes 131104 | tf_op jit(solution)/shard_map/ppermute | solution.py:470
  76.4 0.6 collective-permute-start.11
  77.1 2.1 %collective-permute-start.12 = (bf16[2,128,256]{2,1,0:T(8,128)(2,1)S(1)}, bf16[2,128,256]{2,1,0:T(8,128)(2,1)S(1)}, u32[]{:S(2)}, u32[]{:S(2)}) collective-permute-start(bf16[2,128,256]{2,1,0:T(8,128)(2,1)S(1)} %shard_map.97.dv.refs_0_), channel_id=1, source_target_pairs={{0,16},{8,24},{16,0},{24,8},{1,17},{9,25},{17,1},{25,9},{2,18},{10... | collective-permute-start | bytes 393224 | tf_op jit(solution)/shard_map/ppermute | solution.py:475
  79.1 0.8 collective-permute-start.13
  80.0 4.1 %collective-permute-done.11.refs_1_ = bf16[2,128,256]{2,1,0:T(8,128)(2,1)S(1)} collective-permute-done((bf16[2,128,256]{2,1,0:T(8,128)(2,1)S(1)}, bf16[2,128,256]{2,1,0:T(8,128)(2,1)S(1)}, u32[]{:S(2)}, u32[]{:S(2)}) %collective-permute-start.11) | collective-permute-done | bytes 131104 | tf_op jit(solution)/shard_map/ppermute | solution.py:475
  84.1 0.0 collective-permute-done.12.refs_2_
  84.1 0.9 collective-permute-done.13.refs_3_
  85.0 0.8 shard_map.100.past
  85.8 0.0 collective-permute-done.10.x
  85.8 3.4 %shard_map.101 = bf16[2048,256]{1,0:T(8,128)(2,1)} custom-call(bf16[4,4,128,512]{3,2,1,0:T(8,128)(2,1)} %collective-permute-done.10.x, f32[2048,256]{1,0:T(8,128)S(1)} %shard_map.100.past, bf16[2,128,256]{2,1,0:T(8,128)(2,1)S(1)} %shard_map.97.dv.refs_0_, bf16[2,128,256]{2,1,0:T(8,128)(2,1)S(1)} %collective-permute-done.11.refs_1_, ...), custom_call_target="tpu_custom_call" | custom-call | flops 536870912 | bytes 4194304 | tf_op jit(solution)/shard_map/pallas_call | solution.py:62
  89.1 6.2 %all-to-all-start.1 = ((bf16[32,64,256]{2,1,0:T(8,128)(2,1)}), bf16[32,64,256]{2,1,0:T(8,128)(2,1)S(1)}, u32[]{:S(2)}, u32[]{:S(2)}) async-start(bf16[32,64,256]{2,1,0:T(8,128)(2,1)} %bitcast.8), calls=%async_computation.1 | async-start | bytes 2097152 | tf_op jit(solution)/shard_map/all_to_all | solution.py:442
  95.4 6.5 %shard_map.95 = (bf16[128,4096]{1,0:T(8,128)(2,1)}, bf16[128,2048]{1,0:T(8,128)(2,1)}, bf16[2,128,256]{2,1,0:T(8,128)(2,1)S(1)}, bf16[2,128,256]{2,1,0:T(8,128)(2,1)S(1)}, f32[2,128,256]{2,1,0:T(8,128)S(1)}) custom-call(s32[1,8]{1,0:T(1,128)S(1)} %copy-done.1, bf16[128,4096]{1,0:T(8,128)(2,1)} %bitcast.13, bf16[128,4096]{1,0:T(8,128)(2,1)} %bitcast.16, ...), custom_call_target="tpu_custom_call" | custom-call | flops 2684354560 | bytes 4194304 | tf_op jit(solution)/shard_map/pallas_call | solution.py:62
  101.9 0.4 collective-permute-start.4
  102.3 1.3 %collective-permute-start.5 = (bf16[2,128,256]{2,1,0:T(8,128)(2,1)S(1)}, bf16[2,128,256]{2,1,0:T(8,128)(2,1)S(1)}, u32[]{:S(2)}, u32[]{:S(2)}) collective-permute-start(bf16[2,128,256]{2,1,0:T(8,128)(2,1)S(1)} %get-tuple-element.22), channel_id=1, source_target_pairs={{2,0},{4,2},{6,4},{3,1},{5,3},{7,5},{10,8},{12,10},{14,12},{11,9},... | collective-permute-start | bytes 393224 | tf_op jit(solution)/shard_map/ppermute | solution.py:469
  103.5 1.3 %collective-permute-start.6 = (bf16[2,128,256]{2,1,0:T(8,128)(2,1)S(1)}, bf16[2,128,256]{2,1,0:T(8,128)(2,1)S(1)}, u32[]{:S(2)}, u32[]{:S(2)}) collective-permute-start(bf16[2,128,256]{2,1,0:T(8,128)(2,1)S(1)} %get-tuple-element.23), channel_id=1, source_target_pairs={{4,0},{6,2},{5,1},{7,3},{12,8},{14,10},{13,9},{15,11},{20,16},{22,... | collective-permute-start | bytes 393224 | tf_op jit(solution)/shard_map/ppermute | solution.py:470
  104.9 8.4 %collective-permute-done.5.one = bf16[2,128,256]{2,1,0:T(8,128)(2,1)S(1)} collective-permute-done((bf16[2,128,256]{2,1,0:T(8,128)(2,1)S(1)}, bf16[2,128,256]{2,1,0:T(8,128)(2,1)S(1)}, u32[]{:S(2)}, u32[]{:S(2)}) %collective-permute-start.5) | collective-permute-done | bytes 131104 | tf_op jit(solution)/shard_map/ppermute | solution.py:469
  113.2 3.1 %collective-permute-done.6.two = bf16[2,128,256]{2,1,0:T(8,128)(2,1)S(1)} collective-permute-done((bf16[2,128,256]{2,1,0:T(8,128)(2,1)S(1)}, bf16[2,128,256]{2,1,0:T(8,128)(2,1)S(1)}, u32[]{:S(2)}, u32[]{:S(2)}) %collective-permute-start.6) | collective-permute-done | bytes 131104 | tf_op jit(solution)/shard_map/ppermute | solution.py:470
  116.4 0.1 collective-permute-start.9
  116.5 1.3 %collective-permute-done.9.got = bf16[2,128,256]{2,1,0:T(8,128)(2,1)S(1)} collective-permute-done((bf16[2,128,256]{2,1,0:T(8,128)(2,1)S(1)}, bf16[2,128,256]{2,1,0:T(8,128)(2,1)S(1)}, u32[]{:S(2)}, u32[]{:S(2)}) %collective-permute-start.9) | collective-permute-done | bytes 131104 | tf_op jit(solution)/shard_map/ppermute | solution.py:482
  117.8 0.0 collective-permute-done.4.dq_got
  117.8 0.9 shard_map.98
  118.7 0.0 all-to-all-done.1.got
  118.7 0.8 weight_sum.1
  (9 shorter events, 0.2 us)
Async XLA Ops:
  35.0 1.8 %copy-start.3 = (bf16[1,128,512]{2,1,0:T(8,128)(2,1)S(1)}, bf16[1,128,512]{2,1,0:T(8,128)(2,1)}, u32[]{:S(2)}) copy-start(bf16[1,128,512]{2,1,0:T(8,128)(2,1)} %param.8) | copy-start | bytes 393220
  35.0 1.8 %copy-start.4 = (bf16[1,128,512]{2,1,0:T(8,128)(2,1)S(1)}, bf16[1,128,512]{2,1,0:T(8,128)(2,1)}, u32[]{:S(2)}) copy-start(bf16[1,128,512]{2,1,0:T(8,128)(2,1)} %param.7) | copy-start | bytes 393220
  35.0 50.7 %collective-permute-start.10 = (bf16[4,4,128,512]{3,2,1,0:T(8,128)(2,1)S(1)}, bf16[4,4,128,512]{3,2,1,0:T(8,128)(2,1)}, u32[]{:S(2)}, u32[]{:S(2)}) collective-permute-start(bf16[4,4,128,512]{3,2,1,0:T(8,128)(2,1)S(1)} %all_to_all.10.x), channel_id=1, source_target_pairs={{0,1},{1,0},{2,3},{3,2},{4,5},{5,4},{6,7},{7,6},{8,9},{9,8},{10,11... | collective-permute-start | bytes 6291464 | tf_op jit(solution)/shard_map/ppermute | solution.py:462
  35.0 15.9 %copy-start.1 = (s32[1,8]{1,0:T(1,128)S(1)}, s32[1,8]{1,0:T(1,128)}, u32[]{:S(2)}) copy-start(s32[1,8]{1,0:T(1,128)} %lengths.3) | copy-start | bytes 100
  36.3 14.6 %collective-permute-start = (bf16[2,128,2048]{2,1,0:T(8,128)(2,1)S(1)}, bf16[2,128,2048]{2,1,0:T(8,128)(2,1)}, u32[]{:S(2)}, u32[]{:S(2)}) collective-permute-start(bf16[2,128,2048]{2,1,0:T(8,128)(2,1)S(1)} %shard_map.93), channel_id=1, source_target_pairs={{0,1},{1,0},{2,3},{3,2},{4,5},{5,4},{6,7},{7,6},{8,9},{9,8},{10,11... | collective-permute-start | bytes 3145736 | tf_op jit(solution)/shard_map/ppermute | solution.py:459
  36.9 4.0 %collective-permute-start.1 = (bf16[2,128,256]{2,1,0:T(8,128)(2,1)S(1)}, bf16[2,128,256]{2,1,0:T(8,128)(2,1)S(1)}, u32[]{:S(2)}, u32[]{:S(2)}) collective-permute-start(bf16[2,128,256]{2,1,0:T(8,128)(2,1)S(1)} %pad_maximum_fusion.1), channel_id=1, source_target_pairs={{0,1},{1,0},{2,3},{3,2},{4,5},{5,4},{6,7},{7,6},{8,9},{9,8},{10,11... | collective-permute-start | bytes 393224 | tf_op jit(solution)/shard_map/ppermute | solution.py:455
  40.9 10.0 %copy-start.2 = (bf16[2,2,128,256]{3,2,1,0:T(8,128)(2,1)}, bf16[2,2,128,256]{3,2,1,0:T(8,128)(2,1)S(1)}, u32[]{:S(2)}) copy-start(bf16[2,2,128,256]{3,2,1,0:T(8,128)(2,1)S(1)} %pad_maximum_fusion.kv_here) | copy-start | bytes 786436
  40.9 9.3 %collective-permute-start.2 = (bf16[2,2,128,256]{3,2,1,0:T(8,128)(2,1)S(1)}, bf16[2,2,128,256]{3,2,1,0:T(8,128)(2,1)S(1)}, u32[]{:S(2)}, u32[]{:S(2)}) collective-permute-start(bf16[2,2,128,256]{3,2,1,0:T(8,128)(2,1)S(1)} %pad_maximum_fusion.kv_here), channel_id=1, source_target_pairs={{0,2},{2,4},{4,6},{1,3},{3,5},{5,7},{8,10},{10,12},{12,14},{9,11},... | collective-permute-start | bytes 786440 | tf_op jit(solution)/shard_map/ppermute | solution.py:456
  50.2 0.7 copy-start.5
  50.2 0.7 collective-permute-start.3
  50.9 4.4 %copy-start = (bf16[2,2,128,256]{3,2,1,0:T(8,128)(2,1)}, bf16[2,2,128,256]{3,2,1,0:T(8,128)(2,1)S(1)}, u32[]{:S(2)}) copy-start(bf16[2,2,128,256]{3,2,1,0:T(8,128)(2,1)S(1)} %collective-permute-done.3.kv_two) | copy-start | bytes 786436
  55.3 17.3 %collective-permute-start.7 = (bf16[2,128,256]{2,1,0:T(8,128)(2,1)S(1)}, bf16[2,128,256]{2,1,0:T(8,128)(2,1)S(1)}, u32[]{:S(2)}, u32[]{:S(2)}) collective-permute-start(bf16[2,128,256]{2,1,0:T(8,128)(2,1)S(1)} %get-tuple-element.25), channel_id=1, source_target_pairs={{2,0},{4,2},{6,4},{3,1},{5,3},{7,5},{10,8},{12,10},{14,12},{11,9},... | collective-permute-start | bytes 393224 | tf_op jit(solution)/shard_map/ppermute | solution.py:469
  56.6 19.8 %collective-permute-start.8 = (bf16[2,128,256]{2,1,0:T(8,128)(2,1)S(1)}, bf16[2,128,256]{2,1,0:T(8,128)(2,1)S(1)}, u32[]{:S(2)}, u32[]{:S(2)}) collective-permute-start(bf16[2,128,256]{2,1,0:T(8,128)(2,1)S(1)} %get-tuple-element.26), channel_id=1, source_target_pairs={{4,0},{6,2},{5,1},{7,3},{12,8},{14,10},{13,9},{15,11},{20,16},{22,... | collective-permute-start | bytes 393224 | tf_op jit(solution)/shard_map/ppermute | solution.py:470
  76.4 7.7 %collective-permute-start.11 = (bf16[2,128,256]{2,1,0:T(8,128)(2,1)S(1)}, bf16[2,128,256]{2,1,0:T(8,128)(2,1)S(1)}, u32[]{:S(2)}, u32[]{:S(2)}) collective-permute-start(bf16[2,128,256]{2,1,0:T(8,128)(2,1)S(1)} %shard_map.97.dv.refs_0_), channel_id=1, source_target_pairs={{0,8},{8,16},{16,24},{24,0},{1,9},{9,17},{17,25},{25,1},{2,10},{10... | collective-permute-start | bytes 393224 | tf_op jit(solution)/shard_map/ppermute | solution.py:475
  77.1 7.0 %collective-permute-start.12 = (bf16[2,128,256]{2,1,0:T(8,128)(2,1)S(1)}, bf16[2,128,256]{2,1,0:T(8,128)(2,1)S(1)}, u32[]{:S(2)}, u32[]{:S(2)}) collective-permute-start(bf16[2,128,256]{2,1,0:T(8,128)(2,1)S(1)} %shard_map.97.dv.refs_0_), channel_id=1, source_target_pairs={{0,16},{8,24},{16,0},{24,8},{1,17},{9,25},{17,1},{25,9},{2,18},{10... | collective-permute-start | bytes 393224 | tf_op jit(solution)/shard_map/ppermute | solution.py:475
  79.1 5.9 %collective-permute-start.13 = (bf16[2,128,256]{2,1,0:T(8,128)(2,1)S(1)}, bf16[2,128,256]{2,1,0:T(8,128)(2,1)S(1)}, u32[]{:S(2)}, u32[]{:S(2)}) collective-permute-start(bf16[2,128,256]{2,1,0:T(8,128)(2,1)S(1)} %shard_map.97.dv.refs_0_), channel_id=1, source_target_pairs={{0,24},{8,0},{16,8},{24,16},{1,25},{9,1},{17,9},{25,17},{2,26},{10... | collective-permute-start | bytes 393224 | tf_op jit(solution)/shard_map/ppermute | solution.py:475
  89.1 29.6 %all-to-all-start.1 = ((bf16[32,64,256]{2,1,0:T(8,128)(2,1)}), bf16[32,64,256]{2,1,0:T(8,128)(2,1)S(1)}, u32[]{:S(2)}, u32[]{:S(2)}) async-start(bf16[32,64,256]{2,1,0:T(8,128)(2,1)} %bitcast.8), calls=%async_computation.1 | async-start | bytes 2097152 | tf_op jit(solution)/shard_map/all_to_all | solution.py:442
  101.9 15.9 %collective-permute-start.4 = (bf16[128,2048]{1,0:T(8,128)(2,1)}, bf16[128,2048]{1,0:T(8,128)(2,1)S(1)}, u32[]{:S(2)}, u32[]{:S(2)}) collective-permute-start(bf16[128,2048]{1,0:T(8,128)(2,1)} %get-tuple-element.20), channel_id=1, source_target_pairs={{0,1},{1,0},{2,3},{3,2},{4,5},{5,4},{6,7},{7,6},{8,9},{9,8},{10,11... | collective-permute-start | bytes 1572872 | tf_op jit(solution)/shard_map/ppermute | solution.py:481
  102.3 11.0 %collective-permute-start.5 = (bf16[2,128,256]{2,1,0:T(8,128)(2,1)S(1)}, bf16[2,128,256]{2,1,0:T(8,128)(2,1)S(1)}, u32[]{:S(2)}, u32[]{:S(2)}) collective-permute-start(bf16[2,128,256]{2,1,0:T(8,128)(2,1)S(1)} %get-tuple-element.22), channel_id=1, source_target_pairs={{2,0},{4,2},{6,4},{3,1},{5,3},{7,5},{10,8},{12,10},{14,12},{11,9},... | collective-permute-start | bytes 393224 | tf_op jit(solution)/shard_map/ppermute | solution.py:469
  103.5 12.7 %collective-permute-start.6 = (bf16[2,128,256]{2,1,0:T(8,128)(2,1)S(1)}, bf16[2,128,256]{2,1,0:T(8,128)(2,1)S(1)}, u32[]{:S(2)}, u32[]{:S(2)}) collective-permute-start(bf16[2,128,256]{2,1,0:T(8,128)(2,1)S(1)} %get-tuple-element.23), channel_id=1, source_target_pairs={{4,0},{6,2},{5,1},{7,3},{12,8},{14,10},{13,9},{15,11},{20,16},{22,... | collective-permute-start | bytes 393224 | tf_op jit(solution)/shard_map/ppermute | solution.py:470
  116.4 1.4 %collective-permute-start.9 = (bf16[2,128,256]{2,1,0:T(8,128)(2,1)S(1)}, bf16[2,128,256]{2,1,0:T(8,128)(2,1)S(1)}, u32[]{:S(2)}, u32[]{:S(2)}) collective-permute-start(bf16[2,128,256]{2,1,0:T(8,128)(2,1)S(1)} %pad_maximum_fusion.2), channel_id=1, source_target_pairs={{0,1},{1,0},{2,3},{3,2},{4,5},{5,4},{6,7},{7,6},{8,9},{9,8},{10,11... | collective-permute-start | bytes 393224 | tf_op jit(solution)/shard_map/ppermute | solution.py:482

commit v7 on v6

--- a/solution.py
+++ b/solution.py
@@ -122,7 +122,7 @@
 
 
 def side_parity(core, side):
-    return core if side == 0 else 1 - core
+    return core + side - 2 * core * side
 
 
 def first_place(core, side, small):
@@ -156,26 +156,24 @@
     return raw * EXP2_SCALE + jnp.concatenate([bias, bias], axis=1)
 
 
-def head_pair(own, oth, which, step):
-    group, side, pair = place_of(step)
-    start = group * WIDTH + pair * COLS
-    two = (own if side == 0 else oth)[which, :, start : start + COLS]
+def head_pair(rows, which, side, group, pair):
+    two = rows[side, which, :, lanes(group * WIDTH + pair * COLS, COLS)]
     return jnp.concatenate([two[:, :HD], two[:, HD:]], axis=0)
 
 
-STEPS = 4 * PAIRS
-
-
-def place_of(step):
-    group, rest = divmod(step, 2 * PAIRS)
-    return group, 1 - rest // PAIRS, rest % PAIRS
-
-
-def start_loads(core, q_hbm, do_hbm, oth_hbm, kv_hbm, own, oth, kv, sems):
+def for_each_block(body):
+    def one(at, carry):
+        body(at, 1 - at // 2, at % 2)
+        return carry
+
+    lax.fori_loop(0, 4, one, 0)
+
+
+def start_loads(core, q_hbm, do_hbm, oth_hbm, kv_hbm, rows, kv, sems):
     cols = lanes(core * HALF, HALF)
     moves = [(ref, kv.at[i]) for i, ref in enumerate(kv_hbm)]
-    moves += [(oth_hbm.at[i], oth.at[i]) for i in range(2)]
-    moves += [(ref.at[:, cols], own.at[i]) for i, ref in enumerate((q_hbm, do_hbm))]
+    moves += [(oth_hbm.at[i], rows.at[1, i]) for i in range(2)]
+    moves += [(ref.at[:, cols], rows.at[0, i]) for i, ref in enumerate((q_hbm, do_hbm))]
     copies = [pltpu.make_async_copy(a, b, sems.at[i]) for i, (a, b) in enumerate(moves)]
     for copy in copies:
         copy.start()
@@ -201,47 +199,45 @@
                 part[side, :, group * HD : (group + 1) * HD] = cut.astype(part.dtype)
 
 
-def probs_body(small, core, own, others, loads, k_buf, stat_ref, bias_ref, dv_acc):
+def probs_body(small, core, rows, k_buf, stat_ref, bias_ref, dv_acc):
     win = 2 if small else WIN
 
-    def raw_scores(step):
-        if step == PAIRS:
-            for load in loads:
-                load.wait()
-        group, side, _ = place_of(step)
-        return dot(window(k_buf, group, core, side, small), head_pair(own, others, 0, step), NT)
-
-    following = raw_scores(0)
-    for step in range(STEPS):
-        group, side, _ = place_of(step)
-        raw = following
-        if step + 1 < STEPS:
-            following = raw_scores(step + 1)
-        scores = masked(raw, bias_ref[side, : win * BLK])
-        peak = jnp.max(scores, axis=0, keepdims=True)
-        exponent = jnp.exp2(scores - peak)
-        over = 1.0 / jnp.sum(exponent, axis=0, keepdims=True)
-        stat_ref[0, step : step + 1] = peak
-        stat_ref[1, step : step + 1] = over
-        probs = (exponent * over).astype(BF16)
-        dv_acc[group, window_rows(core, side, small), :] += dot(
-            probs, head_pair(own, others, 1, step), NN
-        )
+    def block(at, side, group):
+        def raw_scores(pair):
+            keys = window(k_buf, group, core, side, small)
+            return dot(keys, head_pair(rows, 0, side, group, pair), NT)
+
+        following = raw_scores(0)
+        for pair in range(PAIRS):
+            raw = following
+            if pair + 1 < PAIRS:
+                following = raw_scores(pair + 1)
+            scores = masked(raw, bias_ref[side, : win * BLK])
+            peak = jnp.max(scores, axis=0, keepdims=True)
+            exponent = jnp.exp2(scores - peak)
+            over = 1.0 / jnp.sum(exponent, axis=0, keepdims=True)
+            stat_ref[at, 0, pair : pair + 1] = peak
+            stat_ref[at, 1, pair : pair + 1] = over
+            probs = (exponent * over).astype(BF16)
+            dv_acc[group, window_rows(core, side, small), :] += dot(
+                probs, head_pair(rows, 1, side, group, pair), NN
+            )
+
+    for_each_block(block)
 
 
 def probs_kernel(
     lengths, q_hbm, do_hbm, oth_hbm, kv_two, kv_one, kv_here,
     dv_two, dv_one, dv_here, stat_ref, bias_ref,
-    k_buf, dv_acc, own, others, kv, sems,
+    k_buf, dv_acc, rows, kv, sems,
 ):
     chip, core = lax.axis_index("x"), lax.axis_index("core")
     loads = start_loads(
-        core, q_hbm, do_hbm, oth_hbm, (kv_two, kv_one, kv_here), own, others, kv, sems
+        core, q_hbm, do_hbm, oth_hbm, (kv_two, kv_one, kv_here), rows, kv, sems
     )
     dv_acc[...] = jnp.zeros_like(dv_acc)
-    for load in loads[:5]:
+    for load in loads:
         load.wait()
-    loads = loads[5:]
     for group in range(2):
         gather_keys(core, [kv.at[i] for i in range(3)], 0, group, k_buf)
     for small in (True, False):
@@ -249,52 +245,47 @@
         def _():
             for side in range(2):
                 write_bias(lengths, chip, core, side, small, bias_ref)
-            probs_body(small, core, own, others, loads, k_buf, stat_ref, bias_ref, dv_acc)
+            probs_body(small, core, rows, k_buf, stat_ref, bias_ref, dv_acc)
     store_parts(core, dv_acc, (dv_two, dv_one, dv_here), None)
 
 
-def scores_body(
-    small, core, own, others, loads, k_buf, v_buf, k_t, stat_ref, bias_ref, dk_acc, dq_buf
-):
+def scores_body(small, core, rows, k_buf, v_buf, k_t, stat_ref, bias_ref, dk_acc, dq_buf):
     win = 2 if small else WIN
 
-    def products(step):
-        if step == PAIRS:
-            for load in loads:
-                load.wait()
-        group, side, _ = place_of(step)
-        raw = dot(window(k_buf, group, core, side, small), head_pair(own, others, 0, step), NT)
-        grad = dot(window(v_buf, group, core, side, small), head_pair(own, others, 1, step), NT)
-        return raw, grad
-
-    following = products(0)
-    for step in range(STEPS):
-        group, side, pair = place_of(step)
-        raw, dprobs = following
-        if step + 1 < STEPS:
-            following = products(step + 1)
-        rows = window_rows(core, side, small)
-        peak, over = stat_ref[0, step : step + 1], stat_ref[1, step : step + 1]
-        scores = masked(raw, bias_ref[side, : win * BLK])
-        probs = jnp.exp2(scores - peak) * over
-        delta = jnp.sum(probs * dprobs, axis=0, keepdims=True)
-        dscores = (probs * (dprobs - delta)).astype(BF16)
-        dk_acc[group, rows, :] += dot(dscores, head_pair(own, others, 0, step), NN)
-        dq_t = dot(k_t[group, :, rows], dscores, NN) * SCALE
-        for i in range(2):
-            start = group * WIDTH + (2 * pair + i) * HD
-            dq = dq_t[:, i * BLK : (i + 1) * BLK].T.astype(BF16)
-            dq_buf[side, :, start : start + HD] = dq
+    def block(at, side, group):
+        def products(pair):
+            keys = window(k_buf, group, core, side, small)
+            values = window(v_buf, group, core, side, small)
+            raw = dot(keys, head_pair(rows, 0, side, group, pair), NT)
+            return raw, dot(values, head_pair(rows, 1, side, group, pair), NT)
+
+        following = products(0)
+        span = window_rows(core, side, small)
+        for pair in range(PAIRS):
+            raw, dprobs = following
+            if pair + 1 < PAIRS:
+                following = products(pair + 1)
+            peak, over = stat_ref[at, 0, pair : pair + 1], stat_ref[at, 1, pair : pair + 1]
+            scores = masked(raw, bias_ref[side, : win * BLK])
+            probs = jnp.exp2(scores - peak) * over
+            delta = jnp.sum(probs * dprobs, axis=0, keepdims=True)
+            dscores = (probs * (dprobs - delta)).astype(BF16)
+            dk_acc[group, span, :] += dot(dscores, head_pair(rows, 0, side, group, pair), NN)
+            dq_t = dot(k_t[group, :, span], dscores, NN) * SCALE
+            dq = [dq_t[:, i * BLK : (i + 1) * BLK].T.astype(BF16) for i in range(2)]
+            dq_buf[side, :, lanes(group * WIDTH + pair * COLS, COLS)] = jnp.concatenate(dq, axis=1)
+
+    for_each_block(block)
 
 
 def scores_kernel(
     lengths, q_hbm, do_hbm, oth_hbm, kv_two, kv_one, kv_here, stat_ref, bias_ref,
     dq_hbm, sent_hbm, dk_two, dk_one, dk_here,
-    k_buf, v_buf, k_t, dk_acc, own, others, kv, sems, dq_buf, out_sems,
+    k_buf, v_buf, k_t, dk_acc, rows, kv, sems, dq_buf, out_sems,
 ):
     chip, core = lax.axis_index("x"), lax.axis_index("core")
     loads = start_loads(
-        core, q_hbm, do_hbm, oth_hbm, (kv_two, kv_one, kv_here), own, others, kv, sems
+        core, q_hbm, do_hbm, oth_hbm, (kv_two, kv_one, kv_here), rows, kv, sems
     )
     targets = (dq_hbm.at[:, lanes(core * HALF, HALF)], sent_hbm)
     stores = [
@@ -302,9 +293,8 @@
         for side, target in enumerate(targets)
     ]
     dk_acc[...] = jnp.zeros_like(dk_acc)
-    for load in loads[:5]:
+    for load in loads:
         load.wait()
-    loads = loads[5:]
     parts = [kv.at[i] for i in range(3)]
     for group in range(2):
         gather_keys(core, parts, 0, group, k_buf)
@@ -314,8 +304,7 @@
         @pl.when((chip == 0) == small)
         def _():
             scores_body(
-                small, core, own, others, loads, k_buf, v_buf, k_t, stat_ref, bias_ref, dk_acc,
-                dq_buf,
+                small, core, rows, k_buf, v_buf, k_t, stat_ref, bias_ref, dk_acc, dq_buf
             )
     for store in stores:
         store.start()
@@ -328,14 +317,13 @@
 KEYS = pltpu.VMEM((2, SPAN, BLK, HD), BF16)
 TURNED = pltpu.VMEM((2, HD, SPAN * BLK), BF16)
 TOTAL = pltpu.VMEM((2, SPAN * BLK, HD), F32)
-ROWS = pltpu.VMEM((2, BLK, HALF), BF16)
-OWN = [ROWS, ROWS, pltpu.VMEM((3, 2, 2, BLK, COLS), BF16), pltpu.SemaphoreType.DMA((7,))]
+OWN = [pltpu.VMEM((2, 2, BLK, HALF), BF16), pltpu.VMEM((3, 2, 2, BLK, COLS), BF16), pltpu.SemaphoreType.DMA((7,))]
 PRODUCT = 2 * 16 * 2 * BLK * WIN * BLK * HD
 OPERANDS = [IN_SMEM] + [IN_HBM] * 6
 
 
 def attention_probs(operands):
-    stats = pltpu.VMEM((2, STEPS, 2 * BLK), F32)
+    stats = pltpu.VMEM((4, 2, PAIRS, 2 * BLK), F32)
     bias = pltpu.VMEM((2, WIN * BLK, BLK), F32)
     return call(
         probs_kernel, OPERANDS[:4] + [IN_VMEM] + OPERANDS[5:],

time: 121 us -> 124 us (1.025)
  Pallas kernels: 20.7 us -> 22.7 us
    pallas_call x9, Pallas kernels: 19.9 us -> 21.9 us  [call(): pl.pallas_call(kernel, in_specs=list(in_specs), out_specs=out_specs, out_...]
  transfers between devices with their start and end apart: 15 -> 15, of which waited for: 9 -> 9; matrix products, arithmetic and copies ran while one was open for 0% -> 0% of each run, Pallas kernels for 12% -> 13%
where the time goes in v7:
time: 124 us; the launch traced here: 122 us
  waiting for transfers between devices  47 us (38%)
  blocking collectives  31.8 us (26%)
  Pallas kernels  22.7 us (18%)
  starting transfers between devices  20.1 us (16%)
    all_to_all x1, blocking collectives, exchange(): return lax.all_to_all(value, axes, 0, 0, tiled=True)  31.8 us
    ppermute x2, waiting for transfers between devices, summed(): one = lax.ppermute(one, 'x', [(1, 0), (2, 1), (3, 2)])  24 us
    pallas_call x9, Pallas kernels, call(): pl.pallas_call(kernel, in_specs=list(in_specs), out_specs=out_specs, out_...  21.9 us
    ppermute x2, waiting for transfers between devices, summed(): two = lax.ppermute(two, 'x', [(2, 0), (3, 1)])  6.91 us
    all_to_all x1, starting transfers between devices, exchange(): return lax.all_to_all(value, axes, 0, 0, tiled=True)  6.22 us
    ppermute x1, waiting for transfers between devices, shards(): kv_one = lax.ppermute(kv_here, 'x', [(0, 1), (1, 2), (2, 3)])  5.83 us
    ppermute x3, waiting for transfers between devices, shards(): lax.ppermute(dv, 'z', [(i, (i + away) % 4) for i in range(4)])  5.03 us
    ppermute x1, waiting for transfers between devices, shards(): kv_here = jnp.stack([kv_keep, lax.ppermute(kv_send, 'core', SWAP)])  3.82 us
  transfers between devices with their start and end apart: 15, of which 9 were waited for; matrix products, arithmetic and copies ran while one was open for 0% of the time, Pallas kernels for 13%

profile of v7, /device:TPU:0, one launch (start us, length us, event | category | flops | bytes accessed | tf_op | source)
XLA Modules:
  0.0 122.5 jit_solution(12906724453530012283)
XLA Ops:
  0.6 2.6 %shard_map.99 = bf16[4,4,128,512]{3,2,1,0:T(8,128)(2,1)} custom-call(bf16[128,8192]{1,0:T(8,128)(2,1)} %bitcast.10), custom_call_target="tpu_custom_call" | custom-call | bytes 4194304 | tf_op jit(solution)/shard_map/pallas_call | solution.py:62
  3.3 31.8 %all_to_all.10.x = bf16[4,4,128,512]{3,2,1,0:T(8,128)(2,1)S(1)} all-to-all(bf16[4,4,128,512]{3,2,1,0:T(8,128)(2,1)} %shard_map.99), channel_id=1, replica_groups=mesh['y'=4,'z'=4,'x'=4,'core'=2] {'z'}, dimensions={0} | all-to-all | bytes 4194304 | tf_op jit(solution)/shard_map/all_to_all | solution.py:430
  35.0 0.0 copy-start.3
  35.0 0.0 copy-start.4
  35.0 0.0 collective-permute-start.10
  35.0 0.0 copy-start.1
  35.0 1.3 %shard_map.93 = bf16[2,128,2048]{2,1,0:T(8,128)(2,1)S(1)} custom-call(bf16[128,4096]{1,0:T(8,128)(2,1)} %bitcast.11, bf16[128,4096]{1,0:T(8,128)(2,1)} %bitcast.14), custom_call_target="tpu_custom_call" | custom-call | bytes 1048576 | tf_op jit(solution)/shard_map/pallas_call | solution.py:62
  36.3 0.5 collective-permute-start
  36.9 0.0 copy-done.3
  36.9 0.0 copy-done.4
  36.9 0.1 collective-permute-start.1
  37.1 3.8 %collective-permute-done.1 = bf16[2,128,256]{2,1,0:T(8,128)(2,1)S(1)} collective-permute-done((bf16[2,128,256]{2,1,0:T(8,128)(2,1)S(1)}, bf16[2,128,256]{2,1,0:T(8,128)(2,1)S(1)}, u32[]{:S(2)}, u32[]{:S(2)}) %collective-permute-start.1) | collective-permute-done | bytes 131104 | tf_op jit(solution)/shard_map/ppermute | solution.py:443
  40.9 0.0 copy-start.2
  40.9 3.4 %collective-permute-start.2 = (bf16[2,2,128,256]{3,2,1,0:T(8,128)(2,1)S(1)}, bf16[2,2,128,256]{3,2,1,0:T(8,128)(2,1)S(1)}, u32[]{:S(2)}, u32[]{:S(2)}) collective-permute-start(bf16[2,2,128,256]{3,2,1,0:T(8,128)(2,1)S(1)} %pad_maximum_fusion.kv_here), channel_id=1, source_target_pairs={{0,2},{2,4},{4,6},{1,3},{3,5},{5,7},{8,10},{10,12},{12,14},{9,11},... | collective-permute-start | bytes 786440 | tf_op jit(solution)/shard_map/ppermute | solution.py:444
  44.3 5.8 %collective-permute-done.2.kv_one = bf16[2,2,128,256]{3,2,1,0:T(8,128)(2,1)S(1)} collective-permute-done((bf16[2,2,128,256]{3,2,1,0:T(8,128)(2,1)S(1)}, bf16[2,2,128,256]{3,2,1,0:T(8,128)(2,1)S(1)}, u32[]{:S(2)}, u32[]{:S(2)}) %collective-permute-start.2) | collective-permute-done | bytes 262176 | tf_op jit(solution)/shard_map/ppermute | solution.py:444
  50.2 0.0 copy-start.5
  50.2 0.7 collective-permute-start.3
  50.8 0.0 collective-permute-done.3.kv_two
  50.9 0.0 copy-start
  50.9 0.0 collective-permute-done.oth_hbm
  50.9 0.0 copy-done.2
  50.9 0.0 copy-done.5
  50.9 0.0 copy-done.1
  50.9 5.3 %shard_map.94 = (bf16[2,128,256]{2,1,0:T(8,128)(2,1)S(1)}, bf16[2,128,256]{2,1,0:T(8,128)(2,1)S(1)}, f32[2,128,256]{2,1,0:T(8,128)S(1)}, f32[4,2,4,256]{3,2,1,0:T(4,128)S(1)}, f32[2,640,128]{2,1,0:T(8,128)S(1)}) custom-call(s32[1,8]{1,0:T(1,128)S(1)} %copy-done.1, bf16[128,4096]{1,0:T(8,128)(2,1)} %bitcast.12, bf16[128,4096]{1,0:T(8,128)(2,1)} %bitcast.15, ...), custom_call_target="tpu_custom_call" | custom-call | flops 1342177280 | bytes 4194304 | tf_op jit(solution)/shard_map/pallas_call | solution.py:62
  56.2 0.0 copy-done
  56.2 1.3 %collective-permute-start.7 = (bf16[2,128,256]{2,1,0:T(8,128)(2,1)S(1)}, bf16[2,128,256]{2,1,0:T(8,128)(2,1)S(1)}, u32[]{:S(2)}, u32[]{:S(2)}) collective-permute-start(bf16[2,128,256]{2,1,0:T(8,128)(2,1)S(1)} %get-tuple-element.25), channel_id=1, source_target_pairs={{2,0},{4,2},{6,4},{3,1},{5,3},{7,5},{10,8},{12,10},{14,12},{11,9},... | collective-permute-start | bytes 393224 | tf_op jit(solution)/shard_map/ppermute | solution.py:457
  57.5 1.3 %collective-permute-start.8 = (bf16[2,128,256]{2,1,0:T(8,128)(2,1)S(1)}, bf16[2,128,256]{2,1,0:T(8,128)(2,1)S(1)}, u32[]{:S(2)}, u32[]{:S(2)}) collective-permute-start(bf16[2,128,256]{2,1,0:T(8,128)(2,1)S(1)} %get-tuple-element.26), channel_id=1, source_target_pairs={{4,0},{6,2},{5,1},{7,3},{12,8},{14,10},{13,9},{15,11},{20,16},{22,... | collective-permute-start | bytes 393224 | tf_op jit(solution)/shard_map/ppermute | solution.py:458
  58.8 15.5 %collective-permute-done.7.one = bf16[2,128,256]{2,1,0:T(8,128)(2,1)S(1)} collective-permute-done((bf16[2,128,256]{2,1,0:T(8,128)(2,1)S(1)}, bf16[2,128,256]{2,1,0:T(8,128)(2,1)S(1)}, u32[]{:S(2)}, u32[]{:S(2)}) %collective-permute-start.7) | collective-permute-done | bytes 131104 | tf_op jit(solution)/shard_map/ppermute | solution.py:457
  74.3 3.8 %collective-permute-done.8.two = bf16[2,128,256]{2,1,0:T(8,128)(2,1)S(1)} collective-permute-done((bf16[2,128,256]{2,1,0:T(8,128)(2,1)S(1)}, bf16[2,128,256]{2,1,0:T(8,128)(2,1)S(1)}, u32[]{:S(2)}, u32[]{:S(2)}) %collective-permute-start.8) | collective-permute-done | bytes 131104 | tf_op jit(solution)/shard_map/ppermute | solution.py:458
  78.1 0.6 collective-permute-start.11
  78.8 2.1 %collective-permute-start.12 = (bf16[2,128,256]{2,1,0:T(8,128)(2,1)S(1)}, bf16[2,128,256]{2,1,0:T(8,128)(2,1)S(1)}, u32[]{:S(2)}, u32[]{:S(2)}) collective-permute-start(bf16[2,128,256]{2,1,0:T(8,128)(2,1)S(1)} %shard_map.97.dv.refs_0_), channel_id=1, source_target_pairs={{0,16},{8,24},{16,0},{24,8},{1,17},{9,25},{17,1},{25,9},{2,18},{10... | collective-permute-start | bytes 393224 | tf_op jit(solution)/shard_map/ppermute | solution.py:463
  80.8 0.8 collective-permute-start.13
  81.7 4.1 %collective-permute-done.11.refs_1_ = bf16[2,128,256]{2,1,0:T(8,128)(2,1)S(1)} collective-permute-done((bf16[2,128,256]{2,1,0:T(8,128)(2,1)S(1)}, bf16[2,128,256]{2,1,0:T(8,128)(2,1)S(1)}, u32[]{:S(2)}, u32[]{:S(2)}) %collective-permute-start.11) | collective-permute-done | bytes 131104 | tf_op jit(solution)/shard_map/ppermute | solution.py:463
  85.8 0.0 collective-permute-done.12.refs_2_
  85.8 0.9 collective-permute-done.13.refs_3_
  86.7 0.8 shard_map.100.past
  87.5 0.0 collective-permute-done.10.x
  87.5 3.4 %shard_map.101 = bf16[2048,256]{1,0:T(8,128)(2,1)} custom-call(bf16[4,4,128,512]{3,2,1,0:T(8,128)(2,1)} %collective-permute-done.10.x, f32[2048,256]{1,0:T(8,128)S(1)} %shard_map.100.past, bf16[2,128,256]{2,1,0:T(8,128)(2,1)S(1)} %shard_map.97.dv.refs_0_, bf16[2,128,256]{2,1,0:T(8,128)(2,1)S(1)} %collective-permute-done.11.refs_1_, ...), custom_call_target="tpu_custom_call" | custom-call | flops 536870912 | bytes 4194304 | tf_op jit(solution)/shard_map/pallas_call | solution.py:62
  90.8 6.2 %all-to-all-start.1 = ((bf16[32,64,256]{2,1,0:T(8,128)(2,1)}), bf16[32,64,256]{2,1,0:T(8,128)(2,1)S(1)}, u32[]{:S(2)}, u32[]{:S(2)}) async-start(bf16[32,64,256]{2,1,0:T(8,128)(2,1)} %bitcast.8), calls=%async_computation.1 | async-start | bytes 2097152 | tf_op jit(solution)/shard_map/all_to_all | solution.py:430
  97.1 7.6 %shard_map.95 = (bf16[128,4096]{1,0:T(8,128)(2,1)}, bf16[128,2048]{1,0:T(8,128)(2,1)}, bf16[2,128,256]{2,1,0:T(8,128)(2,1)S(1)}, bf16[2,128,256]{2,1,0:T(8,128)(2,1)S(1)}, f32[2,128,256]{2,1,0:T(8,128)S(1)}) custom-call(s32[1,8]{1,0:T(1,128)S(1)} %copy-done.1, bf16[128,4096]{1,0:T(8,128)(2,1)} %bitcast.13, bf16[128,4096]{1,0:T(8,128)(2,1)} %bitcast.16, ...), custom_call_target="tpu_custom_call" | custom-call | flops 2684354560 | bytes 4194304 | tf_op jit(solution)/shard_map/pallas_call | solution.py:62
  104.7 0.4 collective-permute-start.4
  105.0 1.3 %collective-permute-start.5 = (bf16[2,128,256]{2,1,0:T(8,128)(2,1)S(1)}, bf16[2,128,256]{2,1,0:T(8,128)(2,1)S(1)}, u32[]{:S(2)}, u32[]{:S(2)}) collective-permute-start(bf16[2,128,256]{2,1,0:T(8,128)(2,1)S(1)} %get-tuple-element.22), channel_id=1, source_target_pairs={{2,0},{4,2},{6,4},{3,1},{5,3},{7,5},{10,8},{12,10},{14,12},{11,9},... | collective-permute-start | bytes 393224 | tf_op jit(solution)/shard_map/ppermute | solution.py:457
  106.3 1.3 %collective-permute-start.6 = (bf16[2,128,256]{2,1,0:T(8,128)(2,1)S(1)}, bf16[2,128,256]{2,1,0:T(8,128)(2,1)S(1)}, u32[]{:S(2)}, u32[]{:S(2)}) collective-permute-start(bf16[2,128,256]{2,1,0:T(8,128)(2,1)S(1)} %get-tuple-element.23), channel_id=1, source_target_pairs={{4,0},{6,2},{5,1},{7,3},{12,8},{14,10},{13,9},{15,11},{20,16},{22,... | collective-permute-start | bytes 393224 | tf_op jit(solution)/shard_map/ppermute | solution.py:458
  107.6 8.5 %collective-permute-done.5.one = bf16[2,128,256]{2,1,0:T(8,128)(2,1)S(1)} collective-permute-done((bf16[2,128,256]{2,1,0:T(8,128)(2,1)S(1)}, bf16[2,128,256]{2,1,0:T(8,128)(2,1)S(1)}, u32[]{:S(2)}, u32[]{:S(2)}) %collective-permute-start.5) | collective-permute-done | bytes 131104 | tf_op jit(solution)/shard_map/ppermute | solution.py:457
  116.2 3.1 %collective-permute-done.6.two = bf16[2,128,256]{2,1,0:T(8,128)(2,1)S(1)} collective-permute-done((bf16[2,128,256]{2,1,0:T(8,128)(2,1)S(1)}, bf16[2,128,256]{2,1,0:T(8,128)(2,1)S(1)}, u32[]{:S(2)}, u32[]{:S(2)}) %collective-permute-start.6) | collective-permute-done | bytes 131104 | tf_op jit(solution)/shard_map/ppermute | solution.py:458
  119.3 0.1 collective-permute-start.9
  119.4 1.3 %collective-permute-done.9.got = bf16[2,128,256]{2,1,0:T(8,128)(2,1)S(1)} collective-permute-done((bf16[2,128,256]{2,1,0:T(8,128)(2,1)S(1)}, bf16[2,128,256]{2,1,0:T(8,128)(2,1)S(1)}, u32[]{:S(2)}, u32[]{:S(2)}) %collective-permute-start.9) | collective-permute-done | bytes 131104 | tf_op jit(solution)/shard_map/ppermute | solution.py:470
  120.8 0.0 collective-permute-done.4.dq_got
  120.8 0.9 shard_map.98
  121.7 0.0 all-to-all-done.1.got
  121.7 0.8 weight_sum.1
  (9 shorter events, 0.2 us)
Async XLA Ops:
  35.0 1.8 %copy-start.3 = (bf16[1,128,512]{2,1,0:T(8,128)(2,1)S(1)}, bf16[1,128,512]{2,1,0:T(8,128)(2,1)}, u32[]{:S(2)}) copy-start(bf16[1,128,512]{2,1,0:T(8,128)(2,1)} %param.8) | copy-start | bytes 393220
  35.0 1.8 %copy-start.4 = (bf16[1,128,512]{2,1,0:T(8,128)(2,1)S(1)}, bf16[1,128,512]{2,1,0:T(8,128)(2,1)}, u32[]{:S(2)}) copy-start(bf16[1,128,512]{2,1,0:T(8,128)(2,1)} %param.7) | copy-start | bytes 393220
  35.0 52.5 %collective-permute-start.10 = (bf16[4,4,128,512]{3,2,1,0:T(8,128)(2,1)S(1)}, bf16[4,4,128,512]{3,2,1,0:T(8,128)(2,1)}, u32[]{:S(2)}, u32[]{:S(2)}) collective-permute-start(bf16[4,4,128,512]{3,2,1,0:T(8,128)(2,1)S(1)} %all_to_all.10.x), channel_id=1, source_target_pairs={{0,1},{1,0},{2,3},{3,2},{4,5},{5,4},{6,7},{7,6},{8,9},{9,8},{10,11... | collective-permute-start | bytes 6291464 | tf_op jit(solution)/shard_map/ppermute | solution.py:450
  35.0 15.9 %copy-start.1 = (s32[1,8]{1,0:T(1,128)S(1)}, s32[1,8]{1,0:T(1,128)}, u32[]{:S(2)}) copy-start(s32[1,8]{1,0:T(1,128)} %lengths.3) | copy-start | bytes 100
  36.3 14.6 %collective-permute-start = (bf16[2,128,2048]{2,1,0:T(8,128)(2,1)S(1)}, bf16[2,128,2048]{2,1,0:T(8,128)(2,1)}, u32[]{:S(2)}, u32[]{:S(2)}) collective-permute-start(bf16[2,128,2048]{2,1,0:T(8,128)(2,1)S(1)} %shard_map.93), channel_id=1, source_target_pairs={{0,1},{1,0},{2,3},{3,2},{4,5},{5,4},{6,7},{7,6},{8,9},{9,8},{10,11... | collective-permute-start | bytes 3145736 | tf_op jit(solution)/shard_map/ppermute | solution.py:447
  36.9 4.0 %collective-permute-start.1 = (bf16[2,128,256]{2,1,0:T(8,128)(2,1)S(1)}, bf16[2,128,256]{2,1,0:T(8,128)(2,1)S(1)}, u32[]{:S(2)}, u32[]{:S(2)}) collective-permute-start(bf16[2,128,256]{2,1,0:T(8,128)(2,1)S(1)} %pad_maximum_fusion.1), channel_id=1, source_target_pairs={{0,1},{1,0},{2,3},{3,2},{4,5},{5,4},{6,7},{7,6},{8,9},{9,8},{10,11... | collective-permute-start | bytes 393224 | tf_op jit(solution)/shard_map/ppermute | solution.py:443
  40.9 10.0 %copy-start.2 = (bf16[2,2,128,256]{3,2,1,0:T(8,128)(2,1)}, bf16[2,2,128,256]{3,2,1,0:T(8,128)(2,1)S(1)}, u32[]{:S(2)}) copy-start(bf16[2,2,128,256]{3,2,1,0:T(8,128)(2,1)S(1)} %pad_maximum_fusion.kv_here) | copy-start | bytes 786436
  40.9 9.3 %collective-permute-start.2 = (bf16[2,2,128,256]{3,2,1,0:T(8,128)(2,1)S(1)}, bf16[2,2,128,256]{3,2,1,0:T(8,128)(2,1)S(1)}, u32[]{:S(2)}, u32[]{:S(2)}) collective-permute-start(bf16[2,2,128,256]{3,2,1,0:T(8,128)(2,1)S(1)} %pad_maximum_fusion.kv_here), channel_id=1, source_target_pairs={{0,2},{2,4},{4,6},{1,3},{3,5},{5,7},{8,10},{10,12},{12,14},{9,11},... | collective-permute-start | bytes 786440 | tf_op jit(solution)/shard_map/ppermute | solution.py:444
  50.2 0.7 copy-start.5
  50.2 0.7 collective-permute-start.3
  50.9 5.3 %copy-start = (bf16[2,2,128,256]{3,2,1,0:T(8,128)(2,1)}, bf16[2,2,128,256]{3,2,1,0:T(8,128)(2,1)S(1)}, u32[]{:S(2)}) copy-start(bf16[2,2,128,256]{3,2,1,0:T(8,128)(2,1)S(1)} %collective-permute-done.3.kv_two) | copy-start | bytes 786436
  56.2 18.1 %collective-permute-start.7 = (bf16[2,128,256]{2,1,0:T(8,128)(2,1)S(1)}, bf16[2,128,256]{2,1,0:T(8,128)(2,1)S(1)}, u32[]{:S(2)}, u32[]{:S(2)}) collective-permute-start(bf16[2,128,256]{2,1,0:T(8,128)(2,1)S(1)} %get-tuple-element.25), channel_id=1, source_target_pairs={{2,0},{4,2},{6,4},{3,1},{5,3},{7,5},{10,8},{12,10},{14,12},{11,9},... | collective-permute-start | bytes 393224 | tf_op jit(solution)/shard_map/ppermute | solution.py:457
  57.5 20.6 %collective-permute-start.8 = (bf16[2,128,256]{2,1,0:T(8,128)(2,1)S(1)}, bf16[2,128,256]{2,1,0:T(8,128)(2,1)S(1)}, u32[]{:S(2)}, u32[]{:S(2)}) collective-permute-start(bf16[2,128,256]{2,1,0:T(8,128)(2,1)S(1)} %get-tuple-element.26), channel_id=1, source_target_pairs={{4,0},{6,2},{5,1},{7,3},{12,8},{14,10},{13,9},{15,11},{20,16},{22,... | collective-permute-start | bytes 393224 | tf_op jit(solution)/shard_map/ppermute | solution.py:458
  78.1 7.7 %collective-permute-start.11 = (bf16[2,128,256]{2,1,0:T(8,128)(2,1)S(1)}, bf16[2,128,256]{2,1,0:T(8,128)(2,1)S(1)}, u32[]{:S(2)}, u32[]{:S(2)}) collective-permute-start(bf16[2,128,256]{2,1,0:T(8,128)(2,1)S(1)} %shard_map.97.dv.refs_0_), channel_id=1, source_target_pairs={{0,8},{8,16},{16,24},{24,0},{1,9},{9,17},{17,25},{25,1},{2,10},{10... | collective-permute-start | bytes 393224 | tf_op jit(solution)/shard_map/ppermute | solution.py:463
  78.8 7.0 %collective-permute-start.12 = (bf16[2,128,256]{2,1,0:T(8,128)(2,1)S(1)}, bf16[2,128,256]{2,1,0:T(8,128)(2,1)S(1)}, u32[]{:S(2)}, u32[]{:S(2)}) collective-permute-start(bf16[2,128,256]{2,1,0:T(8,128)(2,1)S(1)} %shard_map.97.dv.refs_0_), channel_id=1, source_target_pairs={{0,16},{8,24},{16,0},{24,8},{1,17},{9,25},{17,1},{25,9},{2,18},{10... | collective-permute-start | bytes 393224 | tf_op jit(solution)/shard_map/ppermute | solution.py:463
  80.8 5.9 %collective-permute-start.13 = (bf16[2,128,256]{2,1,0:T(8,128)(2,1)S(1)}, bf16[2,128,256]{2,1,0:T(8,128)(2,1)S(1)}, u32[]{:S(2)}, u32[]{:S(2)}) collective-permute-start(bf16[2,128,256]{2,1,0:T(8,128)(2,1)S(1)} %shard_map.97.dv.refs_0_), channel_id=1, source_target_pairs={{0,24},{8,0},{16,8},{24,16},{1,25},{9,1},{17,9},{25,17},{2,26},{10... | collective-permute-start | bytes 393224 | tf_op jit(solution)/shard_map/ppermute | solution.py:463
  90.8 30.8 %all-to-all-start.1 = ((bf16[32,64,256]{2,1,0:T(8,128)(2,1)}), bf16[32,64,256]{2,1,0:T(8,128)(2,1)S(1)}, u32[]{:S(2)}, u32[]{:S(2)}) async-start(bf16[32,64,256]{2,1,0:T(8,128)(2,1)} %bitcast.8), calls=%async_computation.1 | async-start | bytes 2097152 | tf_op jit(solution)/shard_map/all_to_all | solution.py:430
  104.7 16.1 %collective-permute-start.4 = (bf16[128,2048]{1,0:T(8,128)(2,1)}, bf16[128,2048]{1,0:T(8,128)(2,1)S(1)}, u32[]{:S(2)}, u32[]{:S(2)}) collective-permute-start(bf16[128,2048]{1,0:T(8,128)(2,1)} %get-tuple-element.20), channel_id=1, source_target_pairs={{0,1},{1,0},{2,3},{3,2},{4,5},{5,4},{6,7},{7,6},{8,9},{9,8},{10,11... | collective-permute-start | bytes 1572872 | tf_op jit(solution)/shard_map/ppermute | solution.py:469
  105.0 11.1 %collective-permute-start.5 = (bf16[2,128,256]{2,1,0:T(8,128)(2,1)S(1)}, bf16[2,128,256]{2,1,0:T(8,128)(2,1)S(1)}, u32[]{:S(2)}, u32[]{:S(2)}) collective-permute-start(bf16[2,128,256]{2,1,0:T(8,128)(2,1)S(1)} %get-tuple-element.22), channel_id=1, source_target_pairs={{2,0},{4,2},{6,4},{3,1},{5,3},{7,5},{10,8},{12,10},{14,12},{11,9},... | collective-permute-start | bytes 393224 | tf_op jit(solution)/shard_map/ppermute | solution.py:457
  106.3 12.9 %collective-permute-start.6 = (bf16[2,128,256]{2,1,0:T(8,128)(2,1)S(1)}, bf16[2,128,256]{2,1,0:T(8,128)(2,1)S(1)}, u32[]{:S(2)}, u32[]{:S(2)}) collective-permute-start(bf16[2,128,256]{2,1,0:T(8,128)(2,1)S(1)} %get-tuple-element.23), channel_id=1, source_target_pairs={{4,0},{6,2},{5,1},{7,3},{12,8},{14,10},{13,9},{15,11},{20,16},{22,... | collective-permute-start | bytes 393224 | tf_op jit(solution)/shard_map/ppermute | solution.py:458
  119.3 1.4 %collective-permute-start.9 = (bf16[2,128,256]{2,1,0:T(8,128)(2,1)S(1)}, bf16[2,128,256]{2,1,0:T(8,128)(2,1)S(1)}, u32[]{:S(2)}, u32[]{:S(2)}) collective-permute-start(bf16[2,128,256]{2,1,0:T(8,128)(2,1)S(1)} %pad_maximum_fusion.2), channel_id=1, source_target_pairs={{0,1},{1,0},{2,3},{3,2},{4,5},{5,4},{6,7},{7,6},{8,9},{9,8},{10,11... | collective-permute-start | bytes 393224 | tf_op jit(solution)/shard_map/ppermute | solution.py:470

commit v8 on v6

--- a/solution.py
+++ b/solution.py
@@ -205,8 +205,10 @@
     win = 2 if small else WIN
 
     def raw_scores(step):
+        if step == 1:
+            loads[0].wait()
         if step == PAIRS:
-            for load in loads:
+            for load in loads[1:]:
                 load.wait()
         group, side, _ = place_of(step)
         return dot(window(k_buf, group, core, side, small), head_pair(own, others, 0, step), NT)
@@ -231,17 +233,17 @@
 
 def probs_kernel(
     lengths, q_hbm, do_hbm, oth_hbm, kv_two, kv_one, kv_here,
-    dv_two, dv_one, dv_here, stat_ref, bias_ref,
-    k_buf, dv_acc, own, others, kv, sems,
+    dv_two, dv_one, dv_here, stat_ref, bias_ref, own, others, kv,
+    k_buf, dv_acc, sems,
 ):
     chip, core = lax.axis_index("x"), lax.axis_index("core")
     loads = start_loads(
         core, q_hbm, do_hbm, oth_hbm, (kv_two, kv_one, kv_here), own, others, kv, sems
     )
     dv_acc[...] = jnp.zeros_like(dv_acc)
-    for load in loads[:5]:
+    for load in loads[:4]:
         load.wait()
-    loads = loads[5:]
+    loads = loads[4:]
     for group in range(2):
         gather_keys(core, [kv.at[i] for i in range(3)], 0, group, k_buf)
     for small in (True, False):
@@ -254,14 +256,11 @@
 
 
 def scores_body(
-    small, core, own, others, loads, k_buf, v_buf, k_t, stat_ref, bias_ref, dk_acc, dq_buf
+    small, core, own, others, k_buf, v_buf, k_t, stat_ref, bias_ref, dk_acc, dq_buf
 ):
     win = 2 if small else WIN
 
     def products(step):
-        if step == PAIRS:
-            for load in loads:
-                load.wait()
         group, side, _ = place_of(step)
         raw = dot(window(k_buf, group, core, side, small), head_pair(own, others, 0, step), NT)
         grad = dot(window(v_buf, group, core, side, small), head_pair(own, others, 1, step), NT)
@@ -288,23 +287,17 @@
 
 
 def scores_kernel(
-    lengths, q_hbm, do_hbm, oth_hbm, kv_two, kv_one, kv_here, stat_ref, bias_ref,
+    stat_ref, bias_ref, own, others, kv,
     dq_hbm, sent_hbm, dk_two, dk_one, dk_here,
-    k_buf, v_buf, k_t, dk_acc, own, others, kv, sems, dq_buf, out_sems,
+    k_buf, v_buf, k_t, dk_acc, dq_buf, out_sems,
 ):
     chip, core = lax.axis_index("x"), lax.axis_index("core")
-    loads = start_loads(
-        core, q_hbm, do_hbm, oth_hbm, (kv_two, kv_one, kv_here), own, others, kv, sems
-    )
     targets = (dq_hbm.at[:, lanes(core * HALF, HALF)], sent_hbm)
     stores = [
         pltpu.make_async_copy(dq_buf.at[side], target, out_sems.at[side])
         for side, target in enumerate(targets)
     ]
     dk_acc[...] = jnp.zeros_like(dk_acc)
-    for load in loads[:5]:
-        load.wait()
-    loads = loads[5:]
     parts = [kv.at[i] for i in range(3)]
     for group in range(2):
         gather_keys(core, parts, 0, group, k_buf)
@@ -314,7 +307,7 @@
         @pl.when((chip == 0) == small)
         def _():
             scores_body(
-                small, core, own, others, loads, k_buf, v_buf, k_t, stat_ref, bias_ref, dk_acc,
+                small, core, own, others, k_buf, v_buf, k_t, stat_ref, bias_ref, dk_acc,
                 dq_buf,
             )
     for store in stores:
@@ -329,7 +322,7 @@
 TURNED = pltpu.VMEM((2, HD, SPAN * BLK), BF16)
 TOTAL = pltpu.VMEM((2, SPAN * BLK, HD), F32)
 ROWS = pltpu.VMEM((2, BLK, HALF), BF16)
-OWN = [ROWS, ROWS, pltpu.VMEM((3, 2, 2, BLK, COLS), BF16), pltpu.SemaphoreType.DMA((7,))]
+LOADED = [ROWS, ROWS, pltpu.VMEM((3, 2, 2, BLK, COLS), BF16)]
 PRODUCT = 2 * 16 * 2 * BLK * WIN * BLK * HD
 OPERANDS = [IN_SMEM] + [IN_HBM] * 6
 
@@ -339,17 +332,17 @@
     bias = pltpu.VMEM((2, WIN * BLK, BLK), F32)
     return call(
         probs_kernel, OPERANDS[:4] + [IN_VMEM] + OPERANDS[5:],
-        PARTS + [stats, bias], operands,
-        [KEYS, TOTAL] + OWN, flops=2 * PRODUCT, exps=PRODUCT // 256, moved=4 << 20, room=16,
-    )
-
-
-def attention_scores(operands, stats, bias):
-    return call(
-        scores_kernel, OPERANDS + [IN_VMEM] * 2,
+        PARTS + [stats, bias] + LOADED, operands,
+        [KEYS, TOTAL, pltpu.SemaphoreType.DMA((7,))], flops=2 * PRODUCT, exps=PRODUCT // 256, moved=4 << 20, room=16,
+    )
+
+
+def attention_scores(kept):
+    return call(
+        scores_kernel, [IN_VMEM] * 5,
         [pltpu.HBM((BLK, width), BF16) for width in (2 * HALF, HALF)] + PARTS,
-        [*operands, stats, bias],
-        [KEYS, KEYS, TURNED, TOTAL] + OWN
+        kept,
+        [KEYS, KEYS, TURNED, TOTAL]
         + [pltpu.VMEM((2, BLK, HALF), BF16), pltpu.SemaphoreType.DMA((2,))],
         flops=4 * PRODUCT, exps=PRODUCT // 256, moved=4 << 20, room=16,
     )
@@ -462,8 +455,8 @@
     x_oth = lax.ppermute(x_own, "core", SWAP)
 
     operands = (lengths, queries, out_grad, others, kv_two, kv_one, kv_here)
-    dv_two, dv_one, dv_here, stats, bias = attention_probs(operands)
-    dq_kept, dq_sent, dk_two, dk_one, dk_here = attention_scores(operands, stats, bias)
+    dv_two, dv_one, dv_here, *kept = attention_probs(operands)
+    dq_kept, dq_sent, dk_two, dk_one, dk_here = attention_scores(kept)
 
     def summed(here, one, two):
         one = lax.ppermute(one, "x", [(1, 0), (2, 1), (3, 2)])

time: 121 us -> 125 us (1.033)
  local copies, waits for them, and re-layouts: 0.05 us -> 6.34 us
  Pallas kernels: 20.7 us -> 18.4 us
    unnamed x12 -> x26, local copies, waits for them, and re-layouts: 0.02 us -> 6.31 us
    pallas_call x9, Pallas kernels: 19.9 us -> 17.6 us  [call(): pl.pallas_call(kernel, in_specs=list(in_specs), out_specs=out_specs, out_...]
  transfers between devices with their start and end apart: 15 -> 15, of which waited for: 9 -> 9; matrix products, arithmetic and copies ran while one was open for 0% -> 0% of each run, Pallas kernels for 12% -> 9%
where the time goes in v8:
time: 125 us; the launch traced here: 123 us
  waiting for transfers between devices  45.6 us (36%)
  blocking collectives  31.8 us (25%)
  starting transfers between devices  20.2 us (16%)
  Pallas kernels  18.4 us (15%)
  local copies, waits for them, and re-layouts  6.34 us (5%)
    all_to_all x1, blocking collectives, exchange(): return lax.all_to_all(value, axes, 0, 0, tiled=True)  31.8 us
    ppermute x2, waiting for transfers between devices, summed(): one = lax.ppermute(one, 'x', [(1, 0), (2, 1), (3, 2)])  22.7 us
    pallas_call x9, Pallas kernels, call(): pl.pallas_call(kernel, in_specs=list(in_specs), out_specs=out_specs, out_...  17.6 us
    ppermute x2, waiting for transfers between devices, summed(): two = lax.ppermute(two, 'x', [(2, 0), (3, 1)])  6.9 us
    all_to_all x1, starting transfers between devices, exchange(): return lax.all_to_all(value, axes, 0, 0, tiled=True)  6.35 us
    unnamed x26, local copies, waits for them, and re-layouts  6.31 us
    ppermute x1, waiting for transfers between devices, shards(): kv_one = lax.ppermute(kv_here, 'x', [(0, 1), (1, 2), (2, 3)])  5.83 us
    ppermute x3, waiting for transfers between devices, shards(): lax.ppermute(dv, 'z', [(i, (i + away) % 4) for i in range(4)])  5.03 us
  transfers between devices with their start and end apart: 15, of which 9 were waited for; matrix products, arithmetic and copies ran while one was open for 0% of the time, Pallas kernels for 9%

profile of v8, /device:TPU:0, one launch (start us, length us, event | category | flops | bytes accessed | tf_op | source)
XLA Modules:
  0.0 123.3 jit_solution(17980605992204967055)
XLA Ops:
  0.6 2.6 %shard_map.99 = bf16[4,4,128,512]{3,2,1,0:T(8,128)(2,1)} custom-call(bf16[128,8192]{1,0:T(8,128)(2,1)} %bitcast.10), custom_call_target="tpu_custom_call" | custom-call | bytes 4194304 | tf_op jit(solution)/shard_map/pallas_call | solution.py:62
  3.3 31.8 %all_to_all.10.x = bf16[4,4,128,512]{3,2,1,0:T(8,128)(2,1)S(1)} all-to-all(bf16[4,4,128,512]{3,2,1,0:T(8,128)(2,1)} %shard_map.99), channel_id=1, replica_groups=mesh['y'=4,'z'=4,'x'=4,'core'=2] {'z'}, dimensions={0} | all-to-all | bytes 4194304 | tf_op jit(solution)/shard_map/all_to_all | solution.py:435
  35.0 0.0 copy-start.10
  35.0 0.0 copy-start.11
  35.1 0.0 collective-permute-start.10
  35.1 0.0 copy-start
  35.1 1.3 %shard_map.93 = bf16[2,128,2048]{2,1,0:T(8,128)(2,1)S(1)} custom-call(bf16[128,4096]{1,0:T(8,128)(2,1)} %bitcast.11, bf16[128,4096]{1,0:T(8,128)(2,1)} %bitcast.13), custom_call_target="tpu_custom_call" | custom-call | bytes 1048576 | tf_op jit(solution)/shard_map/pallas_call | solution.py:62
  36.3 0.5 collective-permute-start
  36.9 0.0 copy-done.10
  36.9 0.0 copy-done.11
  36.9 0.1 collective-permute-start.1
  37.1 3.8 %collective-permute-done.1 = bf16[2,128,256]{2,1,0:T(8,128)(2,1)S(1)} collective-permute-done((bf16[2,128,256]{2,1,0:T(8,128)(2,1)S(1)}, bf16[2,128,256]{2,1,0:T(8,128)(2,1)S(1)}, u32[]{:S(2)}, u32[]{:S(2)}) %collective-permute-start.1) | collective-permute-done | bytes 131104 | tf_op jit(solution)/shard_map/ppermute | solution.py:448
  40.9 0.0 copy-start.9
  40.9 3.4 %collective-permute-start.2 = (bf16[2,2,128,256]{3,2,1,0:T(8,128)(2,1)S(1)}, bf16[2,2,128,256]{3,2,1,0:T(8,128)(2,1)S(1)}, u32[]{:S(2)}, u32[]{:S(2)}) collective-permute-start(bf16[2,2,128,256]{3,2,1,0:T(8,128)(2,1)S(1)} %pad_maximum_fusion.kv_here), channel_id=1, source_target_pairs={{0,2},{2,4},{4,6},{1,3},{3,5},{5,7},{8,10},{10,12},{12,14},{9,11},... | collective-permute-start | bytes 786440 | tf_op jit(solution)/shard_map/ppermute | solution.py:449
  44.4 5.8 %collective-permute-done.2.kv_one = bf16[2,2,128,256]{3,2,1,0:T(8,128)(2,1)S(1)} collective-permute-done((bf16[2,2,128,256]{3,2,1,0:T(8,128)(2,1)S(1)}, bf16[2,2,128,256]{3,2,1,0:T(8,128)(2,1)S(1)}, u32[]{:S(2)}, u32[]{:S(2)}) %collective-permute-start.2) | collective-permute-done | bytes 262176 | tf_op jit(solution)/shard_map/ppermute | solution.py:449
  50.2 0.0 copy-start.12
  50.2 0.7 collective-permute-start.3
  50.9 0.0 collective-permute-done.3.kv_two
  50.9 0.0 collective-permute-done.oth_hbm
  50.9 0.0 copy-done.9
  50.9 0.0 copy-done.12
  50.9 0.0 copy-done
  50.9 4.3 %shard_map.94 = (bf16[2,128,256]{2,1,0:T(8,128)(2,1)S(1)}, bf16[2,128,256]{2,1,0:T(8,128)(2,1)S(1)}, f32[2,128,256]{2,1,0:T(8,128)S(1)}, f32[2,16,256]{2,1,0:T(8...) custom-call(s32[1,8]{1,0:T(1,128)S(1)} %copy-done, ...), custom_call_target="tpu_custom_call" | custom-call | flops 1342177280 | bytes 4194304 | tf_op jit(solution)/shard_map/pallas_call | solution.py:62
  55.2 0.0 copy-start.1
  55.3 1.0 copy-done.1
  56.2 0.0 copy-start.3
  56.2 1.0 copy-done.3
  57.2 0.0 copy-start.5
  57.2 0.9 copy-done.5
  58.1 0.0 copy-start.7
  58.1 1.3 %collective-permute-start.7 = (bf16[2,128,256]{2,1,0:T(8,128)(2,1)S(1)}, bf16[2,128,256]{2,1,0:T(8,128)(2,1)S(1)}, u32[]{:S(2)}, u32[]{:S(2)}) collective-permute-start(bf16[2,128,256]{2,1,0:T(8,128)(2,1)S(1)} %get-tuple-element.31), channel_id=1, source_target_pairs={{2,0},{4,2},{6,4},{3,1},{5,3},{7,5},{10,8},{12,10},{14,12},{11,9},... | collective-permute-start | bytes 393224 | tf_op jit(solution)/shard_map/ppermute | solution.py:462
  59.4 1.3 %collective-permute-start.8 = (bf16[2,128,256]{2,1,0:T(8,128)(2,1)S(1)}, bf16[2,128,256]{2,1,0:T(8,128)(2,1)S(1)}, u32[]{:S(2)}, u32[]{:S(2)}) collective-permute-start(bf16[2,128,256]{2,1,0:T(8,128)(2,1)S(1)} %get-tuple-element.32), channel_id=1, source_target_pairs={{4,0},{6,2},{5,1},{7,3},{12,8},{14,10},{13,9},{15,11},{20,16},{22,... | collective-permute-start | bytes 393224 | tf_op jit(solution)/shard_map/ppermute | solution.py:463
  60.7 14.6 %collective-permute-done.7.one = bf16[2,128,256]{2,1,0:T(8,128)(2,1)S(1)} collective-permute-done((bf16[2,128,256]{2,1,0:T(8,128)(2,1)S(1)}, bf16[2,128,256]{2,1,0:T(8,128)(2,1)S(1)}, u32[]{:S(2)}, u32[]{:S(2)}) %collective-permute-start.7) | collective-permute-done | bytes 131104 | tf_op jit(solution)/shard_map/ppermute | solution.py:462
  75.3 3.8 %collective-permute-done.8.two = bf16[2,128,256]{2,1,0:T(8,128)(2,1)S(1)} collective-permute-done((bf16[2,128,256]{2,1,0:T(8,128)(2,1)S(1)}, bf16[2,128,256]{2,1,0:T(8,128)(2,1)S(1)}, u32[]{:S(2)}, u32[]{:S(2)}) %collective-permute-start.8) | collective-permute-done | bytes 131104 | tf_op jit(solution)/shard_map/ppermute | solution.py:463
  79.2 0.6 collective-permute-start.11
  79.8 2.1 %collective-permute-start.12 = (bf16[2,128,256]{2,1,0:T(8,128)(2,1)S(1)}, bf16[2,128,256]{2,1,0:T(8,128)(2,1)S(1)}, u32[]{:S(2)}, u32[]{:S(2)}) collective-permute-start(bf16[2,128,256]{2,1,0:T(8,128)(2,1)S(1)} %shard_map.97.dv.refs_0_), channel_id=1, source_target_pairs={{0,16},{8,24},{16,0},{24,8},{1,17},{9,25},{17,1},{25,9},{2,18},{10... | collective-permute-start | bytes 393224 | tf_op jit(solution)/shard_map/ppermute | solution.py:468
  81.9 0.8 collective-permute-start.13
  82.7 4.1 %collective-permute-done.11.refs_1_ = bf16[2,128,256]{2,1,0:T(8,128)(2,1)S(1)} collective-permute-done((bf16[2,128,256]{2,1,0:T(8,128)(2,1)S(1)}, bf16[2,128,256]{2,1,0:T(8,128)(2,1)S(1)}, u32[]{:S(2)}, u32[]{:S(2)}) %collective-permute-start.11) | collective-permute-done | bytes 131104 | tf_op jit(solution)/shard_map/ppermute | solution.py:468
  86.9 0.0 collective-permute-done.12.refs_2_
  86.9 0.9 collective-permute-done.13.refs_3_
  87.8 0.8 shard_map.100.past
  88.5 0.0 copy-done.7
  88.5 0.0 collective-permute-done.10.x
  88.5 3.4 %shard_map.101 = bf16[2048,256]{1,0:T(8,128)(2,1)} custom-call(bf16[4,4,128,512]{3,2,1,0:T(8,128)(2,1)} %collective-permute-done.10.x, f32[2048,256]{1,0:T(8,128)S(1)} %shard_map.100.past, bf16[2,128,256]{2,1,0:T(8,128)(2,1)S(1)} %shard_map.97.dv.refs_0_, bf16[2,128,256]{2,1,0:T(8,128)(2,1)S(1)} %collective-permute-done.11.refs_1_, ...), custom_call_target="tpu_custom_call" | custom-call | flops 536870912 | bytes 4194304 | tf_op jit(solution)/shard_map/pallas_call | solution.py:62
  91.9 0.0 copy-start.2
  91.9 6.4 %all-to-all-start.1 = ((bf16[32,64,256]{2,1,0:T(8,128)(2,1)}), bf16[32,64,256]{2,1,0:T(8,128)(2,1)S(1)}, u32[]{:S(2)}, u32[]{:S(2)}) async-start(bf16[32,64,256]{2,1,0:T(8,128)(2,1)} %bitcast.8), calls=%async_computation.1 | async-start | bytes 2097152 | tf_op jit(solution)/shard_map/all_to_all | solution.py:435
  98.3 0.0 copy-done.2
  98.3 0.0 copy-start.4
  98.3 1.2 copy-done.4
  99.5 0.0 copy-start.6
  99.5 1.1 copy-done.6
  100.6 1.1 copy-done.8
  101.7 4.2 %shard_map.95 = (bf16[128,4096]{1,0:T(8,128)(2,1)}, bf16[128,2048]{1,0:T(8,128)(2,1)}, bf16[2,128,256]{2,1,0:T(8,128)(2,1)S(1)}, bf16[2,128,256]{2,1,0:T(8,128)(2,1)S(1)}, f32[2,128,256]{2,1,0:T(8,128)S(1)}) custom-call(f32[2,16,256]{2,1,0:T(8,128)S(1)} %get-tuple-element.20.stat_ref, f32[2,640,128]{2,1,0:T(8,128)S(1)} %copy-done.8, ...), custom_call_target="tpu_custom_call" | custom-call | flops 2684354560 | bytes 4194304 | tf_op jit(solution)/shard_map/pallas_call | solution.py:62
  105.9 0.3 collective-permute-start.4
  106.3 1.3 %collective-permute-start.5 = (bf16[2,128,256]{2,1,0:T(8,128)(2,1)S(1)}, bf16[2,128,256]{2,1,0:T(8,128)(2,1)S(1)}, u32[]{:S(2)}, u32[]{:S(2)}) collective-permute-start(bf16[2,128,256]{2,1,0:T(8,128)(2,1)S(1)} %get-tuple-element.28), channel_id=1, source_target_pairs={{2,0},{4,2},{6,4},{3,1},{5,3},{7,5},{10,8},{12,10},{14,12},{11,9},... | collective-permute-start | bytes 393224 | tf_op jit(solution)/shard_map/ppermute | solution.py:462
  107.6 1.3 %collective-permute-start.6 = (bf16[2,128,256]{2,1,0:T(8,128)(2,1)S(1)}, bf16[2,128,256]{2,1,0:T(8,128)(2,1)S(1)}, u32[]{:S(2)}, u32[]{:S(2)}) collective-permute-start(bf16[2,128,256]{2,1,0:T(8,128)(2,1)S(1)} %get-tuple-element.29), channel_id=1, source_target_pairs={{4,0},{6,2},{5,1},{7,3},{12,8},{14,10},{13,9},{15,11},{20,16},{22,... | collective-permute-start | bytes 393224 | tf_op jit(solution)/shard_map/ppermute | solution.py:463
  108.9 8.0 %collective-permute-done.5.one = bf16[2,128,256]{2,1,0:T(8,128)(2,1)S(1)} collective-permute-done((bf16[2,128,256]{2,1,0:T(8,128)(2,1)S(1)}, bf16[2,128,256]{2,1,0:T(8,128)(2,1)S(1)}, u32[]{:S(2)}, u32[]{:S(2)}) %collective-permute-start.5) | collective-permute-done | bytes 131104 | tf_op jit(solution)/shard_map/ppermute | solution.py:462
  116.9 3.1 %collective-permute-done.6.two = bf16[2,128,256]{2,1,0:T(8,128)(2,1)S(1)} collective-permute-done((bf16[2,128,256]{2,1,0:T(8,128)(2,1)S(1)}, bf16[2,128,256]{2,1,0:T(8,128)(2,1)S(1)}, u32[]{:S(2)}, u32[]{:S(2)}) %collective-permute-start.6) | collective-permute-done | bytes 131104 | tf_op jit(solution)/shard_map/ppermute | solution.py:463
  120.1 0.1 collective-permute-start.9
  120.2 1.3 %collective-permute-done.9.got = bf16[2,128,256]{2,1,0:T(8,128)(2,1)S(1)} collective-permute-done((bf16[2,128,256]{2,1,0:T(8,128)(2,1)S(1)}, bf16[2,128,256]{2,1,0:T(8,128)(2,1)S(1)}, u32[]{:S(2)}, u32[]{:S(2)}) %collective-permute-start.9) | collective-permute-done | bytes 131104 | tf_op jit(solution)/shard_map/ppermute | solution.py:475
  121.5 0.0 collective-permute-done.4.dq_got
  121.5 0.9 shard_map.98
  122.4 0.0 all-to-all-done.1.got
  122.5 0.8 weight_sum.1
  (10 shorter events, 0.2 us)
Async XLA Ops:
  35.0 1.8 %copy-start.10 = (bf16[1,128,512]{2,1,0:T(8,128)(2,1)S(1)}, bf16[1,128,512]{2,1,0:T(8,128)(2,1)}, u32[]{:S(2)}) copy-start(bf16[1,128,512]{2,1,0:T(8,128)(2,1)} %param.8) | copy-start | bytes 393220
  35.0 1.8 %copy-start.11 = (bf16[1,128,512]{2,1,0:T(8,128)(2,1)S(1)}, bf16[1,128,512]{2,1,0:T(8,128)(2,1)}, u32[]{:S(2)}) copy-start(bf16[1,128,512]{2,1,0:T(8,128)(2,1)} %param.7) | copy-start | bytes 393220
  35.1 53.5 %collective-permute-start.10 = (bf16[4,4,128,512]{3,2,1,0:T(8,128)(2,1)S(1)}, bf16[4,4,128,512]{3,2,1,0:T(8,128)(2,1)}, u32[]{:S(2)}, u32[]{:S(2)}) collective-permute-start(bf16[4,4,128,512]{3,2,1,0:T(8,128)(2,1)S(1)} %all_to_all.10.x), channel_id=1, source_target_pairs={{0,1},{1,0},{2,3},{3,2},{4,5},{5,4},{6,7},{7,6},{8,9},{9,8},{10,11... | collective-permute-start | bytes 6291464 | tf_op jit(solution)/shard_map/ppermute | solution.py:455
  35.1 15.9 %copy-start = (s32[1,8]{1,0:T(1,128)S(1)}, s32[1,8]{1,0:T(1,128)}, u32[]{:S(2)}) copy-start(s32[1,8]{1,0:T(1,128)} %lengths.1) | copy-start | bytes 100
  36.3 14.5 %collective-permute-start = (bf16[2,128,2048]{2,1,0:T(8,128)(2,1)S(1)}, bf16[2,128,2048]{2,1,0:T(8,128)(2,1)}, u32[]{:S(2)}, u32[]{:S(2)}) collective-permute-start(bf16[2,128,2048]{2,1,0:T(8,128)(2,1)S(1)} %shard_map.93), channel_id=1, source_target_pairs={{0,1},{1,0},{2,3},{3,2},{4,5},{5,4},{6,7},{7,6},{8,9},{9,8},{10,11... | collective-permute-start | bytes 3145736 | tf_op jit(solution)/shard_map/ppermute | solution.py:452
  36.9 4.0 %collective-permute-start.1 = (bf16[2,128,256]{2,1,0:T(8,128)(2,1)S(1)}, bf16[2,128,256]{2,1,0:T(8,128)(2,1)S(1)}, u32[]{:S(2)}, u32[]{:S(2)}) collective-permute-start(bf16[2,128,256]{2,1,0:T(8,128)(2,1)S(1)} %pad_maximum_fusion.1), channel_id=1, source_target_pairs={{0,1},{1,0},{2,3},{3,2},{4,5},{5,4},{6,7},{7,6},{8,9},{9,8},{10,11... | collective-permute-start | bytes 393224 | tf_op jit(solution)/shard_map/ppermute | solution.py:448
  40.9 10.0 %copy-start.9 = (bf16[2,2,128,256]{3,2,1,0:T(8,128)(2,1)}, bf16[2,2,128,256]{3,2,1,0:T(8,128)(2,1)S(1)}, u32[]{:S(2)}) copy-start(bf16[2,2,128,256]{3,2,1,0:T(8,128)(2,1)S(1)} %pad_maximum_fusion.kv_here) | copy-start | bytes 786436
  40.9 9.3 %collective-permute-start.2 = (bf16[2,2,128,256]{3,2,1,0:T(8,128)(2,1)S(1)}, bf16[2,2,128,256]{3,2,1,0:T(8,128)(2,1)S(1)}, u32[]{:S(2)}, u32[]{:S(2)}) collective-permute-start(bf16[2,2,128,256]{3,2,1,0:T(8,128)(2,1)S(1)} %pad_maximum_fusion.kv_here), channel_id=1, source_target_pairs={{0,2},{2,4},{4,6},{1,3},{3,5},{5,7},{8,10},{10,12},{12,14},{9,11},... | collective-permute-start | bytes 786440 | tf_op jit(solution)/shard_map/ppermute | solution.py:449
  50.2 0.7 copy-start.12
  50.2 0.7 collective-permute-start.3
  55.2 1.0 copy-start.1
  56.2 1.0 copy-start.3
  57.2 0.9 copy-start.5
  58.1 30.4 %copy-start.7 = (f32[2,640,128]{2,1,0:T(8,128)}, f32[2,640,128]{2,1,0:T(8,128)S(1)}, u32[]{:S(2)}) copy-start(f32[2,640,128]{2,1,0:T(8,128)S(1)} %get-tuple-element.21.bias_ref) | copy-start | bytes 1966084
  58.1 17.2 %collective-permute-start.7 = (bf16[2,128,256]{2,1,0:T(8,128)(2,1)S(1)}, bf16[2,128,256]{2,1,0:T(8,128)(2,1)S(1)}, u32[]{:S(2)}, u32[]{:S(2)}) collective-permute-start(bf16[2,128,256]{2,1,0:T(8,128)(2,1)S(1)} %get-tuple-element.31), channel_id=1, source_target_pairs={{2,0},{4,2},{6,4},{3,1},{5,3},{7,5},{10,8},{12,10},{14,12},{11,9},... | collective-permute-start | bytes 393224 | tf_op jit(solution)/shard_map/ppermute | solution.py:462
  59.4 19.8 %collective-permute-start.8 = (bf16[2,128,256]{2,1,0:T(8,128)(2,1)S(1)}, bf16[2,128,256]{2,1,0:T(8,128)(2,1)S(1)}, u32[]{:S(2)}, u32[]{:S(2)}) collective-permute-start(bf16[2,128,256]{2,1,0:T(8,128)(2,1)S(1)} %get-tuple-element.32), channel_id=1, source_target_pairs={{4,0},{6,2},{5,1},{7,3},{12,8},{14,10},{13,9},{15,11},{20,16},{22,... | collective-permute-start | bytes 393224 | tf_op jit(solution)/shard_map/ppermute | solution.py:463
  79.2 7.7 %collective-permute-start.11 = (bf16[2,128,256]{2,1,0:T(8,128)(2,1)S(1)}, bf16[2,128,256]{2,1,0:T(8,128)(2,1)S(1)}, u32[]{:S(2)}, u32[]{:S(2)}) collective-permute-start(bf16[2,128,256]{2,1,0:T(8,128)(2,1)S(1)} %shard_map.97.dv.refs_0_), channel_id=1, source_target_pairs={{0,8},{8,16},{16,24},{24,0},{1,9},{9,17},{17,25},{25,1},{2,10},{10... | collective-permute-start | bytes 393224 | tf_op jit(solution)/shard_map/ppermute | solution.py:468
  79.8 7.0 %collective-permute-start.12 = (bf16[2,128,256]{2,1,0:T(8,128)(2,1)S(1)}, bf16[2,128,256]{2,1,0:T(8,128)(2,1)S(1)}, u32[]{:S(2)}, u32[]{:S(2)}) collective-permute-start(bf16[2,128,256]{2,1,0:T(8,128)(2,1)S(1)} %shard_map.97.dv.refs_0_), channel_id=1, source_target_pairs={{0,16},{8,24},{16,0},{24,8},{1,17},{9,25},{17,1},{25,9},{2,18},{10... | collective-permute-start | bytes 393224 | tf_op jit(solution)/shard_map/ppermute | solution.py:468
  81.9 5.9 %collective-permute-start.13 = (bf16[2,128,256]{2,1,0:T(8,128)(2,1)S(1)}, bf16[2,128,256]{2,1,0:T(8,128)(2,1)S(1)}, u32[]{:S(2)}, u32[]{:S(2)}) collective-permute-start(bf16[2,128,256]{2,1,0:T(8,128)(2,1)S(1)} %shard_map.97.dv.refs_0_), channel_id=1, source_target_pairs={{0,24},{8,0},{16,8},{24,16},{1,25},{9,1},{17,9},{25,17},{2,26},{10... | collective-permute-start | bytes 393224 | tf_op jit(solution)/shard_map/ppermute | solution.py:468
  91.9 6.4 %copy-start.2 = (bf16[2,128,2048]{2,1,0:T(8,128)(2,1)S(1)}, bf16[2,128,2048]{2,1,0:T(8,128)(2,1)}, u32[]{:S(2)}) copy-start(bf16[2,128,2048]{2,1,0:T(8,128)(2,1)} %copy-done.1) | copy-start | bytes 3145732
  91.9 30.5 %all-to-all-start.1 = ((bf16[32,64,256]{2,1,0:T(8,128)(2,1)}), bf16[32,64,256]{2,1,0:T(8,128)(2,1)S(1)}, u32[]{:S(2)}, u32[]{:S(2)}) async-start(bf16[32,64,256]{2,1,0:T(8,128)(2,1)} %bitcast.8), calls=%async_computation.1 | async-start | bytes 2097152 | tf_op jit(solution)/shard_map/all_to_all | solution.py:435
  98.3 1.2 copy-start.4
  99.5 1.1 copy-start.6
  100.6 1.1 copy-start.8
  105.9 15.6 %collective-permute-start.4 = (bf16[128,2048]{1,0:T(8,128)(2,1)}, bf16[128,2048]{1,0:T(8,128)(2,1)S(1)}, u32[]{:S(2)}, u32[]{:S(2)}) collective-permute-start(bf16[128,2048]{1,0:T(8,128)(2,1)} %get-tuple-element.26), channel_id=1, source_target_pairs={{0,1},{1,0},{2,3},{3,2},{4,5},{5,4},{6,7},{7,6},{8,9},{9,8},{10,11... | collective-permute-start | bytes 1572872 | tf_op jit(solution)/shard_map/ppermute | solution.py:474
  106.3 10.6 %collective-permute-start.5 = (bf16[2,128,256]{2,1,0:T(8,128)(2,1)S(1)}, bf16[2,128,256]{2,1,0:T(8,128)(2,1)S(1)}, u32[]{:S(2)}, u32[]{:S(2)}) collective-permute-start(bf16[2,128,256]{2,1,0:T(8,128)(2,1)S(1)} %get-tuple-element.28), channel_id=1, source_target_pairs={{2,0},{4,2},{6,4},{3,1},{5,3},{7,5},{10,8},{12,10},{14,12},{11,9},... | collective-permute-start | bytes 393224 | tf_op jit(solution)/shard_map/ppermute | solution.py:462
  107.6 12.4 %collective-permute-start.6 = (bf16[2,128,256]{2,1,0:T(8,128)(2,1)S(1)}, bf16[2,128,256]{2,1,0:T(8,128)(2,1)S(1)}, u32[]{:S(2)}, u32[]{:S(2)}) collective-permute-start(bf16[2,128,256]{2,1,0:T(8,128)(2,1)S(1)} %get-tuple-element.29), channel_id=1, source_target_pairs={{4,0},{6,2},{5,1},{7,3},{12,8},{14,10},{13,9},{15,11},{20,16},{22,... | collective-permute-start | bytes 393224 | tf_op jit(solution)/shard_map/ppermute | solution.py:463
  120.1 1.4 %collective-permute-start.9 = (bf16[2,128,256]{2,1,0:T(8,128)(2,1)S(1)}, bf16[2,128,256]{2,1,0:T(8,128)(2,1)S(1)}, u32[]{:S(2)}, u32[]{:S(2)}) collective-permute-start(bf16[2,128,256]{2,1,0:T(8,128)(2,1)S(1)} %pad_maximum_fusion.2), channel_id=1, source_target_pairs={{0,1},{1,0},{2,3},{3,2},{4,5},{5,4},{6,7},{7,6},{8,9},{9,8},{10,11... | collective-permute-start | bytes 393224 | tf_op jit(solution)/shard_map/ppermute | solution.py:475
